TPU v7x, 32 devices: a whole 2x2x4 slice. The times are simulated.
32 devices in a mesh: dp: 8 (over z, y), mp: 4 (over x, core).
Axes of the slice: x: 2, y: 2, z: 4, core: 2. Of those that a mesh axis runs over, the one named last changes fastest.
Arguments:
- tokens: bfloat16 [2048, 1152], P('dp'), may hold values from -6 to 6
- conditioning: bfloat16 [4, 1152], replicated, may hold values from -6 to 6
- segments: int32 [2048], P('dp'), may hold values from 0 to 3, never falling along the last dimension, each value on 1 to 1024 neighbouring positions
- live_counts: int32 [8], P('dp'), may hold values from 32 to 256, as said below
- attn_weight: bfloat16 [3, 1152, 1152], P(None, 'dp', 'mp')
- attn_bias: float32 [2, 1152], P(None, 'mp'), may hold values from -3 to 3
- out_weight: bfloat16 [1152, 1152], P('mp', 'dp'), may hold values from -4 to 4
- out_bias: float32 [1152], replicated, may hold values from -3 to 3
- up_weight: bfloat16 [1152, 4608], P('dp', 'mp'), may hold values from -0.1875 to 0.1875
- up_bias: float32 [4608], P('mp'), may hold values from -3 to 3
- down_weight: bfloat16 [4608, 1152], P('mp', 'dp'), may hold values from -0.1875 to 0.1875
- down_bias: float32 [1152], replicated, may hold values from -3 to 3
- mod_weight: bfloat16 [1152, 6912], P('dp', 'mp'), may hold values from -0.1875 to 0.1875
- mod_bias: float32 [6912], P('mp'), may hold values from -3 to 3
- cotangent: bfloat16 [2048, 1152], P('dp'), may hold values from -6 to 6
Outputs:
- result: bfloat16 [2048, 1152], P(('dp', 'mp'))
- grad_tokens: float32 [2048, 1152], P(('dp', 'mp'))
- grad_conditioning: float32 [4, 1152], replicated
- grad_attn_weight: float32 [3, 1152, 1152], P(None, 'dp', 'mp')
- grad_attn_bias: float32 [2, 1152], P(None, 'mp')
- grad_out_weight: float32 [1152, 1152], P('mp', 'dp')
- grad_out_bias: float32 [1152], replicated
- grad_up_weight: float32 [1152, 4608], P('dp', 'mp')
- grad_up_bias: float32 [4608], P('mp')
- grad_down_weight: float32 [4608, 1152], P('mp', 'dp')
- grad_down_bias: float32 [1152], replicated
- grad_mod_weight: float32 [1152, 6912], P('dp', 'mp')
- grad_mod_bias: float32 [6912], P('mp')
Inputs may be any that keep to these rules, and one draw needn't show every extreme that they name: `segments`: the tokens of each latent stand next to each other; no latent has more than 1024 tokens and some latent has exactly 1024. The first live_counts[i] rows of index i of dp are live; some index has 256 and some other has 32.
All inputs are finite; a program needn't handle non-finite values.
Results may differ from a plain program's by a relative error of at most 0.017.
The roundings to bfloat16 on the way count: a program that leaves them out, or rounds other values in their place, can miss the bound.
Values may be sent and summed in bfloat16 or wider, within the bound.
No kernel may reach another device: no remote copies, remote signals or barrier semaphores. Data moves between devices by JAX's collectives and lax.ppermute only.
A program may use at most 192 MiB of HBM per device.

v0:
```python
import jax
import jax.numpy as jnp
from jax import lax
from jax.sharding import PartitionSpec as P

HD = 72
REACH = 4


EPSILON = 1e-06
NEG_FILL = -1e30


def shifted(x, axis, by):
    length = lax.axis_size(axis)
    pairs = [(i, i + by) for i in range(length) if 0 <= i + by < length]
    return lax.ppermute(x, axis, pairs)


def normalize(values):
    average = jnp.mean(values, axis=-1, keepdims=True)
    centered = values - average
    spread_sq = jnp.mean(centered * centered, axis=-1, keepdims=True)
    inv_std = lax.rsqrt(spread_sq + EPSILON)
    return (centered * inv_std, inv_std)


def normalize_back(grad_hat, normed, inv_std):
    first = jnp.mean(grad_hat, axis=-1, keepdims=True)
    second = jnp.mean(grad_hat * normed, axis=-1, keepdims=True)
    return inv_std * (grad_hat - first - normed * second)


def gelu_tanh(values):
    return jax.nn.gelu(values, approximate=True)


def silu_slope(values):
    sigma = jax.nn.sigmoid(values)
    return sigma * (1.0 + values * (1.0 - sigma))


def fetch_keys(stacked, tags, offset):
    return shifted((stacked, tags), "dp", -offset)


def return_grads(piece, offset):
    return shifted(piece, "dp", offset)


def place_part(part_vec, full_width, offset):
    empty = jnp.zeros(part_vec.shape[:-1] + (full_width,), jnp.float32)
    return lax.dynamic_update_slice_in_dim(empty, part_vec, offset, part_vec.ndim - 1)


def shards(
    tokens,
    conditioning,
    segments,
    live_counts,
    attn_weight,
    attn_bias,
    out_weight,
    out_bias,
    up_weight,
    up_bias,
    down_weight,
    down_bias,
    mod_weight,
    mod_bias,
    cotangent,
):
    tok_rows = tokens.shape[0]
    latents = conditioning.shape[0]
    columns = attn_weight.shape[2]
    hidden_cols = up_bias.shape[0]
    heads_here = columns // HD
    mod_cols = mod_bias.shape[0]
    score_scale = 1.0 / HD**0.5
    reach = REACH
    window = (2 * reach + 1) * tok_rows
    group = lax.axis_size("mp")
    share = tok_rows // group
    member = lax.axis_index("mp")
    row_start = member * share

    def own_rows(values):
        return lax.dynamic_slice_in_dim(values, row_start, share, 0)

    gathered = (
        lax.all_gather(attn_weight, "dp", axis=1, tiled=True),
        lax.all_gather(out_weight, "dp", axis=1, tiled=True),
        lax.all_gather(up_weight, "dp", axis=0, tiled=True),
        lax.all_gather(down_weight, "dp", axis=1, tiled=True),
        lax.all_gather(mod_weight, "dp", axis=0, tiled=True),
    )
    attn_full, out_full, up_full, down_full, mod_full = gathered
    cond_vals = conditioning.astype(jnp.float32)
    silu_cond = jax.nn.silu(cond_vals).astype(jnp.bfloat16)
    mod_part = jnp.dot(silu_cond, mod_full, preferred_element_type=jnp.float32) + mod_bias
    modulation = lax.all_gather(mod_part, "mp", axis=1, tiled=True)
    one_hot = (segments[:, None] == jnp.arange(latents, dtype=jnp.int32)[None, :]).astype(
        jnp.float32
    )
    per_token = jnp.dot(one_hot, modulation, precision=lax.Precision.HIGHEST)
    shift_attn, scale_attn, gate_attn, shift_mlp, scale_mlp, gate_mlp = jnp.split(
        per_token, 6, axis=1
    )
    per_share = own_rows(per_token)
    shift_attn_s, scale_attn_s, gate_attn_s, shift_mlp_s, scale_mlp_s, gate_mlp_s = jnp.split(
        per_share, 6, axis=1
    )
    live = (jnp.arange(tok_rows, dtype=jnp.int32) < live_counts[0]).astype(jnp.float32)[:, None]
    live_s = own_rows(live)
    token_vals = tokens.astype(jnp.float32)
    token_s = own_rows(token_vals)
    normed_one, inv_one = normalize(token_vals)
    attn_input = (normed_one * (1.0 + scale_attn) + shift_attn).astype(jnp.bfloat16)
    query_rows = (
        jnp.dot(attn_input, attn_full[0], preferred_element_type=jnp.float32) + attn_bias[0]
    ).astype(jnp.bfloat16)
    key_rows = jnp.dot(attn_input, attn_full[1], preferred_element_type=jnp.float32).astype(
        jnp.bfloat16
    )
    value_rows = (
        jnp.dot(attn_input, attn_full[2], preferred_element_type=jnp.float32) + attn_bias[1]
    ).astype(jnp.bfloat16)
    key_tag = jnp.where(live[:, 0] > 0.0, segments + 1, 0).astype(jnp.bfloat16)
    query_tag = (segments + 1).astype(jnp.float32)
    local_kv = jnp.stack([key_rows, value_rows])
    kv_pieces = []
    tag_pieces = []
    for offset in range(-reach, reach + 1):
        if offset == 0:
            kv_pieces.append(local_kv)
            tag_pieces.append(key_tag)
        else:
            got_kv, got_tag = fetch_keys(local_kv, key_tag, offset)
            kv_pieces.append(got_kv)
            tag_pieces.append(got_tag)
    window_kv = jnp.concatenate(kv_pieces, axis=1)
    window_tag = jnp.concatenate(tag_pieces).astype(jnp.float32)
    self_mask = (
        jnp.arange(window, dtype=jnp.int32)[None, :]
        == (reach * tok_rows + jnp.arange(tok_rows, dtype=jnp.int32))[:, None]
    )
    allowed = (window_tag[None, :] == query_tag[:, None]) | self_mask
    query_heads = jnp.transpose(query_rows.reshape(tok_rows, heads_here, HD), (1, 0, 2))
    key_heads = jnp.transpose(window_kv[0].reshape(window, heads_here, HD), (1, 0, 2))
    value_heads = jnp.transpose(window_kv[1].reshape(window, heads_here, HD), (1, 0, 2))

    def masked_scores(query_one, key_one):
        scores_raw = (
            lax.dot_general(
                query_one, key_one, (((1,), (1,)), ((), ())), preferred_element_type=jnp.float32
            )
            * score_scale
        )
        return jnp.where(allowed, scores_raw, NEG_FILL)

    def head_forward(operands):
        query_one, key_one, value_one = operands
        scores = masked_scores(query_one, key_one)
        row_max = jnp.max(scores, axis=-1, keepdims=True)
        log_total = row_max + jnp.log(jnp.sum(jnp.exp(scores - row_max), axis=-1, keepdims=True))
        attn_probs = jnp.exp(scores - log_total).astype(jnp.bfloat16)
        attended_one = jnp.dot(attn_probs, value_one, preferred_element_type=jnp.float32).astype(
            jnp.bfloat16
        )
        return (attended_one, log_total)

    attended_heads, log_totals = lax.map(head_forward, (query_heads, key_heads, value_heads))
    attended = jnp.transpose(attended_heads, (1, 0, 2)).reshape(tok_rows, columns)
    attn_out_s = (
        lax.psum_scatter(
            jnp.dot(attended, out_full, preferred_element_type=jnp.float32),
            "mp",
            scatter_dimension=0,
            tiled=True,
        )
        + out_bias
    )
    mid_s = token_s + live_s * gate_attn_s * attn_out_s
    normed_two_s, inv_two_s = normalize(mid_s)
    mlp_input_s = (normed_two_s * (1.0 + scale_mlp_s) + shift_mlp_s).astype(jnp.bfloat16)
    mlp_input = lax.all_gather(mlp_input_s, "mp", axis=0, tiled=True)
    hidden_pre = jnp.dot(mlp_input, up_full, preferred_element_type=jnp.float32) + up_bias
    hidden = gelu_tanh(hidden_pre).astype(jnp.bfloat16)
    mlp_out_s = (
        lax.psum_scatter(
            jnp.dot(hidden, down_full, preferred_element_type=jnp.float32),
            "mp",
            scatter_dimension=0,
            tiled=True,
        )
        + down_bias
    )
    result_s = (mid_s + live_s * gate_mlp_s * mlp_out_s).astype(jnp.bfloat16)
    backing = (
        lax.all_gather(attn_weight, "dp", axis=1, tiled=True),
        lax.all_gather(out_weight, "dp", axis=1, tiled=True),
        lax.all_gather(up_weight, "dp", axis=0, tiled=True),
        lax.all_gather(down_weight, "dp", axis=1, tiled=True),
        lax.all_gather(mod_weight, "dp", axis=0, tiled=True),
    )
    attn_back, out_back, up_back, down_back, mod_back = backing
    grad_result = cotangent.astype(jnp.float32)
    grad_result_s = own_rows(grad_result)
    grad_mlp = grad_result * live * gate_mlp
    grad_mlp_b = grad_mlp.astype(jnp.bfloat16)
    grad_down_w = jnp.dot(hidden.T, grad_mlp_b, preferred_element_type=jnp.float32)
    grad_down_b_s = jnp.sum(own_rows(grad_mlp), axis=0)
    grad_hidden = jnp.dot(grad_mlp_b, down_back.T, preferred_element_type=jnp.float32)
    grad_pre = jax.vjp(gelu_tanh, hidden_pre)[1](grad_hidden)[0]
    grad_pre_b = grad_pre.astype(jnp.bfloat16)
    grad_up_b = jnp.sum(grad_pre, axis=0)
    grad_up_w = jnp.dot(mlp_input.T, grad_pre_b, preferred_element_type=jnp.float32)
    grad_mlp_in_s = lax.psum_scatter(
        jnp.dot(grad_pre_b, up_back.T, preferred_element_type=jnp.float32),
        "mp",
        scatter_dimension=0,
        tiled=True,
    )
    grad_mid_s = grad_result_s + normalize_back(
        grad_mlp_in_s * (1.0 + scale_mlp_s), normed_two_s, inv_two_s
    )
    grad_attn_s = grad_mid_s * live_s * gate_attn_s
    grad_out_b_s = jnp.sum(grad_attn_s, axis=0)
    grad_attn_b = lax.all_gather(grad_attn_s.astype(jnp.bfloat16), "mp", axis=0, tiled=True)
    grad_out_w = jnp.dot(attended.T, grad_attn_b, preferred_element_type=jnp.float32)
    grad_attended = jnp.dot(grad_attn_b, out_back.T, preferred_element_type=jnp.float32).astype(
        jnp.bfloat16
    )
    grad_heads = jnp.transpose(grad_attended.reshape(tok_rows, heads_here, HD), (1, 0, 2))

    def head_backward(operands):
        query_one, key_one, value_one, grad_one, attended_one, log_total = operands
        scores = masked_scores(query_one, key_one)
        attn_exact = jnp.exp(scores - log_total)
        attn_probs = attn_exact.astype(jnp.bfloat16)
        grad_probs = lax.dot_general(
            grad_one, value_one, (((1,), (1,)), ((), ())), preferred_element_type=jnp.float32
        )
        delta = jnp.sum(
            grad_one.astype(jnp.float32) * attended_one.astype(jnp.float32), axis=-1, keepdims=True
        )
        grad_scores = (attn_exact * (grad_probs - delta)).astype(jnp.bfloat16)
        grad_query_one = (
            jnp.dot(grad_scores, key_one, preferred_element_type=jnp.float32) * score_scale
        )
        grad_key_one = (
            lax.dot_general(
                grad_scores, query_one, (((0,), (0,)), ((), ())), preferred_element_type=jnp.float32
            )
            * score_scale
        )
        grad_value_one = lax.dot_general(
            attn_probs, grad_one, (((0,), (0,)), ((), ())), preferred_element_type=jnp.float32
        )
        return (grad_query_one, grad_key_one, grad_value_one)

    grad_query_h, grad_key_h, grad_value_h = lax.map(
        head_backward, (query_heads, key_heads, value_heads, grad_heads, attended_heads, log_totals)
    )
    grad_query = jnp.transpose(grad_query_h, (1, 0, 2)).reshape(tok_rows, columns)
    grad_key_win = jnp.transpose(grad_key_h, (1, 0, 2)).reshape(window, columns)
    grad_value_win = jnp.transpose(grad_value_h, (1, 0, 2)).reshape(window, columns)
    grad_kv_window = jnp.stack([grad_key_win, grad_value_win])
    grad_kv = grad_kv_window[:, reach * tok_rows : (reach + 1) * tok_rows]
    for offset in range(-reach, reach + 1):
        if offset != 0:
            piece = grad_kv_window[:, (offset + reach) * tok_rows : (offset + reach + 1) * tok_rows]
            grad_kv = grad_kv + return_grads(piece, offset)
    grad_attn_bias_part = jnp.stack([jnp.sum(grad_query, axis=0), jnp.sum(grad_kv[1], axis=0)])
    grad_qkv = jnp.stack([grad_query, grad_kv[0], grad_kv[1]]).astype(jnp.bfloat16)
    grad_attn_w = jnp.einsum(
        "td,jtc->jdc", attn_input, grad_qkv, preferred_element_type=jnp.float32
    )
    grad_attn_in_s = lax.psum_scatter(
        jnp.einsum("jtc,jdc->td", grad_qkv, attn_back, preferred_element_type=jnp.float32),
        "mp",
        scatter_dimension=0,
        tiled=True,
    )
    normed_one_s = own_rows(normed_one)
    inv_one_s = own_rows(inv_one)
    grad_tokens_s = grad_mid_s + normalize_back(
        grad_attn_in_s * (1.0 + scale_attn_s), normed_one_s, inv_one_s
    )
    grad_mod_rows = jnp.concatenate(
        [
            grad_attn_in_s,
            grad_attn_in_s * normed_one_s,
            grad_mid_s * live_s * attn_out_s,
            grad_mlp_in_s,
            grad_mlp_in_s * normed_two_s,
            grad_result_s * live_s * mlp_out_s,
        ],
        axis=1,
    )
    grad_mod_share = jnp.dot(own_rows(one_hot).T, grad_mod_rows, precision=lax.Precision.HIGHEST)
    own_cols = lax.psum_scatter(grad_mod_share, "mp", scatter_dimension=1, tiled=True)
    grad_mod_w = jnp.dot(silu_cond.astype(jnp.float32).T, own_cols, precision=lax.Precision.HIGHEST)
    grad_mod_b = jnp.sum(own_cols, axis=0)
    silu_part = jnp.dot(own_cols, mod_back.astype(jnp.float32).T, precision=lax.Precision.HIGHEST)
    attn_b_placed = place_part(grad_attn_bias_part, columns * group, member * columns)
    up_b_placed = place_part(grad_up_b, hidden_cols * group, member * hidden_cols)
    mod_b_placed = place_part(grad_mod_b, mod_cols * group, member * mod_cols)
    summed = lax.psum(
        (silu_part, attn_b_placed, up_b_placed, mod_b_placed, grad_out_b_s, grad_down_b_s),
        ("dp", "mp"),
    )
    grad_silu, attn_b_all, up_b_all, mod_b_all, out_b_all, down_b_all = summed
    grad_conditioning = grad_silu * silu_slope(cond_vals)
    attn_b_out = lax.dynamic_slice_in_dim(attn_b_all, member * columns, columns, 1)
    up_b_out = lax.dynamic_slice_in_dim(up_b_all, member * hidden_cols, hidden_cols, 0)
    mod_b_out = lax.dynamic_slice_in_dim(mod_b_all, member * mod_cols, mod_cols, 0)
    weight_terms = (
        lax.psum_scatter(grad_attn_w, "dp", scatter_dimension=1, tiled=True),
        lax.psum_scatter(grad_out_w, "dp", scatter_dimension=1, tiled=True),
        lax.psum_scatter(grad_up_w, "dp", scatter_dimension=0, tiled=True),
        lax.psum_scatter(grad_down_w, "dp", scatter_dimension=1, tiled=True),
        lax.psum_scatter(grad_mod_w, "dp", scatter_dimension=0, tiled=True),
    )
    attn_w_out, out_w_out, up_w_out, down_w_out, mod_w_out = weight_terms
    return (
        result_s,
        grad_tokens_s,
        grad_conditioning,
        attn_w_out,
        attn_b_out,
        out_w_out,
        out_b_all,
        up_w_out,
        up_b_out,
        down_w_out,
        down_b_all,
        mod_w_out,
        mod_b_out,
    )


def solution(mesh):
    placed = (
        P("dp", None),
        P(),
        P("dp"),
        P("dp"),
        P(None, "dp", "mp"),
        P(None, "mp"),
        P("mp", "dp"),
        P(),
        P("dp", "mp"),
        P("mp"),
        P("mp", "dp"),
        P(),
        P("dp", "mp"),
        P("mp"),
        P("dp", None),
    )
    return jax.shard_map(
        shards,
        mesh=mesh,
        in_specs=placed,
        out_specs=(
            P(("dp", "mp"), None),
            P(("dp", "mp"), None),
            P(),
            P(None, "dp", "mp"),
            P(None, "mp"),
            P("mp", "dp"),
            P(),
            P("dp", "mp"),
            P("mp"),
            P("mp", "dp"),
            P(),
            P("dp", "mp"),
            P("mp"),
        ),
        check_vma=False,
    )
```

profile of v0, /device:TPU:0, one launch (start us, length us, event | category | flops | bytes accessed | tf_op | source)
XLA Modules:
  0.0 1332.4 jit_solution(6206156451120816778)
XLA Ops:
  10.6 6.0 collective-permute-start.8
  16.6 4.4 collective-permute-start.9
  22.3 3.1 collective-permute-start.11
  31.3 35.1 %all_gather.32 = bf16[288,1152]{0,1:T(8,128)(2,1)S(1)} all-gather(bf16[288,144]{0,1:T(8,128)(2,1)} %param.25), channel_id=1, replica_groups=mesh['dp'=8,'mp'=4] {'dp'}, dimensions={1}, use_global_device_ids=true | all-gather | bytes 746496 | tf_op jit(solution)/shard_map/all_gather | solution.py:92
  72.6 1.9 collective-permute-done.14
  74.7 18.7 %all-gather.6.cloned.1.call-done = bf16[1152,1728]{1,0:T(8,128)(2,1)} async-done(((bf16[144,1728]{1,0:T(8,128)(2,1)}), bf16[1152,1728]{1,0:T(8,128)(2,1)}) %all-gather.6.cloned.1.call-update) | async-done | bytes 3981328 | tf_op jit(solution)/shard_map/all_gather | solution.py:95
  93.4 2.8 fusion.51
  96.2 5.4 all-gather
  101.8 3.0 fusion.112
  104.8 2.8 copy-done
  109.4 40.3 %all-gather.8.cloned.1.call-done = bf16[3,1152,288]{2,1,0:T(8,128)(2,1)} async-done(((bf16[3,144,288]{2,1,0:T(8,128)(2,1)}), bf16[3,1152,288]{2,1,0:T(8,128)(2,1)}) %all-gather.8.cloned.1.call-update) | async-done | bytes 1990672 | tf_op jit(solution)/shard_map/all_gather | solution.py:91
  153.0 4.5 collective-permute-start
  158.2 3.2 collective-permute-start.1
  161.3 2.0 collective-permute-start.2
  163.3 3.1 collective-permute-start.3
  181.2 9.4 collective-permute-done.6
  190.6 18.0 %collective-permute-done.7 = bf16[2,256,288]{1,2,0:T(8,128)(2,1)S(1)} collective-permute-done((bf16[2,256,288]{1,2,0:T(8,128)(2,1)S(1)}, bf16[2,256,288]{1,2,0:T(8,128)(2,1)S(1)}, u32[]{:S(2)}, u32[]{:S(2)}) %collective-permute-start.7) | collective-permute-done | bytes 294944 | tf_op jit(solution)/shard_map/ppermute | solution.py:17
  209.9 3.8 copy.43
  213.7 2.4 copy.44
  216.1 18.5 %while.28 = (s32[]{:T(128)}, bf16[4,256,72]{1,2,0:T(8,128)(2,1)S(1)}, f32[4,256,1]{1,2,0:T(1,128)}, bf16[4,256,72]{2,1,0:T(8,128)(2,1)}, bf16[4,2304,72]{2,1,0:T...) while((s32[]{:T(128)}, ...), condition=%wide.region_5.6_spmd.clone, body=%wide.region_2.5_spmd.clone.sunk | while | flops 175785728 | bytes 8386149 | solution.py:172
  238.7 20.5 %reduce-scatter.15.cloned.1.call-done = f32[64,1152]{1,0:T(8,128)} async-done(((f32[256,1152]{1,0:T(8,128)}), f32[64,1152]{1,0:T(8,128)}) %reduce-scatter.15.cloned.1.call-update) | async-done | bytes 294928 | tf_op jit(solution)/shard_map/reduce_scatter | solution.py:175
  262.0 7.0 all_gather.33
  269.0 47.3 %all-gather.10.cloned.1.call-done = bf16[1152,1152]{1,0:T(8,128)(2,1)} async-done(((bf16[144,1152]{1,0:T(8,128)(2,1)}), bf16[1152,1152]{1,0:T(8,128)(2,1)}) %all-gather.10.cloned.1.call-update) | async-done | bytes 2654224 | tf_op jit(solution)/shard_map/all_gather | solution.py:93
  316.3 3.9 convolution_add_fusion
  320.1 51.7 %all-gather.12.cloned.1.call-done = bf16[1152,1152]{0,1:T(8,128)(2,1)} async-done(((bf16[1152,144]{0,1:T(8,128)(2,1)}), bf16[1152,1152]{0,1:T(8,128)(2,1)}) %all-gather.12.cloned.1.call-update) | async-done | bytes 2654224 | tf_op jit(solution)/shard_map/all_gather | solution.py:94
  371.9 4.5 fusion.128
  376.4 2.1 fusion.92
  378.6 4.3 fusion.118
  384.1 18.8 %reduce-scatter.19.cloned.1.call-done = f32[64,1152]{1,0:T(8,128)} async-done(((f32[256,1152]{1,0:T(8,128)}), f32[64,1152]{1,0:T(8,128)}) %reduce-scatter.19.cloned.1.call-update) | async-done | bytes 294928 | tf_op jit(solution)/shard_map/reduce_scatter | solution.py:218
  404.1 26.9 %reduce-scatter.17.cloned.1.call-done = f32[64,1152]{1,0:T(8,128)} async-done(((f32[256,1152]{1,0:T(8,128)}), f32[64,1152]{1,0:T(8,128)}) %reduce-scatter.17.cloned.1.call-update) | async-done | bytes 294928 | tf_op jit(solution)/shard_map/reduce_scatter | solution.py:190
  431.1 2.7 fusion.102
  434.9 7.0 all_gather.36
  442.6 39.7 %while.29 = (s32[]{:T(128)}, f32[4,256,72]{1,2,0:T(8,128)}, f32[4,2304,72]{1,2,0:T(8,128)}, f32[4,2304,72]{1,2,0:T(8,128)}, bf16[4,256,72]{2,1,0:T(8,128)(2,1)},...) while((s32[]{:T(128)}, f32[4,256,72]{1,2,0:T(8,128)}, ...), condition=%wide.region_15.16_spmd.clone, body=%wide.region_13.15_spmd.clone.sunk | while | flops 430829312 | bytes 14292113 | solution.py:262
  447.1 2.1 fusion.191
  450.3 2.2 fusion.190
  457.0 2.1 fusion.191
  460.3 2.2 fusion.190
  463.2 1.9 fusion.187
  466.9 2.1 fusion.191
  470.3 2.2 fusion.190
  476.9 2.1 fusion.191
  480.2 2.2 fusion.190
  482.4 2.9 fusion.78
  490.8 4.6 collective-permute-start.20
  495.4 34.4 %collective-permute-done.16 = f32[2,256,288]{1,2,0:T(8,128)S(1)} collective-permute-done((f32[2,256,288]{1,2,0:T(8,128)S(1)}, f32[2,256,288]{1,2,0:T(8,128)S(1)}, u32[]{:S(2)}, u32[]{:S(2)}) %collective-permute-start.16) | collective-permute-done | bytes 589856 | tf_op jit(solution)/shard_map/ppermute | solution.py:17
  532.5 24.0 %collective-permute-start.23 = (f32[2,256,288]{1,2,0:T(8,128)S(1)}, f32[2,256,288]{1,2,0:T(8,128)S(1)}, u32[]{:S(2)}, u32[]{:S(2)}) collective-permute-start(f32[2,256,288]{1,2,0:T(8,128)S(1)} %get-tuple-element.322), channel_id=1, source_target_pairs={{0,16},{4,20},{8,24},{12,28},{1,17},{5,21},{9,25},{13,29},{2,18},{... | collective-permute-start | bytes 1769480 | tf_op jit(solution)/shard_map/ppermute | solution.py:17
  557.9 11.5 collective-permute-done.23
  570.6 2.1 convolution_bitcast_fusion.3
  575.2 36.4 %reduce-scatter.21.cloned.1.call-done = f32[64,1152]{1,0:T(8,128)} async-done(((f32[256,1152]{1,0:T(8,128)}), f32[64,1152]{1,0:T(8,128)}) %reduce-scatter.21.cloned.1.call-update) | async-done | bytes 294928 | tf_op jit(solution)/shard_map/reduce_scatter | solution.py:279
  617.0 4.7 convolution_bitcast_fusion.1
  623.1 39.1 %reduce-scatter.31.cloned.1.call-done = f32[1728,4]{1,0:T(8,128)} async-done(((f32[6912,4]{1,0:T(8,128)}), f32[1728,4]{1,0:T(8,128)}) %reduce-scatter.31.cloned.1.call-update) | async-done | bytes 27664
  664.1 6.7 fusion.64
  670.9 2.7 convolution_bitcast_fusion.2
  673.6 8.6 copy.50
  682.2 9.0 reshape.214
  694.2 3.4 fusion.90
  698.8 3.4 fusion.94
  703.4 5.8 fusion.66
  709.2 87.2 %all-reduce.3.cloned.1.call-done = (f32[4,1152]{1,0:T(4,128)}, f32[2,1152]{1,0:T(2,128)}, f32[1152]{0:T(1024)}, f32[4608]{0:T(1024)}, f32[1152]{0:T(1024)}, /*index=5*/f32[6912]{0:T(1024)}) async-done(((f32[4,1152]{1,0:T(4,128)}, f32[2,1152]{1,0:T(2,128)}, f32[1152]{0:T(1024)}, f32[4608]{0:T(1024)}, f32[1152]{0:T(1024)}, /*index=5*/f32[6912]{0:T(1024)}), (f32[4,1152]{1,0:T(4,128)}, f32[2,1152]{1,0:T(2,128)}, ...) | async-done | bytes 82960 | tf_op jit(solution)/shard_map/psum | solution.py:309
  801.9 87.0 %reduce-scatter.33.cloned.1.call-done = f32[144,864]{1,0:T(8,128)} async-done(((f32[1152,864]{1,0:T(8,128)}), f32[144,864]{1,0:T(8,128)}) %reduce-scatter.33.cloned.1.call-update) | async-done | bytes 497680
  891.4 67.6 %reduce-scatter.23.cloned.1.call-done = f32[288,144]{0,1:T(8,128)} async-done(((f32[288,1152]{0,1:T(8,128)}), f32[288,144]{0,1:T(8,128)}) %reduce-scatter.23.cloned.1.call-update) | async-done | bytes 165904 | tf_op jit(solution)/shard_map/reduce_scatter | solution.py:320
  959.0 107.6 %reduce-scatter.25.cloned.1.call-done = f32[144,1152]{1,0:T(8,128)} async-done(((f32[1152,1152]{1,0:T(8,128)}), f32[144,1152]{1,0:T(8,128)}) %reduce-scatter.25.cloned.1.call-update) | async-done | bytes 663568 | tf_op jit(solution)/shard_map/reduce_scatter | solution.py:321
  1066.6 108.2 %reduce-scatter.27.cloned.1.call-done = f32[1152,144]{0,1:T(8,128)} async-done(((f32[1152,1152]{0,1:T(8,128)}), f32[1152,144]{0,1:T(8,128)}) %reduce-scatter.27.cloned.1.call-update) | async-done | bytes 663568 | tf_op jit(solution)/shard_map/reduce_scatter | solution.py:322
  1174.8 149.5 %reduce-scatter.29.cloned.1.call-done = f32[144,1728]{1,0:T(8,128)} async-done(((f32[1152,1728]{1,0:T(8,128)}), f32[144,1728]{1,0:T(8,128)}) %reduce-scatter.29.cloned.1.call-update) | async-done | bytes 995344 | tf_op jit(solution)/shard_map/reduce_scatter | solution.py:323
  (308 shorter events, 124.4 us)
Async XLA Ops:
  7.2 86.2 %copy-start.24 = (bf16[4,1152]{1,0:T(4,128)(2,1)S(1)}, bf16[4,1152]{1,0:T(4,128)(2,1)}, u32[]{:S(2)}) copy-start(bf16[4,1152]{1,0:T(4,128)(2,1)} %param.20) | copy-start | bytes 27652
  7.2 86.2 %copy-start.40 = (f32[1728]{0:T(1024)S(1)}, f32[1728]{0:T(1024)}, u32[]{:S(2)}) copy-start(f32[1728]{0:T(1024)} %param.32) | copy-start | bytes 20740
  7.2 86.2 %all-gather.6.cloned.1.call-start = ((), (), s32[]{:S(2)}) async-start(), calls=%async_computation.10 | async-start | bytes 4644864 | tf_op jit(solution)/shard_map/all_gather | solution.py:95
  7.9 141.8 %all-gather.8.cloned.1.call-start = ((), (), s32[]{:S(2)}) async-start(), calls=%async_computation.11 | async-start | bytes 2985984 | tf_op jit(solution)/shard_map/all_gather | solution.py:91
  8.7 250.5 %reduce-scatter.15.cloned.1.call-start = ((), (), s32[]{:S(2)}) async-start(), calls=%async_computation.12 | async-start | bytes 1474560 | tf_op jit(solution)/shard_map/reduce_scatter | solution.py:175
  10.6 55.9 %collective-permute-start.8 = (bf16[256]{0:T(256)(128)(2,1)S(1)}, bf16[256]{0:T(256)(128)(2,1)S(1)}, u32[]{:S(2)}, u32[]{:S(2)}) collective-permute-start(bf16[256]{0:T(256)(128)(2,1)S(1)} %get-tuple-element.330), channel_id=1, source_target_pairs={{0,16},{4,20},{8,24},{12,28},{1,17},{5,21},{9,25},{13,29},{2,18},{... | collective-permute-start | bytes 1544 | tf_op jit(solution)/shard_map/ppermute | solution.py:17
  16.6 51.4 %collective-permute-start.9 = (bf16[256]{0:T(256)(128)(2,1)S(1)}, bf16[256]{0:T(256)(128)(2,1)S(1)}, u32[]{:S(2)}, u32[]{:S(2)}) collective-permute-start(bf16[256]{0:T(256)(128)(2,1)S(1)} %get-tuple-element.330), channel_id=1, source_target_pairs={{0,12},{4,16},{8,20},{12,24},{16,28},{1,13},{5,17},{9,21},{13,25},... | collective-permute-start | bytes 1544 | tf_op jit(solution)/shard_map/ppermute | solution.py:17
  21.0 48.5 %collective-permute-start.10 = (bf16[256]{0:T(256)(128)(2,1)S(1)}, bf16[256]{0:T(256)(128)(2,1)S(1)}, u32[]{:S(2)}, u32[]{:S(2)}) collective-permute-start(bf16[256]{0:T(256)(128)(2,1)S(1)} %get-tuple-element.330), channel_id=1, source_target_pairs={{0,8},{4,12},{8,16},{12,20},{16,24},{20,28},{1,9},{5,13},{9,17},{1... | collective-permute-start | bytes 1544 | tf_op jit(solution)/shard_map/ppermute | solution.py:17
  22.3 48.8 %collective-permute-start.11 = (bf16[256]{0:T(256)(128)(2,1)S(1)}, bf16[256]{0:T(256)(128)(2,1)S(1)}, u32[]{:S(2)}, u32[]{:S(2)}) collective-permute-start(bf16[256]{0:T(256)(128)(2,1)S(1)} %get-tuple-element.330), channel_id=1, source_target_pairs={{0,4},{4,8},{8,12},{12,16},{16,20},{20,24},{24,28},{1,5},{5,9},{9,... | collective-permute-start | bytes 1544 | tf_op jit(solution)/shard_map/ppermute | solution.py:17
  25.4 46.1 %collective-permute-start.12 = (bf16[256]{0:T(256)(128)(2,1)S(1)}, bf16[256]{0:T(256)(128)(2,1)S(1)}, u32[]{:S(2)}, u32[]{:S(2)}) collective-permute-start(bf16[256]{0:T(256)(128)(2,1)S(1)} %get-tuple-element.330), channel_id=1, source_target_pairs={{4,0},{8,4},{12,8},{16,12},{20,16},{24,20},{28,24},{5,1},{9,5},{13... | collective-permute-start | bytes 1544 | tf_op jit(solution)/shard_map/ppermute | solution.py:17
  31.3 73.5 %copy-start.44 = (f32[256]{0:T(256)}, f32[256]{0:T(256)S(1)}, u32[]{:S(2)}) copy-start(f32[256]{0:T(256)S(1)} %add_rsqrt_fusion) | copy-start | bytes 3076
  66.4 38.3 %copy-start.47 = (f32[256]{0:T(256)}, f32[256]{0:T(256)S(1)}, u32[]{:S(2)}) copy-start(f32[256]{0:T(256)S(1)} %compare_convert_fusion) | copy-start | bytes 3076
  66.5 6.0 collective-permute-start.13
  68.0 6.5 collective-permute-start.14
  69.6 88.0 %collective-permute-start.15 = (bf16[256]{0:T(256)(128)(2,1)S(1)}, bf16[256]{0:T(256)(128)(2,1)S(1)}, u32[]{:S(2)}, u32[]{:S(2)}) collective-permute-start(bf16[256]{0:T(256)(128)(2,1)S(1)} %get-tuple-element.330), channel_id=1, source_target_pairs={{16,0},{20,4},{24,8},{28,12},{17,1},{21,5},{25,9},{29,13},{18,2},{... | collective-permute-start | bytes 1544 | tf_op jit(solution)/shard_map/ppermute | solution.py:17
  74.7 27.1 %copy-start.27 = (s32[256]{0:T(256)S(1)}, s32[256]{0:T(256)}, u32[]{:S(2)}) copy-start(s32[256]{0:T(256)} %param.21) | copy-start | bytes 3076
  109.4 60.0 %copy-start.12 = (bf16[256,1152]{1,0:T(8,128)(2,1)}, bf16[256,1152]{1,0:T(8,128)(2,1)S(1)}, u32[]{:S(2)}) copy-start(bf16[256,1152]{1,0:T(8,128)(2,1)S(1)} %get-tuple-element.315) | copy-start | bytes 1769476
  153.0 17.2 %collective-permute-start = (bf16[2,256,288]{1,2,0:T(8,128)(2,1)S(1)}, bf16[2,256,288]{1,2,0:T(8,128)(2,1)}, u32[]{:S(2)}, u32[]{:S(2)}) collective-permute-start(bf16[2,256,288]{1,2,0:T(8,128)(2,1)S(1)} %pad_maximum_fusion.2), channel_id=1, source_target_pairs={{0,16},{4,20},{8,24},{12,28},{1,17},{5,21},{9,25},{13,29},{2,18},{... | collective-permute-start | bytes 884744 | tf_op jit(solution)/shard_map/ppermute | solution.py:17
  158.2 14.4 %collective-permute-start.1 = (bf16[2,256,288]{1,2,0:T(8,128)(2,1)S(1)}, bf16[2,256,288]{1,2,0:T(8,128)(2,1)}, u32[]{:S(2)}, u32[]{:S(2)}) collective-permute-start(bf16[2,256,288]{1,2,0:T(8,128)(2,1)S(1)} %pad_maximum_fusion.2), channel_id=1, source_target_pairs={{0,12},{4,16},{8,20},{12,24},{16,28},{1,13},{5,17},{9,21},{13,25},... | collective-permute-start | bytes 884744 | tf_op jit(solution)/shard_map/ppermute | solution.py:17
  161.3 14.2 %collective-permute-start.2 = (bf16[2,256,288]{1,2,0:T(8,128)(2,1)S(1)}, bf16[2,256,288]{1,2,0:T(8,128)(2,1)}, u32[]{:S(2)}, u32[]{:S(2)}) collective-permute-start(bf16[2,256,288]{1,2,0:T(8,128)(2,1)S(1)} %pad_maximum_fusion.2), channel_id=1, source_target_pairs={{0,8},{4,12},{8,16},{12,20},{16,24},{20,28},{1,9},{5,13},{9,17},{1... | collective-permute-start | bytes 884744 | tf_op jit(solution)/shard_map/ppermute | solution.py:17
  163.3 14.6 %collective-permute-start.3 = (bf16[2,256,288]{1,2,0:T(8,128)(2,1)S(1)}, bf16[2,256,288]{1,2,0:T(8,128)(2,1)}, u32[]{:S(2)}, u32[]{:S(2)}) collective-permute-start(bf16[2,256,288]{1,2,0:T(8,128)(2,1)S(1)} %pad_maximum_fusion.2), channel_id=1, source_target_pairs={{0,4},{4,8},{8,12},{12,16},{16,20},{20,24},{24,28},{1,5},{5,9},{9,... | collective-permute-start | bytes 884744 | tf_op jit(solution)/shard_map/ppermute | solution.py:17
  166.5 12.5 collective-permute-start.4
  170.3 10.9 collective-permute-start.5
  172.5 18.0 %collective-permute-start.6 = (bf16[2,256,288]{1,2,0:T(8,128)(2,1)S(1)}, bf16[2,256,288]{1,2,0:T(8,128)(2,1)S(1)}, u32[]{:S(2)}, u32[]{:S(2)}) collective-permute-start(bf16[2,256,288]{1,2,0:T(8,128)(2,1)S(1)} %pad_maximum_fusion.2), channel_id=1, source_target_pairs={{12,0},{16,4},{20,8},{24,12},{28,16},{13,1},{17,5},{21,9},{25,13},... | collective-permute-start | bytes 884744 | tf_op jit(solution)/shard_map/ppermute | solution.py:17
  175.5 33.1 %collective-permute-start.7 = (bf16[2,256,288]{1,2,0:T(8,128)(2,1)S(1)}, bf16[2,256,288]{1,2,0:T(8,128)(2,1)S(1)}, u32[]{:S(2)}, u32[]{:S(2)}) collective-permute-start(bf16[2,256,288]{1,2,0:T(8,128)(2,1)S(1)} %pad_maximum_fusion.2), channel_id=1, source_target_pairs={{16,0},{20,4},{24,8},{28,12},{17,1},{21,5},{25,9},{29,13},{18,2},{... | collective-permute-start | bytes 884744 | tf_op jit(solution)/shard_map/ppermute | solution.py:17
  236.2 23.0 %copy-start.29 = (f32[1152]{0:T(1024)S(1)}, f32[1152]{0:T(1024)}, u32[]{:S(2)}) copy-start(f32[1152]{0:T(1024)} %param.26) | copy-start | bytes 13828
  236.3 80.0 %all-gather.10.cloned.1.call-start = ((), (), s32[]{:S(2)}) async-start(), calls=%async_computation.13 | async-start | bytes 2985984 | tf_op jit(solution)/shard_map/all_gather | solution.py:93
  236.8 135.0 %all-gather.12.cloned.1.call-start = ((), (), s32[]{:S(2)}) async-start(), calls=%async_computation.14 | async-start | bytes 2985984 | tf_op jit(solution)/shard_map/all_gather | solution.py:94
  237.4 165.4 %reduce-scatter.19.cloned.1.call-start = ((), (), s32[]{:S(2)}) async-start(), calls=%async_computation.16 | async-start | bytes 1474560 | tf_op jit(solution)/shard_map/reduce_scatter | solution.py:218
  237.5 78.8 %copy-start.52 = (f32[1152]{0:T(1024)S(1)}, f32[1152]{0:T(1024)}, u32[]{:S(2)}) copy-start(f32[1152]{0:T(1024)} %param.28) | copy-start | bytes 13828
  238.7 195.1 %copy-start.35 = (f32[64]{0:T(128)}, f32[64]{0:T(128)S(1)}, u32[]{:S(2)}) copy-start(f32[64]{0:T(128)S(1)} %dynamic-slice.6) | copy-start | bytes 772
  260.6 170.5 %copy-start.33 = (f32[64]{0:T(128)}, f32[64]{0:T(128)S(1)}, u32[]{:S(2)}) copy-start(f32[64]{0:T(128)S(1)} %broadcast_multiply_fusion.5) | copy-start | bytes 772
  260.8 170.2 %copy-start.38 = (f32[64]{0:T(128)}, f32[64]{0:T(128)S(1)}, u32[]{:S(2)}) copy-start(f32[64]{0:T(128)S(1)} %add_rsqrt_fusion.1) | copy-start | bytes 772
  269.0 51.2 %copy-start.8 = (bf16[256,1152]{1,0:T(8,128)(2,1)}, bf16[256,1152]{1,0:T(8,128)(2,1)S(1)}, u32[]{:S(2)}) copy-start(bf16[256,1152]{1,0:T(8,128)(2,1)S(1)} %all_gather.33) | copy-start | bytes 1769476
  378.5 52.5 %reduce-scatter.17.cloned.1.call-start = ((), (), s32[]{:S(2)}) async-start(), calls=%async_computation.15 | async-start | bytes 1474560 | tf_op jit(solution)/shard_map/reduce_scatter | solution.py:190
  382.8 48.2 %copy-start.31 = (f32[1152]{0:T(1024)S(1)}, f32[1152]{0:T(1024)}, u32[]{:S(2)}) copy-start(f32[1152]{0:T(1024)} %param.30) | copy-start | bytes 13828
  382.9 228.7 %reduce-scatter.21.cloned.1.call-start = ((), (), s32[]{:S(2)}) async-start(), calls=%async_computation.17 | async-start | bytes 1474560 | tf_op jit(solution)/shard_map/reduce_scatter | solution.py:279
  482.4 87.0 %copy-start.1 = (f32[4,2304,72]{1,2,0:T(8,128)S(1)}, f32[4,2304,72]{1,2,0:T(8,128)}, u32[]{:S(2)}) copy-start(f32[4,2304,72]{1,2,0:T(8,128)} %get-tuple-element.113) | copy-start | bytes 7962628
  482.4 87.0 %copy-start.2 = (f32[4,2304,72]{1,2,0:T(8,128)S(1)}, f32[4,2304,72]{1,2,0:T(8,128)}, u32[]{:S(2)}) copy-start(f32[4,2304,72]{1,2,0:T(8,128)} %get-tuple-element.114) | copy-start | bytes 7962628
  485.3 44.5 %collective-permute-start.16 = (f32[2,256,288]{1,2,0:T(8,128)S(1)}, f32[2,256,288]{1,2,0:T(8,128)S(1)}, u32[]{:S(2)}, u32[]{:S(2)}) collective-permute-start(f32[2,256,288]{1,2,0:T(8,128)S(1)} %get-tuple-element.316), channel_id=1, source_target_pairs={{16,0},{20,4},{24,8},{28,12},{17,1},{21,5},{25,9},{29,13},{18,2},{... | collective-permute-start | bytes 1769480 | tf_op jit(solution)/shard_map/ppermute | solution.py:17
  486.9 44.2 %collective-permute-start.17 = (f32[2,256,288]{1,2,0:T(8,128)S(1)}, f32[2,256,288]{1,2,0:T(8,128)S(1)}, u32[]{:S(2)}, u32[]{:S(2)}) collective-permute-start(f32[2,256,288]{1,2,0:T(8,128)S(1)} %get-tuple-element.317), channel_id=1, source_target_pairs={{12,0},{16,4},{20,8},{24,12},{28,16},{13,1},{17,5},{21,9},{25,13},... | collective-permute-start | bytes 1769480 | tf_op jit(solution)/shard_map/ppermute | solution.py:17
  488.2 44.2 %collective-permute-start.18 = (f32[2,256,288]{1,2,0:T(8,128)S(1)}, f32[2,256,288]{1,2,0:T(8,128)S(1)}, u32[]{:S(2)}, u32[]{:S(2)}) collective-permute-start(f32[2,256,288]{1,2,0:T(8,128)S(1)} %get-tuple-element.318), channel_id=1, source_target_pairs={{8,0},{12,4},{16,8},{20,12},{24,16},{28,20},{9,1},{13,5},{17,9},{2... | collective-permute-start | bytes 1769480 | tf_op jit(solution)/shard_map/ppermute | solution.py:17
  489.5 68.0 %collective-permute-start.19 = (f32[2,256,288]{1,2,0:T(8,128)S(1)}, f32[2,256,288]{1,2,0:T(8,128)S(1)}, u32[]{:S(2)}, u32[]{:S(2)}) collective-permute-start(f32[2,256,288]{1,2,0:T(8,128)S(1)} %get-tuple-element.319), channel_id=1, source_target_pairs={{4,0},{8,4},{12,8},{16,12},{20,16},{24,20},{28,24},{5,1},{9,5},{13... | collective-permute-start | bytes 1769480 | tf_op jit(solution)/shard_map/ppermute | solution.py:17
  490.8 66.7 %collective-permute-start.20 = (f32[2,256,288]{1,2,0:T(8,128)S(1)}, f32[2,256,288]{1,2,0:T(8,128)S(1)}, u32[]{:S(2)}, u32[]{:S(2)}) collective-permute-start(f32[2,256,288]{1,2,0:T(8,128)S(1)} %get-tuple-element.320), channel_id=1, source_target_pairs={{0,4},{4,8},{8,12},{12,16},{16,20},{20,24},{24,28},{1,5},{5,9},{9,... | collective-permute-start | bytes 1769480 | tf_op jit(solution)/shard_map/ppermute | solution.py:17
  529.8 27.7 %collective-permute-start.21 = (f32[2,256,288]{1,2,0:T(8,128)S(1)}, f32[2,256,288]{1,2,0:T(8,128)S(1)}, u32[]{:S(2)}, u32[]{:S(2)}) collective-permute-start(f32[2,256,288]{1,2,0:T(8,128)S(1)} %get-tuple-element.321), channel_id=1, source_target_pairs={{0,8},{4,12},{8,16},{12,20},{16,24},{20,28},{1,9},{5,13},{9,17},{1... | collective-permute-start | bytes 1769480 | tf_op jit(solution)/shard_map/ppermute | solution.py:17
  531.1 26.8 %collective-permute-start.22 = (f32[2,256,288]{1,2,0:T(8,128)S(1)}, f32[2,256,288]{1,2,0:T(8,128)S(1)}, u32[]{:S(2)}, u32[]{:S(2)}) collective-permute-start(f32[2,256,288]{1,2,0:T(8,128)S(1)} %get-tuple-element.323), channel_id=1, source_target_pairs={{0,12},{4,16},{8,20},{12,24},{16,28},{1,13},{5,17},{9,21},{13,25},... | collective-permute-start | bytes 1769480 | tf_op jit(solution)/shard_map/ppermute | solution.py:17
  532.5 36.9 %collective-permute-start.23 = (f32[2,256,288]{1,2,0:T(8,128)S(1)}, f32[2,256,288]{1,2,0:T(8,128)S(1)}, u32[]{:S(2)}, u32[]{:S(2)}) collective-permute-start(f32[2,256,288]{1,2,0:T(8,128)S(1)} %get-tuple-element.322), channel_id=1, source_target_pairs={{0,16},{4,20},{8,24},{12,28},{1,17},{5,21},{9,25},{13,29},{2,18},{... | collective-permute-start | bytes 1769480 | tf_op jit(solution)/shard_map/ppermute | solution.py:17
  570.6 41.9 %copy-start.10 = (f32[256,1152]{1,0:T(8,128)S(1)}, f32[256,1152]{1,0:T(8,128)}, u32[]{:S(2)}) copy-start(f32[256,1152]{1,0:T(8,128)} %get-tuple-element.327) | copy-start | bytes 3538948
  572.8 41.1 %copy-start.30 = (f32[1152]{0:T(1024)S(1)}, f32[1152]{0:T(1024)}, u32[]{:S(2)}) copy-start(f32[1152]{0:T(1024)} %param.26) | copy-start | bytes 13828
  572.8 41.1 %copy-start.36 = (f32[64]{0:T(128)S(1)}, f32[64]{0:T(128)}, u32[]{:S(2)}) copy-start(f32[64]{0:T(128)} %copy-done.35) | copy-start | bytes 772
  572.8 42.9 %copy-start.11 = (f32[64,1152]{1,0:T(8,128)S(1)}, f32[64,1152]{1,0:T(8,128)}, u32[]{:S(2)}) copy-start(f32[64,1152]{1,0:T(8,128)} %reduce-scatter.19.cloned.1.call-done) | copy-start | bytes 884740
  572.8 89.4 %reduce-scatter.31.cloned.1.call-start = ((), (), s32[]{:S(2)}) async-start(), calls=%async_computation.22 | async-start | bytes 4423680
  574.0 41.8 %copy-start.26 = (f32[4608]{0:T(1024)}, f32[4608]{0:T(1024)S(1)}, u32[]{:S(2)}) copy-start(f32[4608]{0:T(1024)S(1)} %dynamic_update_slice.29) | copy-start | bytes 55300
  574.0 41.8 %copy-start.34 = (f32[64]{0:T(128)S(1)}, f32[64]{0:T(128)}, u32[]{:S(2)}) copy-start(f32[64]{0:T(128)} %copy-done.33) | copy-start | bytes 772
  574.0 41.8 %copy-start.39 = (f32[64]{0:T(128)S(1)}, f32[64]{0:T(128)}, u32[]{:S(2)}) copy-start(f32[64]{0:T(128)} %copy-done.38) | copy-start | bytes 772
  621.7 174.7 %all-reduce.3.cloned.1.call-start = ((), (), s32[]{:S(2)}) async-start(), calls=%async_computation.24 | async-start | bytes 186368 | tf_op jit(solution)/shard_map/psum | solution.py:309
  623.1 47.7 %copy-start.28 = (f32[2,1152]{1,0:T(2,128)}, f32[2,1152]{1,0:T(2,128)S(1)}, u32[]{:S(2)}) copy-start(f32[2,1152]{1,0:T(2,128)S(1)} %dynamic_update_slice.28) | copy-start | bytes 27652
  670.8 218.1 %reduce-scatter.33.cloned.1.call-start = ((), (), s32[]{:S(2)}) async-start(), calls=%async_computation.23 | async-start | bytes 4644864
  691.2 267.8 %reduce-scatter.23.cloned.1.call-start = ((), (), s32[]{:S(2)}) async-start(), calls=%async_computation.18 | async-start | bytes 1990656 | tf_op jit(solution)/shard_map/reduce_scatter | solution.py:320
  694.1 372.5 %reduce-scatter.25.cloned.1.call-start = ((), (), s32[]{:S(2)}) async-start(), calls=%async_computation.19 | async-start | bytes 5971968 | tf_op jit(solution)/shard_map/reduce_scatter | solution.py:321
  697.6 477.2 %reduce-scatter.27.cloned.1.call-start = ((), (), s32[]{:S(2)}) async-start(), calls=%async_computation.20 | async-start | bytes 5971968 | tf_op jit(solution)/shard_map/reduce_scatter | solution.py:322
  702.2 622.0 %reduce-scatter.29.cloned.1.call-start = ((), (), s32[]{:S(2)}) async-start(), calls=%async_computation.21 | async-start | bytes 9289728 | tf_op jit(solution)/shard_map/reduce_scatter | solution.py:323
  796.4 527.8 %copy-start.43 = (f32[1152]{0:T(1024)S(1)}, f32[1152]{0:T(1024)}, u32[]{:S(2)}) copy-start(f32[1152]{0:T(1024)} %get-tuple-element.554) | copy-start | bytes 13828
  796.4 528.4 %copy-start.42 = (f32[1152]{0:T(1024)S(1)}, f32[1152]{0:T(1024)}, u32[]{:S(2)}) copy-start(f32[1152]{0:T(1024)} %get-tuple-element.558) | copy-start | bytes 13828
  (29 other events, 157.2 us)
Sparse Core Ops, SparseCore 0:
  10.2 83.1 all-gather.5
  95.6 54.0 all-gather.7
  236.4 22.8 reduce-scatter.14
  261.2 54.9 all-gather.9
  318.3 53.5 all-gather.11
  378.6 24.1 reduce-scatter.18
  405.4 25.6 reduce-scatter.16
  573.0 38.5 reduce-scatter.20
  621.9 40.3 reduce-scatter.30
  671.0 125.3 all-reduce.2
  800.0 88.8 reduce-scatter.32
  892.8 66.1 reduce-scatter.22
  963.2 103.3 reduce-scatter.24
  1070.6 104.0 reduce-scatter.26
  1178.9 145.3 reduce-scatter.28
where the time goes:
time: 1340 us; the launch traced here: 1330 us
  waiting for transfers between devices  987 us (74%)
  matrix products  108 us (8%)
  starting transfers between devices  75.7 us (6%)
  local copies, waits for them, and re-layouts  56.8 us (4%)
  blocking collectives  54.4 us (4%)
  other arithmetic  33.6 us (3%)
  between operations  16 us (1%)
    reduce_scatter x1, waiting for transfers between devices, shards(): lax.psum_scatter(grad_mod_w, 'dp', scatter_dimension=0, tiled=True)  149 us
    unnamed x17, waiting for transfers between devices  129 us
    reduce_scatter x1, waiting for transfers between devices, shards(): lax.psum_scatter(grad_down_w, 'dp', scatter_dimension=1, tiled=True)  108 us
    reduce_scatter x1, waiting for transfers between devices, shards(): lax.psum_scatter(grad_up_w, 'dp', scatter_dimension=0, tiled=True)  108 us
    psum x1, waiting for transfers between devices, shards(): lax.psum((silu_part, attn_b_placed, up_b_placed, mod_b_placed, grad_out_b...  87.2 us
    ppermute x24, waiting for transfers between devices, shifted(): return lax.ppermute(x, axis, pairs)  78.1 us
    ppermute x24, starting transfers between devices, shifted(): return lax.ppermute(x, axis, pairs)  74.8 us
    reduce_scatter x1, waiting for transfers between devices, shards(): lax.psum_scatter(grad_out_w, 'dp', scatter_dimension=1, tiled=True)  67.6 us
  transfers between devices with their start and end apart: 39, of which 24 were waited for; matrix products, arithmetic and copies ran while one was open for 7% of the time, Pallas kernels for 0%

commit v1 on v0

v1 whole, which is shorter than its diff:
```python
import jax
import jax.numpy as jnp
from jax import lax
from jax.sharding import Mesh
from jax.sharding import PartitionSpec as P

HD = 72
KV_ROWS = 152
BLOCK = 4

EPSILON = 1e-06
NEG_FILL = -1e30
DP = ("da", "db")
ALL = ("da", "db", "mp")
BF = jnp.bfloat16
F32 = jnp.float32


def normalize(values):
    average = jnp.mean(values, axis=-1, keepdims=True)
    centered = values - average
    spread_sq = jnp.mean(centered * centered, axis=-1, keepdims=True)
    inv_std = lax.rsqrt(spread_sq + EPSILON)
    return (centered * inv_std, inv_std)


def normalize_back(grad_hat, normed, inv_std):
    first = jnp.mean(grad_hat, axis=-1, keepdims=True)
    second = jnp.mean(grad_hat * normed, axis=-1, keepdims=True)
    return inv_std * (grad_hat - first - normed * second)


def gelu_tanh(values):
    return jax.nn.gelu(values, approximate=True)


def silu_slope(values):
    sigma = jax.nn.sigmoid(values)
    return sigma * (1.0 + values * (1.0 - sigma))


def dot(left, right, left_dim, right_dim, **kw):
    return lax.dot_general(
        left, right, (((left_dim,), (right_dim,)), ((), ())), preferred_element_type=F32, **kw
    )


def scatter_rows(partial):
    rows, width = partial.shape
    member = lax.axis_index("mp")
    low, high = member % 2, member // 2
    halves = partial.reshape(2, 2, rows // 4, width)
    keep = lax.dynamic_index_in_dim(halves, low, 1, keepdims=False)
    give = lax.dynamic_index_in_dim(halves, 1 - low, 1, keepdims=False).astype(BF)
    kept = keep + lax.ppermute(give, "mp", [(m, m ^ 1) for m in range(4)]).astype(F32)
    keep = lax.dynamic_index_in_dim(kept, high, 0, keepdims=False)
    give = lax.dynamic_index_in_dim(kept, 1 - high, 0, keepdims=False).astype(BF)
    return keep + lax.ppermute(give, "mp", [(m, m ^ 2) for m in range(4)]).astype(F32)


def neighbours(block_kv, blocks):
    if blocks == 2:
        return [lax.ppermute(block_kv, "da", [(0, 1), (1, 0)])]
    return [
        lax.ppermute(block_kv, "da", [(i, i + 1) for i in range(blocks - 1)]),
        lax.ppermute(block_kv, "da", [(i + 1, i) for i in range(blocks - 1)]),
    ]


def return_grads(pieces, blocks):
    if blocks == 2:
        return lax.ppermute(pieces[0], "da", [(0, 1), (1, 0)]).astype(F32)
    return lax.ppermute(pieces[0], "da", [(i + 1, i) for i in range(blocks - 1)]).astype(
        F32
    ) + lax.ppermute(pieces[1], "da", [(i, i + 1) for i in range(blocks - 1)]).astype(F32)


def shards(
    tokens,
    conditioning,
    segments,
    live_counts,
    attn_weight,
    attn_bias,
    out_weight,
    out_bias,
    up_weight,
    up_bias,
    down_weight,
    down_bias,
    mod_weight,
    mod_bias,
    cotangent,
):
    tok_rows, width = tokens.shape
    latents = conditioning.shape[0]
    columns = attn_weight.shape[2]
    heads_here = columns // HD
    weight_rows = up_weight.shape[0]
    hidden_cols = up_bias.shape[0]
    mod_cols = mod_bias.shape[0]
    score_scale = 1.0 / HD**0.5
    blocks = lax.axis_size("da")
    group = lax.axis_size("mp")
    n_dp = blocks * BLOCK
    share = tok_rows // group
    member = lax.axis_index("mp")
    block_at = lax.axis_index("db")
    dp_at = lax.axis_index("da") * BLOCK + block_at
    row_start = member * share
    block_rows = BLOCK * tok_rows

    def own_rows(values):
        return lax.dynamic_slice_in_dim(values, row_start, share, 0)

    attn_local = jnp.transpose(
        attn_weight.reshape(3, weight_rows, heads_here, HD), (1, 2, 0, 3)
    )
    attn_local = attn_local[:, :, jnp.array([1, 2, 0])].reshape(weight_rows, 3 * columns)
    attn_full = lax.all_gather(attn_local, DP, axis=0, tiled=True)
    out_t = lax.all_gather(out_weight.T, DP, axis=0, tiled=True)
    up_full = lax.all_gather(up_weight, DP, axis=0, tiled=True)
    down_t = lax.all_gather(down_weight.T, DP, axis=0, tiled=True)

    cond_vals = conditioning.astype(F32)
    silu_cond = jax.nn.silu(cond_vals).astype(BF)
    silu_own = lax.dynamic_slice_in_dim(silu_cond, dp_at * weight_rows, weight_rows, 1)
    mod_part = dot(silu_own, mod_weight, 1, 0)
    mod_part = mod_part + jnp.where(dp_at == 0, 1.0, 0.0) * mod_bias
    mod_parts = lax.all_gather(mod_part, ALL, axis=0, tiled=False)
    modulation = jnp.sum(mod_parts.reshape(n_dp, group, latents, mod_cols), axis=0)
    modulation = jnp.transpose(modulation, (1, 0, 2)).reshape(latents, 6 * width)
    one_hot = (segments[:, None] == jnp.arange(latents, dtype=jnp.int32)[None, :]).astype(F32)
    one_hot_s = own_rows(one_hot)

    def modulate(hot, first, last):
        return jnp.dot(
            hot, modulation[:, first * width : last * width], precision=lax.Precision.HIGHEST
        )

    shift_attn, scale_attn = jnp.split(modulate(one_hot, 0, 2), 2, axis=1)
    gate_mlp = modulate(one_hot, 5, 6)
    scale_attn_s, gate_attn_s, shift_mlp_s, scale_mlp_s, gate_mlp_s = jnp.split(
        modulate(one_hot_s, 1, 6), 5, axis=1
    )
    live = (jnp.arange(tok_rows, dtype=jnp.int32) < live_counts[0]).astype(F32)[:, None]
    live_s = own_rows(live)
    token_vals = tokens.astype(F32)
    token_s = own_rows(token_vals)
    normed_one, inv_one = normalize(token_vals)
    attn_input = (normed_one * (1.0 + scale_attn) + shift_attn).astype(BF)

    head_bias = attn_bias.reshape(2, heads_here, HD)
    bias_t = jnp.stack([jnp.zeros_like(head_bias[0]), head_bias[1], head_bias[0]], axis=1)
    kvq_t = (dot(attn_full, attn_input, 0, 1) + bias_t.reshape(3 * columns)[:, None]).astype(BF)
    kvq_t = kvq_t.reshape(heads_here, 3 * HD, tok_rows)
    tags = jnp.stack(
        [jnp.where(live[:, 0] > 0.0, segments + 1, 0).astype(BF), (segments + 1).astype(BF)]
    )
    tags = jnp.pad(tags, ((0, KV_ROWS - 2 * HD - 2), (0, 0)))
    tags = jnp.broadcast_to(tags[None], (heads_here,) + tags.shape)
    sent = jnp.concatenate([kvq_t[:, : 2 * HD], tags, kvq_t[:, 2 * HD :]], axis=1)
    got = lax.all_to_all(sent, "db", 0, 0)
    kv_own = got[:, :KV_ROWS]
    kv_all = jnp.stack([kv_own] + neighbours(kv_own, blocks))
    key_blocks = kv_all.shape[0]
    keys_seen = key_blocks * block_rows
    kv_t = jnp.transpose(kv_all, (2, 0, 1, 3)).reshape(KV_ROWS, keys_seen)
    key_t, value_t = kv_t[:HD], kv_t[HD : 2 * HD]
    key_tag = kv_t[2 * HD].astype(F32)
    query_tag = kv_t[2 * HD + 1, :block_rows].astype(F32)
    query_t = jnp.transpose(got[:, KV_ROWS:], (1, 0, 2)).reshape(HD, block_rows)
    self_mask = (
        jnp.arange(keys_seen, dtype=jnp.int32)[None, :]
        == jnp.arange(block_rows, dtype=jnp.int32)[:, None]
    )
    allowed = (key_tag[None, :] == query_tag[:, None]) | self_mask

    def masked_scores():
        return jnp.where(allowed, dot(query_t, key_t, 0, 0) * score_scale, NEG_FILL)

    scores = masked_scores()
    row_max = jnp.max(scores, axis=-1, keepdims=True)
    log_total = row_max + jnp.log(jnp.sum(jnp.exp(scores - row_max), axis=-1, keepdims=True))
    attn_exact = jnp.exp(scores - log_total)
    attn_probs = attn_exact.astype(BF)
    head_attended = dot(value_t, attn_probs, 1, 1).astype(BF)

    def to_owners(head_rows):
        rows = head_rows.shape[0]
        parts = jnp.transpose(head_rows.reshape(rows, BLOCK, tok_rows), (1, 0, 2))
        return lax.all_to_all(parts, "db", 0, 0).reshape(heads_here * rows, tok_rows)

    attended_t = to_owners(head_attended)
    attn_out_s = scatter_rows(dot(attended_t, out_t, 0, 1)) + out_bias
    mid_s = token_s + live_s * gate_attn_s * attn_out_s
    normed_two_s, inv_two_s = normalize(mid_s)
    mlp_input_s = (normed_two_s * (1.0 + scale_mlp_s) + shift_mlp_s).astype(BF)
    mlp_input = lax.all_gather(mlp_input_s, "mp", axis=0, tiled=True)
    hidden_pre = dot(mlp_input, up_full, 1, 0) + up_bias
    hidden = gelu_tanh(hidden_pre).astype(BF)

    grad_result = cotangent.astype(F32)
    grad_result_s = own_rows(grad_result)
    grad_mlp = grad_result * live * gate_mlp
    grad_mlp_b = grad_mlp.astype(BF)
    grad_hidden = dot(grad_mlp_b, down_t, 1, 0)
    grad_pre = jax.vjp(gelu_tanh, hidden_pre)[1](grad_hidden)[0]
    grad_pre_b = grad_pre.astype(BF)
    grad_mlp_in_s = scatter_rows(dot(grad_pre_b, up_full, 1, 1))
    grad_mid_s = grad_result_s + normalize_back(
        grad_mlp_in_s * (1.0 + scale_mlp_s), normed_two_s, inv_two_s
    )
    grad_attn_s = grad_mid_s * live_s * gate_attn_s
    grad_attn_b = lax.all_gather(grad_attn_s.astype(BF), "mp", axis=0, tiled=True)
    grad_down_w = dot(grad_mlp_b, hidden, 0, 0)
    grad_up_w = dot(mlp_input, grad_pre_b, 0, 0)
    mlp_w = lax.psum_scatter(
        jnp.concatenate([grad_up_w.astype(BF), grad_down_w.astype(BF)], axis=1),
        DP,
        scatter_dimension=0,
        tiled=True,
    ).astype(F32)
    up_w_out, down_w_out = mlp_w[:, :hidden_cols], mlp_w[:, hidden_cols:].T
    mlp_out_s = scatter_rows(dot(hidden, down_t, 1, 1)) + down_bias
    result_s = (mid_s + live_s * gate_mlp_s * mlp_out_s).astype(BF)

    grad_attended_t = dot(out_t, grad_attn_b, 0, 1).astype(BF)
    got_grad = lax.all_to_all(grad_attended_t.reshape(heads_here, HD, tok_rows), "db", 0, 0)
    grad_t = jnp.transpose(got_grad, (1, 0, 2)).reshape(HD, block_rows)
    grad_probs = dot(grad_t, value_t, 0, 0)
    delta = jnp.sum(grad_t.astype(F32) * head_attended.astype(F32), axis=0)[:, None]
    grad_scores = (attn_exact * (grad_probs - delta)).astype(BF)
    grad_query_t = dot(key_t, grad_scores, 1, 1) * score_scale
    grad_key_t = dot(query_t, grad_scores, 1, 0) * score_scale
    grad_value_t = dot(grad_t, attn_probs, 1, 0)
    grad_kv_t = jnp.concatenate([grad_key_t, grad_value_t])
    others = [
        grad_kv_t[:, i * block_rows : (i + 1) * block_rows].astype(BF)
        for i in range(1, key_blocks)
    ]
    grad_kv_own = grad_kv_t[:, :block_rows] + return_grads(others, blocks)
    attn_b_part = jnp.concatenate(
        [jnp.sum(grad_query_t, axis=1), jnp.sum(grad_kv_own[HD:], axis=1)]
    )
    grad_kvq_t = to_owners(jnp.concatenate([grad_kv_own, grad_query_t]).astype(BF))
    grad_attn_w = dot(attn_input, grad_kvq_t, 0, 1)
    grad_out_w = dot(grad_attn_b, attended_t, 0, 1)
    attn_w = lax.psum_scatter(
        jnp.concatenate([grad_attn_w.astype(BF), grad_out_w.astype(BF)], axis=1),
        DP,
        scatter_dimension=0,
        tiled=True,
    ).astype(F32)
    out_w_out = attn_w[:, 3 * columns :].T
    attn_w_out = attn_w[:, : 3 * columns].reshape(weight_rows, heads_here, 3, HD)
    attn_w_out = jnp.transpose(attn_w_out[:, :, jnp.array([2, 0, 1])], (2, 0, 1, 3)).reshape(
        3, weight_rows, columns
    )
    grad_attn_in_s = scatter_rows(dot(grad_kvq_t, attn_full, 0, 1))
    normed_one_s = own_rows(normed_one)
    inv_one_s = own_rows(inv_one)
    grad_tokens_s = grad_mid_s + normalize_back(
        grad_attn_in_s * (1.0 + scale_attn_s), normed_one_s, inv_one_s
    )

    grad_mod_rows = jnp.concatenate(
        [
            grad_attn_in_s,
            grad_attn_in_s * normed_one_s,
            grad_mid_s * live_s * attn_out_s,
            grad_mlp_in_s,
            grad_mlp_in_s * normed_two_s,
            grad_result_s * live_s * mlp_out_s,
        ],
        axis=1,
    )
    grad_mod_share = jnp.dot(one_hot_s.T, grad_mod_rows, precision=lax.Precision.HIGHEST)
    piece_cols = mod_cols // n_dp
    pieces = jnp.transpose(
        grad_mod_share.reshape(latents, group, n_dp, piece_cols), (2, 1, 0, 3)
    ).reshape(n_dp * group, latents * piece_cols)
    own_piece = jnp.sum(lax.all_to_all(pieces, ALL, 0, 0), axis=0)
    small = jnp.concatenate(
        [
            own_piece,
            attn_b_part,
            jnp.sum(grad_pre, axis=0),
            jnp.sum(own_rows(grad_mlp), axis=0),
            jnp.sum(grad_attn_s, axis=0),
        ]
    )
    small_all = lax.all_gather(small, ALL, axis=0, tiled=False).reshape(n_dp, group, -1)
    small_own = lax.dynamic_index_in_dim(small_all, member, 1, keepdims=False)
    at = own_piece.shape[0]
    own_cols = jnp.transpose(
        small_own[:, :at].reshape(n_dp, latents, piece_cols), (1, 0, 2)
    ).reshape(latents, mod_cols)
    attn_b_own = small_own[:, at : at + 2 * HD].reshape(blocks, heads_here, 2, HD)
    attn_b_out = jnp.transpose(jnp.sum(attn_b_own, axis=0), (1, 0, 2)).reshape(2, columns)
    at = at + 2 * HD
    up_b_out = jnp.sum(small_own[:, at : at + hidden_cols], axis=0)
    at = at + hidden_cols
    both_b = jnp.sum(small_all[:, :, at:], axis=(0, 1))
    down_b_all, out_b_all = both_b[:width], both_b[width:]
    mod_w_out = jnp.dot(silu_own.astype(F32).T, own_cols, precision=lax.Precision.HIGHEST)
    mod_b_out = jnp.sum(own_cols, axis=0)
    silu_part = jnp.dot(own_cols, mod_weight.astype(F32).T, precision=lax.Precision.HIGHEST)
    silu_parts = lax.all_gather(silu_part, ALL, axis=0, tiled=False)
    silu_parts = jnp.sum(silu_parts.reshape(n_dp, group, latents, weight_rows), axis=1)
    grad_silu = jnp.transpose(silu_parts, (1, 0, 2)).reshape(latents, width)
    grad_conditioning = grad_silu * silu_slope(cond_vals)
    return (
        result_s,
        grad_tokens_s,
        grad_conditioning,
        attn_w_out,
        attn_b_out,
        out_w_out,
        out_b_all,
        up_w_out,
        up_b_out,
        down_w_out,
        down_b_all,
        mod_w_out,
        mod_b_out,
    )


def solution(mesh):
    n_dp = mesh.shape["dp"]
    fine = Mesh(mesh.devices.reshape(n_dp // BLOCK, BLOCK, mesh.shape["mp"]), ALL)
    placed = (
        P(DP, None),
        P(),
        P(DP),
        P(DP),
        P(None, DP, "mp"),
        P(None, "mp"),
        P("mp", DP),
        P(),
        P(DP, "mp"),
        P("mp"),
        P("mp", DP),
        P(),
        P(DP, "mp"),
        P("mp"),
        P(DP, None),
    )
    return jax.shard_map(
        shards,
        mesh=fine,
        in_specs=placed,
        out_specs=(
            P(ALL, None),
            P(ALL, None),
            P(),
            P(None, DP, "mp"),
            P(None, "mp"),
            P("mp", DP),
            P(),
            P(DP, "mp"),
            P("mp"),
            P("mp", DP),
            P(),
            P(DP, "mp"),
            P("mp"),
        ),
        check_vma=False,
    )
```

time: 1340 us -> 628 us (0.47)
  waiting for transfers between devices: 987 us -> 297 us
  blocking collectives: 54.4 us -> 167 us
  matrix products: 108 us -> 44.9 us
  starting transfers between devices: 75.7 us -> 16.2 us
    reduce_scatter x8 -> x0, waiting for transfers between devices: 535 us -> none  [the longest x1 149 us: shards(): lax.psum_scatter(grad_mod_w, 'dp', scatter_dimension=0, tiled=True)]
    all_gather x4 -> x3, waiting for transfers between devices: 158 us -> 9.73 us  [the longest x1 9.73 us: shards(): down_t = lax.all_gather(down_weight.T, DP, axis=0, tiled=True)]
    unnamed x17 -> x9, waiting for transfers between devices: 129 us -> 233 us
    all_gather x3 -> x4, blocking collectives: 47.5 us -> 141 us  [the longest x1 48.1 us: shards(): mod_parts = lax.all_gather(mod_part, ALL, axis=0, tiled=False)]
    psum x1 -> x0, waiting for transfers between devices: 87.2 us -> none  [shards(): lax.psum((silu_part, attn_b_placed, up_b_placed, mod_b_placed, grad_out_b...]
    ppermute x24 -> x10, starting transfers between devices: 74.8 us -> 6.13 us  [the longest x4 3.92 us: scatter_rows(): lax.ppermute(give, 'mp', [(m, m ^ 2) for m in range(4)]).astype(F32)]
    dot_general x46 -> x25, matrix products: 104 us -> 44.9 us  [the longest x19 37.8 us: dot(): lax.dot_general(left, right, (((left_dim,), (right_dim,)), ((), ())), pre...]
    ppermute x24 -> x10, waiting for transfers between devices: 78.1 us -> 26.9 us  [the longest x4 15.6 us: scatter_rows(): lax.ppermute(give, 'mp', [(m, m ^ 2) for m in range(4)]).astype(F32)]
  transfers between devices with their start and end apart: 39 -> 19, of which waited for: 24 -> 13; matrix products, arithmetic and copies ran while one was open for 7% -> 13% of each run, Pallas kernels for 0% -> 0%
where the time goes in v1:
time: 628 us; the launch traced here: 619 us
  waiting for transfers between devices  297 us (47%)
  blocking collectives  167 us (27%)
  matrix products  44.9 us (7%)
  local copies, waits for them, and re-layouts  44.6 us (7%)
  other arithmetic  32.4 us (5%)
  between operations  16.6 us (3%)
  starting transfers between devices  16.2 us (3%)
    unnamed x9, waiting for transfers between devices  233 us
    all_gather x1, blocking collectives, shards(): mod_parts = lax.all_gather(mod_part, ALL, axis=0, tiled=False)  48.1 us
    all_gather x1, blocking collectives, shards(): out_t = lax.all_gather(out_weight.T, DP, axis=0, tiled=True)  43.4 us
    all_gather x1, blocking collectives, shards(): silu_parts = lax.all_gather(silu_part, ALL, axis=0, tiled=False)  42.3 us
    dot_general x19, matrix products, dot(): lax.dot_general(left, right, (((left_dim,), (right_dim,)), ((), ())), pre...  37.8 us
    unnamed x143, local copies, waits for them, and re-layouts  24.3 us
    ppermute x4, waiting for transfers between devices, scatter_rows(): lax.ppermute(give, 'mp', [(m, m ^ 2) for m in range(4)]).astype(F32)  15.6 us
    all_to_all x1, waiting for transfers between devices, shards(): got = lax.all_to_all(sent, 'db', 0, 0)  14.3 us
  transfers between devices with their start and end apart: 19, of which 13 were waited for; matrix products, arithmetic and copies ran while one was open for 13% of the time, Pallas kernels for 0%

profile of v1, /device:TPU:0, one launch (start us, length us, event | category | flops | bytes accessed | tf_op | source)
XLA Modules:
  0.0 618.9 jit_solution(1780278821378144237)
XLA Ops:
  7.3 1.3 reshape.224
  12.2 48.1 %all-gather.3 = f32[32,4,1728]{2,1,0:T(4,128)S(1)} all-gather(f32[1,4,1728]{2,1,0:T(4,128)S(1)} %fusion.2), channel_id=2, replica_groups=mesh['da'=2,'db'=4,'mp'=4] {'da','db','mp'}, dimensions={0}, use_global_device_ids=true | all-gather | bytes 912384 | tf_op jit(solution)/shard_map/all_gather | solution.py:130
  62.3 1.1 fusion.47
  63.5 1.4 subtract_multiply_fusion
  64.9 2.6 fusion.5
  68.4 3.5 all-to-all-start
  72.6 14.3 %all-to-all-done = bf16[4,224,256]{2,1,0:T(8,128)(2,1)S(1)} async-done(((bf16[4,224,256]{2,1,0:T(8,128)(2,1)}), bf16[4,224,256]{2,1,0:T(8,128)(2,1)S(1)}, u32[]{:S(2)}, u32[]{:S(2)}) %all-to-all-start) | async-done | bytes 458784 | tf_op jit(solution)/shard_map/all_to_all | solution.py:163
  87.1 43.4 %all_gather.39 = bf16[1152,288]{1,0:T(8,128)(2,1)S(1)} all-gather(bf16[144,288]{1,0:T(8,128)(2,1)S(1)} %bitcast.247), channel_id=1, replica_groups=mesh['da'=2,'db'=4,'mp'=4] {'da','db'}, dimensions={0}, use_global_device_ids=true | all-gather | bytes 746496 | tf_op jit(solution)/shard_map/all_gather | solution.py:121
  131.8 1.3 reshape.227
  133.8 3.6 fusion.76
  137.4 1.3 exponential_reduce_fusion
  138.7 2.0 copy-done.1
  140.7 3.1 fusion.1
  144.2 3.6 convolution_convert_fusion.4
  148.5 3.5 all-to-all-start.1
  152.1 7.1 %all-to-all-done.1 = bf16[4,72,256]{2,1,0:T(8,128)(2,1)S(1)} async-done(((bf16[4,72,256]{2,1,0:T(8,128)(2,1)}), bf16[4,72,256]{2,1,0:T(8,128)(2,1)S(1)}, u32[]{:S(2)}, u32[]{:S(2)}) %all-to-all-start.1) | async-done | bytes 147488 | tf_op jit(solution)/shard_map/all_to_all | solution.py:192
  160.1 1.5 fusion.14
  162.3 1.1 convert_element_type.191
  163.4 2.2 convert_element_type.220
  165.8 2.5 convolution_multiply_fusion
  170.2 5.5 collective-permute-done.2
  175.7 1.2 fusion.72
  177.4 7.5 %all_gather.40 = bf16[256,1152]{1,0:T(8,128)(2,1)} all-gather(bf16[64,1152]{1,0:T(8,128)(2,1)S(1)} %fusion.24), channel_id=1, replica_groups=mesh['da'=2,'db'=4,'mp'=4] {'mp'}, dimensions={0}, use_global_device_ids=true | all-gather | bytes 737280 | tf_op jit(solution)/shard_map/all_gather | solution.py:199
  184.9 4.0 convolution_add_fusion
  188.9 9.7 %all-gather.13.cloned.1.call-done = bf16[1152,1152]{1,0:T(8,128)(2,1)} async-done(((bf16[144,1152]{1,0:T(8,128)(2,1)}), bf16[1152,1152]{1,0:T(8,128)(2,1)}) %all-gather.13.cloned.1.call-update) | async-done | bytes 2654224 | tf_op jit(solution)/shard_map/all_gather | solution.py:123
  198.6 4.5 fusion.77
  206.9 1.5 collective-permute-start.6
  208.6 1.4 collective-permute-start.4
  210.0 3.7 collective-permute-done.6
  213.9 2.4 collective-permute-done.4
  216.4 2.0 fusion.51
  218.6 7.6 %all_gather.43 = bf16[256,1152]{1,0:T(8,128)(2,1)S(1)} all-gather(bf16[64,1152]{1,0:T(8,128)(2,1)S(1)} %fusion.52), channel_id=1, replica_groups=mesh['da'=2,'db'=4,'mp'=4] {'mp'}, dimensions={0}, use_global_device_ids=true | all-gather | bytes 737280 | tf_op jit(solution)/shard_map/all_gather | solution.py:215
  226.7 8.2 %all_to_all.30 = bf16[4,72,256]{2,1,0:T(8,128)(2,1)S(1)} all-to-all(bf16[4,72,256]{2,1,0:T(8,128)(2,1)S(1)} %bitcast.233), channel_id=1, replica_groups=mesh['da'=2,'db'=4,'mp'=4] {'db'}, dimensions={0} | all-to-all | bytes 294912 | tf_op jit(solution)/shard_map/all_to_all | solution.py:229
  235.8 2.3 multiply_convert_fusion
  239.0 1.9 collective-permute-start.7
  241.0 2.0 fusion.74
  243.0 11.2 %collective-permute-done.7 = bf16[144,1024]{1,0:T(8,128)(2,1)S(1)} collective-permute-done((bf16[144,1024]{1,0:T(8,128)(2,1)S(1)}, bf16[144,1024]{1,0:T(8,128)(2,1)S(1)}, u32[]{:S(2)}, u32[]{:S(2)}) %collective-permute-start.7) | collective-permute-done | bytes 294944 | tf_op jit(solution)/shard_map/ppermute | solution.py:72
  255.2 10.4 %all_to_all.31 = bf16[4,216,256]{2,1,0:T(8,128)(2,1)S(1)} all-to-all(bf16[4,216,256]{2,1,0:T(8,128)(2,1)S(1)} %maximum_bitcast_fusion.1), channel_id=1, replica_groups=mesh['da'=2,'db'=4,'mp'=4] {'db'}, dimensions={0} | all-to-all | bytes 884736 | tf_op jit(solution)/shard_map/all_to_all | solution.py:192
  266.5 2.6 fusion.3
  272.1 1.3 bitcast_add_fusion
  274.3 1.2 convolution_convert_fusion.3
  275.6 4.0 collective-permute-done.9
  284.0 2.6 all-to-all-start.4
  286.7 2.0 convolution_convert_fusion.2
  288.7 5.9 all-to-all-done.4
  296.2 2.0 pad_maximum_fusion.1
  298.2 3.3 copy.166
  302.5 2.0 convolution_convert_fusion.1
  304.6 1.2 convolution_convert_fusion
  305.8 2.8 pad_maximum_fusion
  308.6 8.6 %copy.168 = bf16[1152,2304]{1,0:T(8,128)(2,1)} copy(bf16[1152,2304]{0,1:T(8,128)(2,1)} %pad_maximum_fusion) | data formatting | bytes 10616832
  317.2 104.5 %all-reduce.4.cloned.1.call-done = f32[142848]{0:T(1024)} async-done(((f32[142848]{0:T(1024)}), f32[142848]{0:T(1024)}) %all-reduce.4.cloned.1.call-update) | async-done | bytes 571408
  421.7 1.5 reshape.237
  424.1 42.3 %all-gather.4 = f32[32,4,144]{2,1,0:T(4,128)S(1)} all-gather(f32[1,4,144]{2,1,0:T(4,128)S(1)} %convolution_bitcast_fusion), channel_id=4, replica_groups=mesh['da'=2,'db'=4,'mp'=4] {'da','db','mp'}, dimensions={0}, use_global_device_ids=true | all-gather | bytes 76032 | tf_op jit(solution)/shard_map/all_gather | solution.py:309
  469.5 1.6 fusion.79
  471.7 26.1 %reduce-scatter.7.cloned.1.call-done = bf16[144,1152]{1,0:T(8,128)(2,1)} async-done(((bf16[1152,1152]{1,0:T(8,128)(2,1)}), bf16[144,1152]{1,0:T(8,128)(2,1)}) %reduce-scatter.7.cloned.1.call-update) | async-done | bytes 331792
  497.9 1.2 copy.167
  501.0 1.2 copy.165
  504.0 100.8 %reduce-scatter.9.cloned.1.call-done = bf16[144,2304]{1,0:T(8,128)(2,1)} async-done(((bf16[1152,2304]{1,0:T(8,128)(2,1)}), bf16[144,2304]{1,0:T(8,128)(2,1)}) %reduce-scatter.9.cloned.1.call-update) | async-done | bytes 663568
  604.8 1.5 copy.169
  606.3 1.6 convert_element_type.247
  607.9 1.2 copy.161
  609.1 1.3 slice_bitcast_fusion
  610.5 1.2 copy.162
  (286 shorter events, 41.1 us)
Async XLA Ops:
  7.2 4.8 copy-start
  7.2 57.7 %all-gather.9.cloned.1.call-start = ((), (), s32[]{:S(2)}) async-start(), calls=%async_computation.7 | async-start | bytes 2322432 | tf_op jit(solution)/shard_map/all_gather | solution.py:120
  9.3 2.6 copy-start.44
  9.3 2.7 copy-start.51
  11.1 173.8 %all-gather.11.cloned.1.call-start = ((), (), s32[]{:S(2)}) async-start(), calls=%async_computation.8 | async-start | bytes 2985984 | tf_op jit(solution)/shard_map/all_gather | solution.py:122
  12.0 49.4 %copy-start.56 = (f32[2,288]{1,0:T(2,128)S(1)}, f32[2,288]{1,0:T(2,128)}, u32[]{:S(2)}) copy-start(f32[2,288]{1,0:T(2,128)} %param.22) | copy-start | bytes 6916
  12.0 49.7 %copy-start.47 = (s32[256]{0:T(256)S(1)}, s32[256]{0:T(256)}, u32[]{:S(2)}) copy-start(s32[256]{0:T(256)} %param.19) | copy-start | bytes 3076
  12.0 49.8 %copy-start.3 = (bf16[256,1152]{1,0:T(8,128)(2,1)S(1)}, bf16[256,1152]{1,0:T(8,128)(2,1)}, u32[]{:S(2)}) copy-start(bf16[256,1152]{1,0:T(8,128)(2,1)} %param.17) | copy-start | bytes 1769476
  62.3 2.6 copy-start.54
  64.9 2.6 copy-start.21
  67.6 19.5 %copy-start.43 = (bf16[288,144]{0,1:T(8,128)(2,1)S(1)}, bf16[288,144]{0,1:T(8,128)(2,1)}, u32[]{:S(2)}) copy-start(bf16[288,144]{0,1:T(8,128)(2,1)} %param.23) | copy-start | bytes 248836
  68.4 18.5 %all-to-all-start = ((bf16[4,224,256]{2,1,0:T(8,128)(2,1)}), bf16[4,224,256]{2,1,0:T(8,128)(2,1)S(1)}, u32[]{:S(2)}, u32[]{:S(2)}) async-start(bf16[4,224,256]{2,1,0:T(8,128)(2,1)} %pad_maximum_fusion.3), calls=%async_computation | async-start | bytes 917504 | tf_op jit(solution)/shard_map/all_to_all | solution.py:163
  71.9 126.8 %all-gather.13.cloned.1.call-start = ((), (), s32[]{:S(2)}) async-start(), calls=%async_computation.9 | async-start | bytes 2985984 | tf_op jit(solution)/shard_map/all_gather | solution.py:123
  87.0 44.1 %collective-permute-start = (bf16[4,152,256]{2,1,0:T(8,128)(2,1)S(1)}, bf16[4,152,256]{2,1,0:T(8,128)(2,1)S(1)}, u32[]{:S(2)}, u32[]{:S(2)}) collective-permute-start(bf16[4,152,256]{2,1,0:T(8,128)(2,1)S(1)} %get-tuple-element.112), channel_id=1, source_target_pairs={{0,16},{16,0},{1,17},{17,1},{2,18},{18,2},{3,19},{19,3},{4,20},{20... | collective-permute-start | bytes 933896 | tf_op jit(solution)/shard_map/ppermute | solution.py:63
  131.8 5.6 copy-start.31
  137.4 3.3 copy-start.1
  147.8 12.3 %copy-start.26 = (bf16[72,1024]{1,0:T(8,128)(2,1)}, bf16[72,1024]{1,0:T(8,128)(2,1)S(1)}, u32[]{:S(2)}) copy-start(bf16[72,1024]{1,0:T(8,128)(2,1)S(1)} %convolution_convert_fusion.4) | copy-start | bytes 442372
  148.5 10.7 %all-to-all-start.1 = ((bf16[4,72,256]{2,1,0:T(8,128)(2,1)}), bf16[4,72,256]{2,1,0:T(8,128)(2,1)S(1)}, u32[]{:S(2)}, u32[]{:S(2)}) async-start(bf16[4,72,256]{2,1,0:T(8,128)(2,1)} %bitcast.201), calls=%async_computation.1 | async-start | bytes 294912 | tf_op jit(solution)/shard_map/all_to_all | solution.py:192
  162.3 6.0 collective-permute-start.1
  165.8 52.7 %copy-start.48 = (f32[64]{0:T(128)}, f32[64]{0:T(128)S(1)}, u32[]{:S(2)}) copy-start(f32[64]{0:T(128)S(1)} %dynamic-slice.6) | copy-start | bytes 772
  165.8 3.7 copy-start.36
  168.3 7.4 %copy-start.45 = (f32[1152]{0:T(1024)S(1)}, f32[1152]{0:T(1024)}, u32[]{:S(2)}) copy-start(f32[1152]{0:T(1024)} %param.24) | copy-start | bytes 13828
  169.4 7.6 %copy-start.13 = (f32[2,64,1152]{2,1,0:T(8,128)}, f32[2,64,1152]{2,1,0:T(8,128)S(1)}, u32[]{:S(2)}) copy-start(f32[2,64,1152]{2,1,0:T(8,128)S(1)} %bitcast_add_fusion.3) | copy-start | bytes 1769476
  169.4 6.3 %collective-permute-start.2 = (bf16[64,1152]{1,0:T(8,128)(2,1)S(1)}, bf16[64,1152]{1,0:T(8,128)(2,1)S(1)}, u32[]{:S(2)}, u32[]{:S(2)}) collective-permute-start(bf16[64,1152]{1,0:T(8,128)(2,1)S(1)} %fusion.39), channel_id=1, source_target_pairs={{0,2},{1,3},{2,0},{3,1},{4,6},{5,7},{6,4},{7,5},{8,10},{9,11},{10,... | collective-permute-start | bytes 442376 | tf_op jit(solution)/shard_map/ppermute | solution.py:58
  170.2 14.6 %copy-start.63 = (f32[1152]{0:T(1024)S(1)}, f32[1152]{0:T(1024)}, u32[]{:S(2)}) copy-start(f32[1152]{0:T(1024)} %param.26) | copy-start | bytes 13828
  177.2 39.2 %copy-start.52 = (f32[64]{0:T(128)}, f32[64]{0:T(128)S(1)}, u32[]{:S(2)}) copy-start(f32[64]{0:T(128)S(1)} %add_rsqrt_fusion.1) | copy-start | bytes 772
  198.6 4.6 copy-start.61
  204.3 2.5 collective-permute-start.5
  206.7 1.8 collective-permute-start.3
  206.8 29.0 %slice-start = ((s8[8388608]{0:T(1024)(128)(4,1)}), s8[4194304]{0:T(1024)(128)(4,1)S(1)}, s32[]{:S(2)}) async-start(s8[8388608]{0:T(1024)(128)(4,1)} %bitcast.206), calls=%async_computation.13 | async-start | bytes 8388608
  206.9 7.1 %copy-start.8 = (f32[2,64,1152]{2,1,0:T(8,128)}, f32[2,64,1152]{2,1,0:T(8,128)S(1)}, u32[]{:S(2)}) copy-start(f32[2,64,1152]{2,1,0:T(8,128)S(1)} %bitcast_add_fusion.1) | copy-start | bytes 1769476
  206.9 9.5 %copy-start.46 = (f32[1152]{0:T(1024)S(1)}, f32[1152]{0:T(1024)}, u32[]{:S(2)}) copy-start(f32[1152]{0:T(1024)} %param.28) | copy-start | bytes 13828
  206.9 6.8 %collective-permute-start.6 = (bf16[64,1152]{1,0:T(8,128)(2,1)S(1)}, bf16[64,1152]{1,0:T(8,128)(2,1)S(1)}, u32[]{:S(2)}, u32[]{:S(2)}) collective-permute-start(bf16[64,1152]{1,0:T(8,128)(2,1)S(1)} %fusion.41), channel_id=1, source_target_pairs={{0,2},{1,3},{2,0},{3,1},{4,6},{5,7},{6,4},{7,5},{8,10},{9,11},{10,... | collective-permute-start | bytes 442376 | tf_op jit(solution)/shard_map/ppermute | solution.py:58
  208.5 9.9 %copy-start.15 = (f32[2,64,1152]{2,1,0:T(8,128)}, f32[2,64,1152]{2,1,0:T(8,128)S(1)}, u32[]{:S(2)}) copy-start(f32[2,64,1152]{2,1,0:T(8,128)S(1)} %bitcast_add_fusion.2) | copy-start | bytes 1769476
  208.6 7.8 %collective-permute-start.4 = (bf16[64,1152]{1,0:T(8,128)(2,1)S(1)}, bf16[64,1152]{1,0:T(8,128)(2,1)S(1)}, u32[]{:S(2)}, u32[]{:S(2)}) collective-permute-start(bf16[64,1152]{1,0:T(8,128)(2,1)S(1)} %fusion.40), channel_id=1, source_target_pairs={{0,2},{1,3},{2,0},{3,1},{4,6},{5,7},{6,4},{7,5},{8,10},{9,11},{10,... | collective-permute-start | bytes 442376 | tf_op jit(solution)/shard_map/ppermute | solution.py:58
  213.7 2.7 copy-start.24
  216.4 18.5 %copy-start.2 = (bf16[1024,2048]{1,0:T(8,128)(2,1)S(1)}, bf16[1024,2048]{1,0:T(8,128)(2,1)}, u32[]{:S(2)}) copy-start(bf16[1024,2048]{1,0:T(8,128)(2,1)} %fusion.1) | copy-start | bytes 12582916
  218.4 8.2 %copy-start.18 = (f32[64,1152]{1,0:T(8,128)}, f32[64,1152]{1,0:T(8,128)S(1)}, u32[]{:S(2)}) copy-start(f32[64,1152]{1,0:T(8,128)S(1)} %get-tuple-element.98) | copy-start | bytes 884740
  218.4 16.4 %copy-start.27 = (bf16[72,1024]{1,0:T(8,128)(2,1)S(1)}, bf16[72,1024]{1,0:T(8,128)(2,1)}, u32[]{:S(2)}) copy-start(bf16[72,1024]{1,0:T(8,128)(2,1)} %copy-done.26) | copy-start | bytes 442372
  218.5 17.3 %slice-start.1 = ((s8[8388608]{0:T(1024)(128)(4,1)}), s8[4194304]{0:T(1024)(128)(4,1)S(1)}, s32[]{:S(2)}) async-start(s8[8388608]{0:T(1024)(128)(4,1)} %bitcast.206), calls=%async_computation.14 | async-start | bytes 8388608
  226.2 8.7 %copy-start.5 = (bf16[256,1152]{1,0:T(8,128)(2,1)}, bf16[256,1152]{1,0:T(8,128)(2,1)S(1)}, u32[]{:S(2)}) copy-start(bf16[256,1152]{1,0:T(8,128)(2,1)S(1)} %all_gather.43) | copy-start | bytes 1769476
  239.0 15.2 %collective-permute-start.7 = (bf16[144,1024]{1,0:T(8,128)(2,1)S(1)}, bf16[144,1024]{1,0:T(8,128)(2,1)S(1)}, u32[]{:S(2)}, u32[]{:S(2)}) collective-permute-start(bf16[144,1024]{1,0:T(8,128)(2,1)S(1)} %fusion.18), channel_id=1, source_target_pairs={{0,16},{16,0},{1,17},{17,1},{2,18},{18,2},{3,19},{19,3},{4,20},{20... | collective-permute-start | bytes 884744 | tf_op jit(solution)/shard_map/ppermute | solution.py:72
  266.5 3.8 copy-start.55
  270.2 4.0 copy-start.6
  270.2 4.0 copy-start.30
  270.3 1.8 collective-permute-start.8
  271.9 3.6 copy-start.28
  273.3 6.3 %copy-start.17 = (f32[256,1152]{1,0:T(8,128)S(1)}, f32[256,1152]{1,0:T(8,128)}, u32[]{:S(2)}) copy-start(f32[256,1152]{1,0:T(8,128)} %get-tuple-element.109) | copy-start | bytes 3538948
  273.4 6.2 %collective-permute-start.9 = (bf16[64,1152]{1,0:T(8,128)(2,1)S(1)}, bf16[64,1152]{1,0:T(8,128)(2,1)S(1)}, u32[]{:S(2)}, u32[]{:S(2)}) collective-permute-start(bf16[64,1152]{1,0:T(8,128)(2,1)S(1)} %fusion.42), channel_id=1, source_target_pairs={{0,2},{1,3},{2,0},{3,1},{4,6},{5,7},{6,4},{7,5},{8,10},{9,11},{10,... | collective-permute-start | bytes 442376 | tf_op jit(solution)/shard_map/ppermute | solution.py:58
  275.5 4.4 copy-start.14
  275.5 4.4 copy-start.19
  275.5 4.4 copy-start.42
  275.5 4.4 copy-start.49
  275.5 4.4 copy-start.60
  282.1 4.5 copy-start.11
  282.2 4.5 copy-start.22
  284.0 10.6 %all-to-all-start.4 = ((f32[32,1,864]{2,1,0:T(1,128)}), f32[32,1,864]{2,1,0:T(1,128)S(1)}, u32[]{:S(2)}, u32[]{:S(2)}) async-start(f32[32,1,864]{2,1,0:T(1,128)} %all_to_all.24), calls=%async_computation.4 | async-start | bytes 229376 | tf_op jit(solution)/shard_map/all_to_all | solution.py:283
  286.6 135.1 %all-reduce.4.cloned.1.call-start = ((), (), s32[]{:S(2)}) async-start(), calls=%async_computation.10 | async-start | bytes 1146880
  286.7 8.0 %copy-start.50 = (f32[1152]{0:T(1024)S(1)}, f32[1152]{0:T(1024)}, u32[]{:S(2)}) copy-start(f32[1152]{0:T(1024)} %get-tuple-element.124) | copy-start | bytes 13828
  286.7 8.0 %copy-start.57 = (f32[72]{0:T(128)S(1)}, f32[72]{0:T(128)}, u32[]{:S(2)}) copy-start(f32[72]{0:T(128)} %get-tuple-element.113) | copy-start | bytes 868
  296.1 201.7 %reduce-scatter.7.cloned.1.call-start = ((), (), s32[]{:S(2)}) async-start(), calls=%async_computation.11 | async-start | bytes 2985984
  301.5 3.1 copy-start.4
  301.5 3.1 copy-start.34
  301.5 303.3 %reduce-scatter.9.cloned.1.call-start = ((), (), s32[]{:S(2)}) async-start(), calls=%async_computation.12 | async-start | bytes 5971968
  (21 other events, 29.8 us)
Sparse Core Ops, SparseCore 0:
  11.2 53.6 all-gather.8
  67.0 76.5 all-gather.10
  145.8 52.7 all-gather.12
  296.2 125.3 all-reduce.3
  425.2 72.6 reduce-scatter.6
  501.3 103.4 reduce-scatter.8

commit v2 on v1

--- a/solution.py
+++ b/solution.py
@@ -56,6 +56,10 @@
     keep = lax.dynamic_index_in_dim(kept, high, 0, keepdims=False)
     give = lax.dynamic_index_in_dim(kept, 1 - high, 0, keepdims=False).astype(BF)
     return keep + lax.ppermute(give, "mp", [(m, m ^ 2) for m in range(4)]).astype(F32)
+
+
+def spread(values, axes, count):
+    return lax.all_to_all(jnp.broadcast_to(values[None], (count,) + values.shape), axes, 0, 0)
 
 
 def neighbours(block_kv, blocks):
@@ -117,8 +121,10 @@
         attn_weight.reshape(3, weight_rows, heads_here, HD), (1, 2, 0, 3)
     )
     attn_local = attn_local[:, :, jnp.array([1, 2, 0])].reshape(weight_rows, 3 * columns)
-    attn_full = lax.all_gather(attn_local, DP, axis=0, tiled=True)
-    out_t = lax.all_gather(out_weight.T, DP, axis=0, tiled=True)
+    attn_and_out = lax.all_gather(
+        jnp.concatenate([attn_local, out_weight.T], axis=1), DP, axis=0, tiled=True
+    )
+    attn_full, out_t = attn_and_out[:, : 3 * columns], attn_and_out[:, 3 * columns :]
     up_full = lax.all_gather(up_weight, DP, axis=0, tiled=True)
     down_t = lax.all_gather(down_weight.T, DP, axis=0, tiled=True)
 
@@ -127,9 +133,13 @@
     silu_own = lax.dynamic_slice_in_dim(silu_cond, dp_at * weight_rows, weight_rows, 1)
     mod_part = dot(silu_own, mod_weight, 1, 0)
     mod_part = mod_part + jnp.where(dp_at == 0, 1.0, 0.0) * mod_bias
-    mod_parts = lax.all_gather(mod_part, ALL, axis=0, tiled=False)
-    modulation = jnp.sum(mod_parts.reshape(n_dp, group, latents, mod_cols), axis=0)
-    modulation = jnp.transpose(modulation, (1, 0, 2)).reshape(latents, 6 * width)
+    piece_cols = mod_cols // n_dp
+    mod_pieces = jnp.transpose(mod_part.reshape(latents, n_dp, piece_cols), (1, 0, 2))
+    mod_piece = jnp.sum(
+        lax.all_to_all(mod_pieces.reshape(n_dp, latents * piece_cols), DP, 0, 0), axis=0
+    )
+    modulation = spread(mod_piece, ALL, n_dp * group).reshape(n_dp, group, latents, piece_cols)
+    modulation = jnp.transpose(modulation, (2, 1, 0, 3)).reshape(latents, 6 * width)
     one_hot = (segments[:, None] == jnp.arange(latents, dtype=jnp.int32)[None, :]).astype(F32)
     one_hot_s = own_rows(one_hot)
 
@@ -220,8 +230,7 @@
         DP,
         scatter_dimension=0,
         tiled=True,
-    ).astype(F32)
-    up_w_out, down_w_out = mlp_w[:, :hidden_cols], mlp_w[:, hidden_cols:].T
+    )
     mlp_out_s = scatter_rows(dot(hidden, down_t, 1, 1)) + down_bias
     result_s = (mid_s + live_s * gate_mlp_s * mlp_out_s).astype(BF)
 
@@ -246,12 +255,11 @@
     grad_kvq_t = to_owners(jnp.concatenate([grad_kv_own, grad_query_t]).astype(BF))
     grad_attn_w = dot(attn_input, grad_kvq_t, 0, 1)
     grad_out_w = dot(grad_attn_b, attended_t, 0, 1)
-    attn_w = lax.psum_scatter(
-        jnp.concatenate([grad_attn_w.astype(BF), grad_out_w.astype(BF)], axis=1),
-        DP,
-        scatter_dimension=0,
-        tiled=True,
-    ).astype(F32)
+    late_terms, mlp_w = lax.optimization_barrier(
+        (jnp.concatenate([grad_attn_w.astype(BF), grad_out_w.astype(BF)], axis=1), mlp_w)
+    )
+    up_w_out, down_w_out = mlp_w[:, :hidden_cols].astype(F32), mlp_w[:, hidden_cols:].T.astype(F32)
+    attn_w = lax.psum_scatter(late_terms, DP, scatter_dimension=0, tiled=True).astype(F32)
     out_w_out = attn_w[:, 3 * columns :].T
     attn_w_out = attn_w[:, : 3 * columns].reshape(weight_rows, heads_here, 3, HD)
     attn_w_out = jnp.transpose(attn_w_out[:, :, jnp.array([2, 0, 1])], (2, 0, 1, 3)).reshape(
@@ -276,7 +284,6 @@
         axis=1,
     )
     grad_mod_share = jnp.dot(one_hot_s.T, grad_mod_rows, precision=lax.Precision.HIGHEST)
-    piece_cols = mod_cols // n_dp
     pieces = jnp.transpose(
         grad_mod_share.reshape(latents, group, n_dp, piece_cols), (2, 1, 0, 3)
     ).reshape(n_dp * group, latents * piece_cols)
@@ -290,7 +297,7 @@
             jnp.sum(grad_attn_s, axis=0),
         ]
     )
-    small_all = lax.all_gather(small, ALL, axis=0, tiled=False).reshape(n_dp, group, -1)
+    small_all = spread(small, ALL, n_dp * group).reshape(n_dp, group, -1)
     small_own = lax.dynamic_index_in_dim(small_all, member, 1, keepdims=False)
     at = own_piece.shape[0]
     own_cols = jnp.transpose(
@@ -306,7 +313,7 @@
     mod_w_out = jnp.dot(silu_own.astype(F32).T, own_cols, precision=lax.Precision.HIGHEST)
     mod_b_out = jnp.sum(own_cols, axis=0)
     silu_part = jnp.dot(own_cols, mod_weight.astype(F32).T, precision=lax.Precision.HIGHEST)
-    silu_parts = lax.all_gather(silu_part, ALL, axis=0, tiled=False)
+    silu_parts = spread(silu_part.reshape(-1), ALL, n_dp * group)
     silu_parts = jnp.sum(silu_parts.reshape(n_dp, group, latents, weight_rows), axis=1)
     grad_silu = jnp.transpose(silu_parts, (1, 0, 2)).reshape(latents, width)
     grad_conditioning = grad_silu * silu_slope(cond_vals)

time: 628 us -> 435 us (0.69)
  blocking collectives: 167 us -> 39 us
  waiting for transfers between devices: 297 us -> 214 us
  starting transfers between devices: 16.2 us -> 37.6 us
    unnamed x9 -> x7, waiting for transfers between devices: 233 us -> 35.5 us
    all_gather x3 -> x0, blocking collectives: 134 us -> none  [the longest x1 48.1 us: shards(): mod_parts = lax.all_gather(mod_part, ALL, axis=0, tiled=False)]
    all_gather x1, waiting for transfers between devices: 0.01 us -> 27.7 us  [shards(): lax.all_gather(jnp.concatenate([attn_local, out_weight.T], axis=1), DP, a...]
    all_gather x1, waiting for transfers between devices: 9.73 us -> 36.3 us  [shards(): down_t = lax.all_gather(down_weight.T, DP, axis=0, tiled=True)]
    all_to_all x1 -> x4, waiting for transfers between devices: 14.3 us -> 39.3 us  [the longest x3 34 us: spread(): lax.all_to_all(jnp.broadcast_to(values[None], (count,) + values.shape), a...]
    ppermute x1, waiting for transfers between devices: 0.01 us -> 21.9 us  [neighbours(): return [lax.ppermute(block_kv, 'da', [(0, 1), (1, 0)])]]
    all_to_all x1 -> x4, starting transfers between devices: 3.47 us -> 17.4 us  [the longest x3 10.1 us: spread(): lax.all_to_all(jnp.broadcast_to(values[None], (count,) + values.shape), a...]
    unnamed x143 -> x134, local copies, waits for them, and re-layouts: 24.3 us -> 29.5 us
  transfers between devices with their start and end apart: 19 -> 22, of which waited for: 13 -> 18; matrix products, arithmetic and copies ran while one was open for 13% -> 21% of each run, Pallas kernels for 0% -> 0%
where the time goes in v2:
time: 435 us; the launch traced here: 430 us
  waiting for transfers between devices  214 us (49%)
  local copies, waits for them, and re-layouts  49.4 us (11%)
  matrix products  41.3 us (9%)
  blocking collectives  39 us (9%)
  starting transfers between devices  37.6 us (9%)
  other arithmetic  31.9 us (7%)
  between operations  16.3 us (4%)
    all_gather x1, waiting for transfers between devices, shards(): down_t = lax.all_gather(down_weight.T, DP, axis=0, tiled=True)  36.3 us
    unnamed x7, waiting for transfers between devices  35.5 us
    all_to_all x3, waiting for transfers between devices, spread(): lax.all_to_all(jnp.broadcast_to(values[None], (count,) + values.shape), a...  34 us
    dot_general x19, matrix products, dot(): lax.dot_general(left, right, (((left_dim,), (right_dim,)), ((), ())), pre...  33.5 us
    unnamed x134, local copies, waits for them, and re-layouts  29.5 us
    all_gather x1, waiting for transfers between devices, shards(): lax.all_gather(jnp.concatenate([attn_local, out_weight.T], axis=1), DP, a...  27.7 us
    ppermute x1, waiting for transfers between devices, neighbours(): return [lax.ppermute(block_kv, 'da', [(0, 1), (1, 0)])]  21.9 us
    ppermute x1, waiting for transfers between devices, return_grads(): return lax.ppermute(pieces[0], 'da', [(0, 1), (1, 0)]).astype(F32)  17.3 us
  transfers between devices with their start and end apart: 22, of which 18 were waited for; matrix products, arithmetic and copies ran while one was open for 21% of the time, Pallas kernels for 0%

profile of v2, /device:TPU:0, one launch (start us, length us, event | category | flops | bytes accessed | tf_op | source)
XLA Modules:
  0.0 429.7 jit_solution(16896568040625093436)
XLA Ops:
  8.3 1.3 reshape.255
  14.3 7.3 %all-to-all-start = ((f32[8,1,864]{2,1,0:T(1,128)}), f32[8,1,864]{2,1,0:T(1,128)S(1)}, u32[]{:S(2)}, u32[]{:S(2)}) async-start(f32[8,1,864]{2,1,0:T(1,128)} %all_to_all.47), calls=%async_computation | async-start | bytes 57344 | tf_op jit(solution)/shard_map/all_to_all | solution.py:139
  23.1 5.3 %all-to-all-done = f32[8,1,864]{2,1,0:T(1,128)S(1)} async-done(((f32[8,1,864]{2,1,0:T(1,128)}), f32[8,1,864]{2,1,0:T(1,128)S(1)}, u32[]{:S(2)}, u32[]{:S(2)}) %all-to-all-start) | async-done | bytes 27680 | tf_op jit(solution)/shard_map/all_to_all | solution.py:139
  29.2 2.6 all-to-all-start.1
  31.8 9.3 %all-to-all-done.1 = f32[32,1,864]{2,1,0:T(1,128)S(1)} async-done(((f32[32,1,864]{2,1,0:T(1,128)}), f32[32,1,864]{2,1,0:T(1,128)S(1)}, u32[]{:S(2)}, u32[]{:S(2)}) %all-to-all-start.1) | async-done | bytes 110624 | tf_op jit(solution)/shard_map/all_to_all | solution.py:62
  43.0 1.4 subtract_multiply_fusion
  44.4 27.7 %all-gather.4.cloned.1.call-done = bf16[1152,1152]{1,0:T(8,128)(2,1)} async-done(((bf16[144,1152]{1,0:T(8,128)(2,1)}), bf16[1152,1152]{1,0:T(8,128)(2,1)}) %all-gather.4.cloned.1.call-update) | async-done | bytes 2654224 | tf_op jit(solution)/shard_map/all_gather | solution.py:124
  72.0 2.4 fusion.10
  74.5 9.7 %all_to_all.58 = bf16[4,224,256]{2,1,0:T(8,128)(2,1)S(1)} all-to-all(bf16[4,224,256]{2,1,0:T(8,128)(2,1)S(1)} %pad_maximum_fusion.4), channel_id=1, replica_groups=mesh['da'=2,'db'=4,'mp'=4] {'db'}, dimensions={0} | all-to-all | bytes 917504 | tf_op jit(solution)/shard_map/all_to_all | solution.py:173
  84.3 2.4 collective-permute-start
  86.7 21.9 %collective-permute-done = bf16[4,152,256]{2,1,0:T(8,128)(2,1)S(1)} collective-permute-done((bf16[4,152,256]{2,1,0:T(8,128)(2,1)S(1)}, bf16[4,152,256]{2,1,0:T(8,128)(2,1)S(1)}, u32[]{:S(2)}, u32[]{:S(2)}) %collective-permute-start) | collective-permute-done | bytes 311328 | tf_op jit(solution)/shard_map/ppermute | solution.py:67
  110.2 1.7 fusion.85
  112.0 1.3 exponential_reduce_fusion
  113.3 2.0 copy-done.1
  115.2 1.5 fusion.1
  116.8 1.4 convolution_convert_fusion.4
  120.1 3.3 all-to-all-start.3
  123.6 5.7 %all-to-all-done.3 = bf16[4,72,256]{2,1,0:T(8,128)(2,1)S(1)} async-done(((bf16[4,72,256]{2,1,0:T(8,128)(2,1)}), bf16[4,72,256]{2,1,0:T(8,128)(2,1)S(1)}, u32[]{:S(2)}, u32[]{:S(2)}) %all-to-all-start.3) | async-done | bytes 147488 | tf_op jit(solution)/shard_map/all_to_all | solution.py:202
  129.9 1.8 fusion.21
  134.2 1.7 convolution_multiply_fusion
  137.0 1.5 collective-permute-start.2
  139.3 4.0 collective-permute-done.2
  143.3 1.2 fusion.81
  144.9 7.7 %all_gather.16 = bf16[256,1152]{1,0:T(8,128)(2,1)S(1)} all-gather(bf16[64,1152]{1,0:T(8,128)(2,1)S(1)} %fusion.33), channel_id=1, replica_groups=mesh['da'=2,'db'=4,'mp'=4] {'mp'}, dimensions={0}, use_global_device_ids=true | all-gather | bytes 737280 | tf_op jit(solution)/shard_map/all_gather | solution.py:209
  153.5 2.9 convolution_add_fusion
  157.4 1.2 convolution_convert_fusion
  158.6 36.3 %all-gather.8.cloned.1.call-done = bf16[1152,1152]{1,0:T(8,128)(2,1)} async-done(((bf16[144,1152]{1,0:T(8,128)(2,1)}), bf16[1152,1152]{1,0:T(8,128)(2,1)}) %all-gather.8.cloned.1.call-update) | async-done | bytes 2654224 | tf_op jit(solution)/shard_map/all_gather | solution.py:129
  194.9 4.5 %fusion.86 = (f32[1152]{0:T(1024)}, bf16[256,1152]{1,0:T(8,128)(2,1)S(1)}) fusion(f32[256,1152]{1,0:T(8,128)} %copy-done.35, bf16[1152,1152]{1,0:T(8,128)(2,1)} %all-gather.8.cloned.1.call-done, f32[256,1152]{1,0:T(8,128)} %convolution_multiply_fusion), kind=kOutput, calls=%fused_computation.190 | convolution fusion | flops 685964160 | bytes 5607936 | tf_op jit(solution)/shard_map/dot_general | solution.py:43
  204.0 2.7 pad_maximum_fusion
  206.7 8.5 %copy.279 = bf16[1152,2304]{1,0:T(8,128)(2,1)} copy(bf16[1152,2304]{0,1:T(8,128)(2,1)} %pad_maximum_fusion) | data formatting | bytes 10616832
  215.2 1.2 copy-done.36
  216.5 3.0 fusion.74
  221.4 1.5 collective-permute-start.6
  223.6 4.5 %collective-permute-done.6 = bf16[64,1152]{1,0:T(8,128)(2,1)S(1)} collective-permute-done((bf16[64,1152]{1,0:T(8,128)(2,1)S(1)}, bf16[64,1152]{1,0:T(8,128)(2,1)S(1)}, u32[]{:S(2)}, u32[]{:S(2)}) %collective-permute-start.6) | collective-permute-done | bytes 147488 | tf_op jit(solution)/shard_map/ppermute | solution.py:58
  228.4 2.0 collective-permute-done.4
  230.4 2.0 fusion.60
  232.5 7.6 %all_gather.19 = bf16[256,1152]{1,0:T(8,128)(2,1)S(1)} all-gather(bf16[64,1152]{1,0:T(8,128)(2,1)S(1)} %fusion.61), channel_id=1, replica_groups=mesh['da'=2,'db'=4,'mp'=4] {'mp'}, dimensions={0}, use_global_device_ids=true | all-gather | bytes 737280 | tf_op jit(solution)/shard_map/all_gather | solution.py:225
  240.1 2.0 convolution_convert_fusion.5
  242.1 14.0 %all_to_all.59 = bf16[4,72,256]{2,1,0:T(8,128)(2,1)S(1)} all-to-all(bf16[4,72,256]{2,1,0:T(8,128)(2,1)S(1)} %bitcast.243), channel_id=1, replica_groups=mesh['da'=2,'db'=4,'mp'=4] {'db'}, dimensions={0} | all-to-all | bytes 294912 | tf_op jit(solution)/shard_map/all_to_all | solution.py:238
  257.2 2.2 multiply_convert_fusion
  261.3 2.0 fusion.83
  263.3 17.3 %collective-permute-done.7 = bf16[144,1024]{1,0:T(8,128)(2,1)S(1)} collective-permute-done((bf16[144,1024]{1,0:T(8,128)(2,1)S(1)}, bf16[144,1024]{1,0:T(8,128)(2,1)S(1)}, u32[]{:S(2)}, u32[]{:S(2)}) %collective-permute-start.7) | collective-permute-done | bytes 294944 | tf_op jit(solution)/shard_map/ppermute | solution.py:76
  282.3 3.5 all-to-all-start.5
  287.6 6.6 %all-to-all-done.5 = bf16[4,216,256]{2,1,0:T(8,128)(2,1)S(1)} async-done(((bf16[4,216,256]{2,1,0:T(8,128)(2,1)}), bf16[4,216,256]{2,1,0:T(8,128)(2,1)S(1)}, u32[]{:S(2)}, u32[]{:S(2)}) %all-to-all-start.5) | async-done | bytes 442400 | tf_op jit(solution)/shard_map/all_to_all | solution.py:202
  294.5 2.6 fusion.2
  298.9 2.1 collective-permute-start.9
  301.2 3.9 collective-permute-done.9
  305.9 1.9 fusion.75
  308.8 21.4 %reduce-scatter.7.cloned.1.call-done = bf16[144,2304]{1,0:T(8,128)(2,1)} async-done(((bf16[1152,2304]{1,0:T(8,128)(2,1)}), bf16[144,2304]{1,0:T(8,128)(2,1)}) %reduce-scatter.7.cloned.1.call-update) | async-done | bytes 663568
  330.2 2.3 copy.280
  332.5 3.3 copy.281
  338.5 1.8 multiply_dynamic-update-slice_fusion
  340.3 2.2 fusion.62
  343.6 4.3 all-to-all-start.6
  349.1 8.6 %all-to-all-done.6 = f32[32,1,864]{2,1,0:T(1,128)S(1)} async-done(((f32[32,1,864]{2,1,0:T(1,128)}), f32[32,1,864]{2,1,0:T(1,128)S(1)}, u32[]{:S(2)}, u32[]{:S(2)}) %all-to-all-start.6) | async-done | bytes 110624 | tf_op jit(solution)/shard_map/all_to_all | solution.py:290
  358.9 3.1 all-to-all-start.7
  362.0 21.7 %all-to-all-done.7 = f32[32,1,4464]{2,1,0:T(1,128)S(1)} async-done(((f32[32,1,4464]{2,1,0:T(1,128)}), f32[32,1,4464]{2,1,0:T(1,128)S(1)}, u32[]{:S(2)}, u32[]{:S(2)}) %all-to-all-start.7) | async-done | bytes 571424 | tf_op jit(solution)/shard_map/all_to_all | solution.py:62
  383.8 1.4 reduce.6
  387.0 4.4 %all-to-all-start.8 = ((f32[32,1,576]{2,1,0:T(1,128)}), f32[32,1,576]{2,1,0:T(1,128)S(1)}, u32[]{:S(2)}, u32[]{:S(2)}) async-start(f32[32,1,576]{2,1,0:T(1,128)} %broadcast_in_dim.29), calls=%async_computation.8 | async-start | bytes 163840 | tf_op jit(solution)/shard_map/all_to_all | solution.py:62
  392.3 1.6 fusion.89
  396.1 2.9 all-to-all-done.8
  401.3 2.6 copy.275
  405.1 13.4 %reduce-scatter.9.cloned.1.call-done = bf16[144,1152]{1,0:T(8,128)(2,1)} async-done(((bf16[1152,1152]{1,0:T(8,128)(2,1)}), bf16[144,1152]{1,0:T(8,128)(2,1)}) %reduce-scatter.9.cloned.1.call-update) | async-done | bytes 331792
  418.5 1.2 copy.282
  (290 shorter events, 55.1 us)
Async XLA Ops:
  7.2 6.1 %copy-start = (bf16[144,1728]{1,0:T(8,128)(2,1)S(1)}, bf16[144,1728]{1,0:T(8,128)(2,1)}, u32[]{:S(2)}) copy-start(bf16[144,1728]{1,0:T(8,128)(2,1)} %param.29) | copy-start | bytes 1492996
  7.2 2.5 copy-start.55
  7.2 2.5 copy-start.56
  7.2 64.8 %all-gather.4.cloned.1.call-start = ((), (), s32[]{:S(2)}) async-start(), calls=%async_computation.11 | async-start | bytes 2985984 | tf_op jit(solution)/shard_map/all_gather | solution.py:124
  11.3 10.9 %copy-start.48 = (s32[256]{0:T(256)S(1)}, s32[256]{0:T(256)}, u32[]{:S(2)}) copy-start(s32[256]{0:T(256)} %param.19) | copy-start | bytes 3076
  11.3 11.0 %copy-start.53 = (f32[2,288]{1,0:T(2,128)S(1)}, f32[2,288]{1,0:T(2,128)}, u32[]{:S(2)}) copy-start(f32[2,288]{1,0:T(2,128)} %param.22) | copy-start | bytes 6916
  11.3 11.1 %copy-start.6 = (bf16[256,1152]{1,0:T(8,128)(2,1)S(1)}, bf16[256,1152]{1,0:T(8,128)(2,1)}, u32[]{:S(2)}) copy-start(bf16[256,1152]{1,0:T(8,128)(2,1)} %param.17) | copy-start | bytes 1769476
  12.3 140.3 %all-gather.6.cloned.1.call-start = ((), (), s32[]{:S(2)}) async-start(), calls=%async_computation.12 | async-start | bytes 2985984 | tf_op jit(solution)/shard_map/all_gather | solution.py:128
  14.3 14.2 %all-to-all-start = ((f32[8,1,864]{2,1,0:T(1,128)}), f32[8,1,864]{2,1,0:T(1,128)S(1)}, u32[]{:S(2)}, u32[]{:S(2)}) async-start(f32[8,1,864]{2,1,0:T(1,128)} %all_to_all.47), calls=%async_computation | async-start | bytes 57344 | tf_op jit(solution)/shard_map/all_to_all | solution.py:139
  29.2 12.0 %all-to-all-start.1 = ((f32[32,1,864]{2,1,0:T(1,128)}), f32[32,1,864]{2,1,0:T(1,128)S(1)}, u32[]{:S(2)}, u32[]{:S(2)}) async-start(f32[32,1,864]{2,1,0:T(1,128)} %broadcast_in_dim.21), calls=%async_computation.1 | async-start | bytes 229376 | tf_op jit(solution)/shard_map/all_to_all | solution.py:62
  31.8 163.2 %all-gather.8.cloned.1.call-start = ((), (), s32[]{:S(2)}) async-start(), calls=%async_computation.13 | async-start | bytes 2985984 | tf_op jit(solution)/shard_map/all_gather | solution.py:129
  31.8 11.2 %copy-start.51 = (f32[256]{0:T(256)}, f32[256]{0:T(256)S(1)}, u32[]{:S(2)}) copy-start(f32[256]{0:T(256)S(1)} %add_rsqrt_fusion) | copy-start | bytes 3076
  44.4 30.1 %copy-start.24 = (bf16[256,1152]{1,0:T(8,128)(2,1)}, bf16[256,1152]{1,0:T(8,128)(2,1)S(1)}, u32[]{:S(2)}) copy-start(bf16[256,1152]{1,0:T(8,128)(2,1)S(1)} %get-tuple-element.155) | copy-start | bytes 1769476
  84.3 24.4 %collective-permute-start = (bf16[4,152,256]{2,1,0:T(8,128)(2,1)S(1)}, bf16[4,152,256]{2,1,0:T(8,128)(2,1)S(1)}, u32[]{:S(2)}, u32[]{:S(2)}) collective-permute-start(bf16[4,152,256]{2,1,0:T(8,128)(2,1)S(1)} %get-tuple-element.157), channel_id=1, source_target_pairs={{0,16},{16,0},{1,17},{17,1},{2,18},{18,2},{3,19},{19,3},{4,20},{20... | collective-permute-start | bytes 933896 | tf_op jit(solution)/shard_map/ppermute | solution.py:67
  86.7 23.5 %copy-start.41 = (bf16[4,9,8,256]{3,2,0,1:T(8,128)(2,1)}, bf16[4,9,8,256]{3,2,0,1:T(8,128)(2,1)S(1)}, u32[]{:S(2)}) copy-start(bf16[4,9,8,256]{3,2,0,1:T(8,128)(2,1)S(1)} %copy.295) | copy-start | bytes 442372
  110.2 6.6 %copy-start.17 = (bf16[72,2048]{1,0:T(8,128)(2,1)}, bf16[72,2048]{1,0:T(8,128)(2,1)S(1)}, u32[]{:S(2)}) copy-start(bf16[72,2048]{1,0:T(8,128)(2,1)S(1)} %slice.103) | copy-start | bytes 884740
  112.0 3.3 copy-start.1
  120.1 9.2 %all-to-all-start.3 = ((bf16[4,72,256]{2,1,0:T(8,128)(2,1)}), bf16[4,72,256]{2,1,0:T(8,128)(2,1)S(1)}, u32[]{:S(2)}, u32[]{:S(2)}) async-start(bf16[4,72,256]{2,1,0:T(8,128)(2,1)} %bitcast.197), calls=%async_computation.3 | async-start | bytes 294912 | tf_op jit(solution)/shard_map/all_to_all | solution.py:202
  123.4 206.7 %reduce-scatter.7.cloned.1.call-start = ((), (), s32[]{:S(2)}) async-start(), calls=%async_computation.14 | async-start | bytes 5971968
  131.8 4.2 collective-permute-start.1
  135.9 7.4 %copy-start.46 = (f32[1152]{0:T(1024)S(1)}, f32[1152]{0:T(1024)}, u32[]{:S(2)}) copy-start(f32[1152]{0:T(1024)} %param.24) | copy-start | bytes 13828
  137.0 7.6 %copy-start.13 = (f32[2,64,1152]{2,1,0:T(8,128)}, f32[2,64,1152]{2,1,0:T(8,128)S(1)}, u32[]{:S(2)}) copy-start(f32[2,64,1152]{2,1,0:T(8,128)S(1)} %bitcast_add_fusion.3) | copy-start | bytes 1769476
  137.0 6.3 %collective-permute-start.2 = (bf16[64,1152]{1,0:T(8,128)(2,1)S(1)}, bf16[64,1152]{1,0:T(8,128)(2,1)S(1)}, u32[]{:S(2)}, u32[]{:S(2)}) collective-permute-start(bf16[64,1152]{1,0:T(8,128)(2,1)S(1)} %fusion.48), channel_id=1, source_target_pairs={{0,2},{1,3},{2,0},{3,1},{4,6},{5,7},{6,4},{7,5},{8,10},{9,11},{10,... | collective-permute-start | bytes 442376 | tf_op jit(solution)/shard_map/ppermute | solution.py:58
  139.3 5.5 %copy-start.4 = (f32[64,5760]{1,0:T(8,128)}, f32[64,5760]{1,0:T(8,128)S(1)}, u32[]{:S(2)}) copy-start(f32[64,5760]{1,0:T(8,128)S(1)} %fusion.52) | copy-start | bytes 4423684
  139.3 14.2 %copy-start.59 = (f32[1152]{0:T(1024)S(1)}, f32[1152]{0:T(1024)}, u32[]{:S(2)}) copy-start(f32[1152]{0:T(1024)} %param.26) | copy-start | bytes 13828
  153.5 3.9 copy-start.7
  194.9 4.5 %copy-start.10 = (bf16[256,1152]{1,0:T(8,128)(2,1)S(1)}, bf16[256,1152]{1,0:T(8,128)(2,1)}, u32[]{:S(2)}) copy-start(bf16[256,1152]{1,0:T(8,128)(2,1)} %copy-done.9) | copy-start | bytes 1769476
  203.9 16.2 %collective-permute-start.5 = (bf16[2,64,1152]{2,1,0:T(8,128)(2,1)}, bf16[2,64,1152]{2,1,0:T(8,128)(2,1)}, u32[]{:S(2)}, u32[]{:S(2)}) collective-permute-start(bf16[2,64,1152]{2,1,0:T(8,128)(2,1)} %fusion.29), channel_id=1, source_target_pairs={{0,1},{1,0},{2,3},{3,2},{4,5},{5,4},{6,7},{7,6},{8,9},{9,8},{10,11... | collective-permute-start | bytes 884744 | tf_op jit(solution)/shard_map/ppermute | solution.py:55
  216.5 3.6 copy-start.38
  219.5 8.6 %copy-start.5 = (f32[64,5760]{1,0:T(8,128)S(1)}, f32[64,5760]{1,0:T(8,128)}, u32[]{:S(2)}) copy-start(f32[64,5760]{1,0:T(8,128)} %copy-done.4) | copy-start | bytes 4423684
  219.5 3.3 collective-permute-start.3
  220.1 10.3 %copy-start.47 = (f32[1152]{0:T(1024)S(1)}, f32[1152]{0:T(1024)}, u32[]{:S(2)}) copy-start(f32[1152]{0:T(1024)} %param.28) | copy-start | bytes 13828
  220.1 37.0 %slice-start = ((s8[8388608]{0:T(1024)(128)(4,1)}), s8[4194304]{0:T(1024)(128)(4,1)S(1)}, s32[]{:S(2)}) async-start(s8[8388608]{0:T(1024)(128)(4,1)} %bitcast.204), calls=%async_computation.16 | async-start | bytes 8388608
  221.3 7.0 %copy-start.11 = (f32[2,64,1152]{2,1,0:T(8,128)}, f32[2,64,1152]{2,1,0:T(8,128)S(1)}, u32[]{:S(2)}) copy-start(f32[2,64,1152]{2,1,0:T(8,128)S(1)} %bitcast_add_fusion.1) | copy-start | bytes 1769476
  221.4 6.8 %collective-permute-start.6 = (bf16[64,1152]{1,0:T(8,128)(2,1)S(1)}, bf16[64,1152]{1,0:T(8,128)(2,1)S(1)}, u32[]{:S(2)}, u32[]{:S(2)}) collective-permute-start(bf16[64,1152]{1,0:T(8,128)(2,1)S(1)} %fusion.50), channel_id=1, source_target_pairs={{0,2},{1,3},{2,0},{3,1},{4,6},{5,7},{6,4},{7,5},{8,10},{9,11},{10,... | collective-permute-start | bytes 442376 | tf_op jit(solution)/shard_map/ppermute | solution.py:58
  222.9 9.4 %copy-start.15 = (f32[2,64,1152]{2,1,0:T(8,128)}, f32[2,64,1152]{2,1,0:T(8,128)S(1)}, u32[]{:S(2)}) copy-start(f32[2,64,1152]{2,1,0:T(8,128)S(1)} %bitcast_add_fusion.2) | copy-start | bytes 1769476
  223.0 7.4 %collective-permute-start.4 = (bf16[64,1152]{1,0:T(8,128)(2,1)S(1)}, bf16[64,1152]{1,0:T(8,128)(2,1)S(1)}, u32[]{:S(2)}, u32[]{:S(2)}) collective-permute-start(bf16[64,1152]{1,0:T(8,128)(2,1)S(1)} %fusion.49), channel_id=1, source_target_pairs={{0,2},{1,3},{2,0},{3,1},{4,6},{5,7},{6,4},{7,5},{8,10},{9,11},{10,... | collective-permute-start | bytes 442376 | tf_op jit(solution)/shard_map/ppermute | solution.py:58
  230.4 25.8 %copy-start.29 = (bf16[72,1024]{1,0:T(8,128)(2,1)S(1)}, bf16[72,1024]{1,0:T(8,128)(2,1)}, u32[]{:S(2)}) copy-start(bf16[72,1024]{1,0:T(8,128)(2,1)} %copy-done.28) | copy-start | bytes 442372
  232.3 9.8 %copy-start.20 = (f32[64,1152]{1,0:T(8,128)}, f32[64,1152]{1,0:T(8,128)S(1)}, u32[]{:S(2)}) copy-start(f32[64,1152]{1,0:T(8,128)S(1)} %get-tuple-element.141) | copy-start | bytes 884740
  232.3 23.9 %copy-start.3 = (bf16[1024,2048]{1,0:T(8,128)(2,1)S(1)}, bf16[1024,2048]{1,0:T(8,128)(2,1)}, u32[]{:S(2)}) copy-start(bf16[1024,2048]{1,0:T(8,128)(2,1)} %copy-done.2) | copy-start | bytes 12582916
  232.4 24.7 %slice-start.1 = ((s8[8388608]{0:T(1024)(128)(4,1)}), s8[4194304]{0:T(1024)(128)(4,1)S(1)}, s32[]{:S(2)}) async-start(s8[8388608]{0:T(1024)(128)(4,1)} %bitcast.204), calls=%async_computation.17 | async-start | bytes 8388608
  260.3 20.2 %collective-permute-start.7 = (bf16[144,1024]{1,0:T(8,128)(2,1)S(1)}, bf16[144,1024]{1,0:T(8,128)(2,1)S(1)}, u32[]{:S(2)}, u32[]{:S(2)}) collective-permute-start(bf16[144,1024]{1,0:T(8,128)(2,1)S(1)} %fusion.27), channel_id=1, source_target_pairs={{0,16},{16,0},{1,17},{17,1},{2,18},{18,2},{3,19},{19,3},{4,20},{20... | collective-permute-start | bytes 884744 | tf_op jit(solution)/shard_map/ppermute | solution.py:76
  281.5 4.4 %copy-start.52 = (f32[256]{0:T(256)S(1)}, f32[256]{0:T(256)}, u32[]{:S(2)}) copy-start(f32[256]{0:T(256)} %copy-done.51) | copy-start | bytes 3076
  281.5 5.0 %copy-start.32 = (bf16[4,72,256]{2,1,0:T(8,128)(2,1)S(1)}, bf16[4,72,256]{2,1,0:T(8,128)(2,1)}, u32[]{:S(2)}) copy-start(bf16[4,72,256]{2,1,0:T(8,128)(2,1)} %copy-done.31) | copy-start | bytes 442372
  282.3 12.0 %all-to-all-start.5 = ((bf16[4,216,256]{2,1,0:T(8,128)(2,1)}), bf16[4,216,256]{2,1,0:T(8,128)(2,1)S(1)}, u32[]{:S(2)}, u32[]{:S(2)}) async-start(bf16[4,216,256]{2,1,0:T(8,128)(2,1)} %maximum_bitcast_fusion.1), calls=%async_computation.5 | async-start | bytes 884736 | tf_op jit(solution)/shard_map/all_to_all | solution.py:202
  285.8 132.7 %reduce-scatter.9.cloned.1.call-start = ((), (), s32[]{:S(2)}) async-start(), calls=%async_computation.15 | async-start | bytes 2985984
  294.5 2.7 copy-start.25
  297.2 1.6 collective-permute-start.8
  298.0 3.0 copy-start.22
  298.9 7.0 %copy-start.19 = (f32[256,1152]{1,0:T(8,128)S(1)}, f32[256,1152]{1,0:T(8,128)}, u32[]{:S(2)}) copy-start(f32[256,1152]{1,0:T(8,128)} %get-tuple-element.154) | copy-start | bytes 3538948
  298.9 6.2 %collective-permute-start.9 = (bf16[64,1152]{1,0:T(8,128)(2,1)S(1)}, bf16[64,1152]{1,0:T(8,128)(2,1)S(1)}, u32[]{:S(2)}, u32[]{:S(2)}) collective-permute-start(bf16[64,1152]{1,0:T(8,128)(2,1)S(1)} %fusion.51), channel_id=1, source_target_pairs={{0,2},{1,3},{2,0},{3,1},{4,6},{5,7},{6,4},{7,5},{8,10},{9,11},{10,... | collective-permute-start | bytes 442376 | tf_op jit(solution)/shard_map/ppermute | solution.py:58
  301.2 6.6 %copy-start.14 = (f32[2,64,1152]{2,1,0:T(8,128)S(1)}, f32[2,64,1152]{2,1,0:T(8,128)}, u32[]{:S(2)}) copy-start(f32[2,64,1152]{2,1,0:T(8,128)} %copy-done.13) | copy-start | bytes 1769476
  301.2 6.6 %copy-start.21 = (f32[64,1152]{1,0:T(8,128)S(1)}, f32[64,1152]{1,0:T(8,128)}, u32[]{:S(2)}) copy-start(f32[64,1152]{1,0:T(8,128)} %copy-done.20) | copy-start | bytes 884740
  301.2 6.6 %copy-start.44 = (bf16[64,1152]{1,0:T(8,128)(2,1)S(1)}, bf16[64,1152]{1,0:T(8,128)(2,1)}, u32[]{:S(2)}) copy-start(bf16[64,1152]{1,0:T(8,128)(2,1)} %copy-done.43) | copy-start | bytes 442372
  301.2 6.6 %copy-start.57 = (f32[64]{0:T(128)S(1)}, f32[64]{0:T(128)}, u32[]{:S(2)}) copy-start(f32[64]{0:T(128)} %dynamic-slice.7) | copy-start | bytes 772
  335.8 2.7 copy-start.16
  335.8 2.7 copy-start.40
  340.3 8.7 %copy-start.30 = (f32[144,1024]{1,0:T(8,128)S(1)}, f32[144,1024]{1,0:T(8,128)}, u32[]{:S(2)}) copy-start(f32[144,1024]{1,0:T(8,128)} %get-tuple-element.144) | copy-start | bytes 1769476
  340.3 17.5 %copy-start.49 = (f32[1152]{0:T(1024)S(1)}, f32[1152]{0:T(1024)}, u32[]{:S(2)}) copy-start(f32[1152]{0:T(1024)} %get-tuple-element.169) | copy-start | bytes 13828
  340.3 17.5 %copy-start.54 = (f32[72]{0:T(128)S(1)}, f32[72]{0:T(128)}, u32[]{:S(2)}) copy-start(f32[72]{0:T(128)} %get-tuple-element.158) | copy-start | bytes 868
  343.6 14.0 %all-to-all-start.6 = ((f32[32,1,864]{2,1,0:T(1,128)}), f32[32,1,864]{2,1,0:T(1,128)S(1)}, u32[]{:S(2)}, u32[]{:S(2)}) async-start(f32[32,1,864]{2,1,0:T(1,128)} %all_to_all.48), calls=%async_computation.6 | async-start | bytes 229376 | tf_op jit(solution)/shard_map/all_to_all | solution.py:290
  358.9 24.8 %all-to-all-start.7 = ((f32[32,1,4464]{2,1,0:T(1,128)}), f32[32,1,4464]{2,1,0:T(1,128)S(1)}, u32[]{:S(2)}, u32[]{:S(2)}) async-start(f32[32,1,4464]{2,1,0:T(1,128)} %broadcast_in_dim.27), calls=%async_computation.7 | async-start | bytes 1146880 | tf_op jit(solution)/shard_map/all_to_all | solution.py:62
  385.7 14.5 %copy-start.8 = (bf16[144,2304]{0,1:T(8,128)(2,1)S(1)}, bf16[144,2304]{0,1:T(8,128)(2,1)}, u32[]{:S(2)}) copy-start(bf16[144,2304]{0,1:T(8,128)(2,1)} %copy.280) | copy-start | bytes 1990660
  387.0 12.0 %all-to-all-start.8 = ((f32[32,1,576]{2,1,0:T(1,128)}), f32[32,1,576]{2,1,0:T(1,128)S(1)}, u32[]{:S(2)}, u32[]{:S(2)}) async-start(f32[32,1,576]{2,1,0:T(1,128)} %broadcast_in_dim.29), calls=%async_computation.8 | async-start | bytes 163840 | tf_op jit(solution)/shard_map/all_to_all | solution.py:62
  (20 other events, 28.5 us)
Sparse Core Ops, SparseCore 0:
  12.4 59.5 all-gather.3
  74.2 64.9 all-gather.5
  141.4 53.5 all-gather.7
  215.4 114.7 reduce-scatter.6
  335.9 82.5 reduce-scatter.8

commit v3 on v2

--- a/solution.py
+++ b/solution.py
@@ -125,8 +125,10 @@
         jnp.concatenate([attn_local, out_weight.T], axis=1), DP, axis=0, tiled=True
     )
     attn_full, out_t = attn_and_out[:, : 3 * columns], attn_and_out[:, 3 * columns :]
-    up_full = lax.all_gather(up_weight, DP, axis=0, tiled=True)
-    down_t = lax.all_gather(down_weight.T, DP, axis=0, tiled=True)
+    up_and_down = lax.all_gather(
+        jnp.concatenate([up_weight, down_weight.T], axis=1), DP, axis=0, tiled=True
+    )
+    up_full, down_t = up_and_down[:, :hidden_cols], up_and_down[:, hidden_cols:]
 
     cond_vals = conditioning.astype(F32)
     silu_cond = jax.nn.silu(cond_vals).astype(BF)
@@ -255,13 +257,12 @@
     grad_kvq_t = to_owners(jnp.concatenate([grad_kv_own, grad_query_t]).astype(BF))
     grad_attn_w = dot(attn_input, grad_kvq_t, 0, 1)
     grad_out_w = dot(grad_attn_b, attended_t, 0, 1)
-    late_terms, mlp_w = lax.optimization_barrier(
-        (jnp.concatenate([grad_attn_w.astype(BF), grad_out_w.astype(BF)], axis=1), mlp_w)
-    )
+    attn_terms, mlp_w = lax.optimization_barrier((grad_attn_w.astype(BF), mlp_w))
     up_w_out, down_w_out = mlp_w[:, :hidden_cols].astype(F32), mlp_w[:, hidden_cols:].T.astype(F32)
-    attn_w = lax.psum_scatter(late_terms, DP, scatter_dimension=0, tiled=True).astype(F32)
-    out_w_out = attn_w[:, 3 * columns :].T
-    attn_w_out = attn_w[:, : 3 * columns].reshape(weight_rows, heads_here, 3, HD)
+    pieces = grad_out_w.astype(BF).reshape(n_dp, weight_rows, columns)
+    out_w_out = jnp.sum(lax.all_to_all(pieces, DP, 0, 0).astype(F32), axis=0).T
+    attn_w = lax.psum_scatter(attn_terms, DP, scatter_dimension=0, tiled=True).astype(F32)
+    attn_w_out = attn_w.reshape(weight_rows, heads_here, 3, HD)
     attn_w_out = jnp.transpose(attn_w_out[:, :, jnp.array([2, 0, 1])], (2, 0, 1, 3)).reshape(
         3, weight_rows, columns
     )
@@ -287,29 +288,28 @@
     pieces = jnp.transpose(
         grad_mod_share.reshape(latents, group, n_dp, piece_cols), (2, 1, 0, 3)
     ).reshape(n_dp * group, latents * piece_cols)
-    own_piece = jnp.sum(lax.all_to_all(pieces, ALL, 0, 0), axis=0)
-    small = jnp.concatenate(
-        [
-            own_piece,
-            attn_b_part,
-            jnp.sum(grad_pre, axis=0),
-            jnp.sum(own_rows(grad_mlp), axis=0),
-            jnp.sum(grad_attn_s, axis=0),
-        ]
-    )
+    up_piece = jnp.repeat(jnp.sum(grad_pre, axis=0).reshape(n_dp, -1), group, axis=0)
+    both_part = jnp.concatenate([jnp.sum(own_rows(grad_mlp), axis=0), jnp.sum(grad_attn_s, axis=0)])
+    both_piece = both_part.reshape(n_dp * group, -1)
+    taken = lax.all_to_all(
+        jnp.concatenate([pieces, both_piece, up_piece], axis=1), ALL, 0, 0
+    )
+    at = latents * piece_cols
+    both_at = at + both_piece.shape[1]
+    from_group = taken[:, both_at:].reshape(n_dp, group, -1)
+    up_sum = jnp.sum(lax.dynamic_index_in_dim(from_group, member, 1, keepdims=False), axis=0)
+    small = jnp.concatenate([jnp.sum(taken[:, :both_at], axis=0), up_sum, attn_b_part])
     small_all = spread(small, ALL, n_dp * group).reshape(n_dp, group, -1)
     small_own = lax.dynamic_index_in_dim(small_all, member, 1, keepdims=False)
-    at = own_piece.shape[0]
     own_cols = jnp.transpose(
         small_own[:, :at].reshape(n_dp, latents, piece_cols), (1, 0, 2)
     ).reshape(latents, mod_cols)
-    attn_b_own = small_own[:, at : at + 2 * HD].reshape(blocks, heads_here, 2, HD)
+    both_b = small_all[:, :, at:both_at].reshape(2 * width)
+    down_b_all, out_b_all = both_b[:width], both_b[width:]
+    up_at = both_at + up_sum.shape[0]
+    up_b_out = small_own[:, both_at:up_at].reshape(hidden_cols)
+    attn_b_own = small_own[:, up_at:].reshape(blocks, heads_here, 2, HD)
     attn_b_out = jnp.transpose(jnp.sum(attn_b_own, axis=0), (1, 0, 2)).reshape(2, columns)
-    at = at + 2 * HD
-    up_b_out = jnp.sum(small_own[:, at : at + hidden_cols], axis=0)
-    at = at + hidden_cols
-    both_b = jnp.sum(small_all[:, :, at:], axis=(0, 1))
-    down_b_all, out_b_all = both_b[:width], both_b[width:]
     mod_w_out = jnp.dot(silu_own.astype(F32).T, own_cols, precision=lax.Precision.HIGHEST)
     mod_b_out = jnp.sum(own_cols, axis=0)
     silu_part = jnp.dot(own_cols, mod_weight.astype(F32).T, precision=lax.Precision.HIGHEST)

time: 435 us -> 420 us (0.966)
  waiting for transfers between devices: 214 us -> 187 us
  blocking collectives: 39 us -> 52.7 us
  local copies, waits for them, and re-layouts: 49.4 us -> 56.2 us
  matrix products: 41.3 us -> 36.8 us
    all_gather x2 -> x1, waiting for transfers between devices: 36.3 us -> 5.19 us  [shards(): lax.all_gather(jnp.concatenate([up_weight, down_weight.T], axis=1), DP, a...]
    all_to_all x1 -> x2, waiting for transfers between devices: 8.59 us -> 36.6 us  [the longest x1 36.6 us: shards(): out_w_out = jnp.sum(lax.all_to_all(pieces, DP, 0, 0).astype(F32), axis=0).T]
    unnamed x7 -> x6, waiting for transfers between devices: 35.5 us -> 17.7 us
    all_to_all x3, waiting for transfers between devices: 34 us -> 19.6 us  [spread(): lax.all_to_all(jnp.broadcast_to(values[None], (count,) + values.shape), a...]
    all_to_all x0 -> x1, blocking collectives: none -> 13.4 us  [to_owners(): lax.all_to_all(parts, 'db', 0, 0).reshape(heads_here * rows, tok_rows)]
    ppermute x1, waiting for transfers between devices: 21.9 us -> 29.6 us  [neighbours(): return [lax.ppermute(block_kv, 'da', [(0, 1), (1, 0)])]]
    all_to_all x2 -> x1, waiting for transfers between devices: 12.3 us -> 10.2 us  [to_owners(): lax.all_to_all(parts, 'db', 0, 0).reshape(heads_here * rows, tok_rows)]
    unnamed x134 -> x142, local copies, waits for them, and re-layouts: 29.5 us -> 28.2 us
  transfers between devices with their start and end apart: 22 -> 21, of which waited for: 18 -> 17; matrix products, arithmetic and copies ran while one was open for 21% -> 23% of each run, Pallas kernels for 0% -> 0%
where the time goes in v3:
time: 420 us; the launch traced here: 414 us
  waiting for transfers between devices  187 us (45%)
  local copies, waits for them, and re-layouts  56.2 us (13%)
  blocking collectives  52.7 us (13%)
  matrix products  36.8 us (9%)
  starting transfers between devices  34.5 us (8%)
  other arithmetic  30.7 us (7%)
  between operations  16.2 us (4%)
    all_to_all x1, waiting for transfers between devices, shards(): out_w_out = jnp.sum(lax.all_to_all(pieces, DP, 0, 0).astype(F32), axis=0).T  36.6 us
    dot_general x19, matrix products, dot(): lax.dot_general(left, right, (((left_dim,), (right_dim,)), ((), ())), pre...  30 us
    ppermute x1, waiting for transfers between devices, neighbours(): return [lax.ppermute(block_kv, 'da', [(0, 1), (1, 0)])]  29.6 us
    unnamed x142, local copies, waits for them, and re-layouts  28.2 us
    all_gather x1, waiting for transfers between devices, shards(): lax.all_gather(jnp.concatenate([attn_local, out_weight.T], axis=1), DP, a...  27.7 us
    ppermute x1, waiting for transfers between devices, return_grads(): return lax.ppermute(pieces[0], 'da', [(0, 1), (1, 0)]).astype(F32)  21.6 us
    all_to_all x3, waiting for transfers between devices, spread(): lax.all_to_all(jnp.broadcast_to(values[None], (count,) + values.shape), a...  19.6 us
    unnamed x6, waiting for transfers between devices  17.7 us
  transfers between devices with their start and end apart: 21, of which 17 were waited for; matrix products, arithmetic and copies ran while one was open for 23% of the time, Pallas kernels for 0%

profile of v3, /device:TPU:0, one launch (start us, length us, event | category | flops | bytes accessed | tf_op | source)
XLA Modules:
  0.0 413.8 jit_solution(17859741602025628991)
XLA Ops:
  8.3 1.3 reshape.280
  13.5 7.3 %all-to-all-start = ((f32[8,1,864]{2,1,0:T(1,128)}), f32[8,1,864]{2,1,0:T(1,128)S(1)}, u32[]{:S(2)}, u32[]{:S(2)}) async-start(f32[8,1,864]{2,1,0:T(1,128)} %all_to_all.54), calls=%async_computation | async-start | bytes 57344 | tf_op jit(solution)/shard_map/all_to_all | solution.py:141
  23.4 4.3 %all-to-all-done = f32[8,1,864]{2,1,0:T(1,128)S(1)} async-done(((f32[8,1,864]{2,1,0:T(1,128)}), f32[8,1,864]{2,1,0:T(1,128)S(1)}, u32[]{:S(2)}, u32[]{:S(2)}) %all-to-all-start) | async-done | bytes 27680 | tf_op jit(solution)/shard_map/all_to_all | solution.py:141
  28.4 2.6 all-to-all-start.1
  31.0 9.4 %all-to-all-done.1 = f32[32,1,864]{2,1,0:T(1,128)S(1)} async-done(((f32[32,1,864]{2,1,0:T(1,128)}), f32[32,1,864]{2,1,0:T(1,128)S(1)}, u32[]{:S(2)}, u32[]{:S(2)}) %all-to-all-start.1) | async-done | bytes 110624 | tf_op jit(solution)/shard_map/all_to_all | solution.py:62
  42.9 1.4 subtract_multiply_fusion
  44.2 27.7 %all-gather.3.cloned.1.call-done = bf16[1152,1152]{1,0:T(8,128)(2,1)} async-done(((bf16[144,1152]{1,0:T(8,128)(2,1)}), bf16[1152,1152]{1,0:T(8,128)(2,1)}) %all-gather.3.cloned.1.call-update) | async-done | bytes 2654224 | tf_op jit(solution)/shard_map/all_gather | solution.py:124
  72.0 2.4 fusion.17
  74.5 10.0 %all_to_all.65 = bf16[4,224,256]{2,1,0:T(8,128)(2,1)S(1)} all-to-all(bf16[4,224,256]{2,1,0:T(8,128)(2,1)S(1)} %pad_maximum_fusion.4), channel_id=1, replica_groups=mesh['da'=2,'db'=4,'mp'=4] {'db'}, dimensions={0} | all-to-all | bytes 917504 | tf_op jit(solution)/shard_map/all_to_all | solution.py:175
  84.5 2.5 collective-permute-start
  87.7 29.6 %collective-permute-done = bf16[4,152,256]{2,1,0:T(8,128)(2,1)S(1)} collective-permute-done((bf16[4,152,256]{2,1,0:T(8,128)(2,1)S(1)}, bf16[4,152,256]{2,1,0:T(8,128)(2,1)S(1)}, u32[]{:S(2)}, u32[]{:S(2)}) %collective-permute-start) | collective-permute-done | bytes 311328 | tf_op jit(solution)/shard_map/ppermute | solution.py:67
  118.3 1.3 reshape.283
  120.4 3.6 fusion.90
  124.0 1.3 exponential_reduce_fusion
  125.3 2.2 copy-done.1
  127.4 1.5 fusion.1
  129.0 1.4 convolution_convert_fusion.4
  131.7 3.3 all-to-all-start.3
  135.2 10.2 %all-to-all-done.3 = bf16[4,72,256]{2,1,0:T(8,128)(2,1)S(1)} async-done(((bf16[4,72,256]{2,1,0:T(8,128)(2,1)}), bf16[4,72,256]{2,1,0:T(8,128)(2,1)S(1)}, u32[]{:S(2)}, u32[]{:S(2)}) %all-to-all-start.3) | async-done | bytes 147488 | tf_op jit(solution)/shard_map/all_to_all | solution.py:204
  146.1 1.8 fusion.30
  151.0 1.5 convolution_multiply_fusion
  153.6 1.5 collective-permute-start.2
  155.8 4.1 collective-permute-done.2
  160.0 1.2 fusion.85
  161.6 8.1 %all_gather.13 = bf16[256,1152]{1,0:T(8,128)(2,1)} all-gather(bf16[64,1152]{1,0:T(8,128)(2,1)S(1)} %fusion.42), channel_id=1, replica_groups=mesh['da'=2,'db'=4,'mp'=4] {'mp'}, dimensions={0}, use_global_device_ids=true | all-gather | bytes 737280 | tf_op jit(solution)/shard_map/all_gather | solution.py:211
  169.7 5.2 %all-gather.5.cloned.1.call-done = bf16[1152,2304]{1,0:T(8,128)(2,1)} async-done(((bf16[144,2304]{1,0:T(8,128)(2,1)}), bf16[1152,2304]{1,0:T(8,128)(2,1)}) %all-gather.5.cloned.1.call-update) | async-done | bytes 5308432 | tf_op jit(solution)/shard_map/all_gather | solution.py:128
  174.9 2.9 convolution_add_fusion
  179.1 1.3 copy-done.62
  180.3 1.4 fusion.91
  188.3 2.7 pad_maximum_fusion
  191.0 8.5 %copy.278 = bf16[1152,2304]{1,0:T(8,128)(2,1)} copy(bf16[1152,2304]{0,1:T(8,128)(2,1)} %pad_maximum_fusion) | data formatting | bytes 10616832
  199.6 1.4 bitcast_add_fusion.1
  201.0 1.5 collective-permute-start.6
  204.3 3.4 collective-permute-done.6
  207.9 2.1 collective-permute-done.4
  210.0 2.0 fusion.65
  212.1 7.6 %all_gather.15 = bf16[256,1152]{1,0:T(8,128)(2,1)S(1)} all-gather(bf16[64,1152]{1,0:T(8,128)(2,1)S(1)} %fusion.66), channel_id=1, replica_groups=mesh['da'=2,'db'=4,'mp'=4] {'mp'}, dimensions={0}, use_global_device_ids=true | all-gather | bytes 737280 | tf_op jit(solution)/shard_map/all_gather | solution.py:227
  219.7 2.2 convolution_convert_fusion.5
  222.0 13.6 %all_to_all.66 = bf16[4,72,256]{2,1,0:T(8,128)(2,1)S(1)} all-to-all(bf16[4,72,256]{2,1,0:T(8,128)(2,1)S(1)} %bitcast.247), channel_id=1, replica_groups=mesh['da'=2,'db'=4,'mp'=4] {'db'}, dimensions={0} | all-to-all | bytes 294912 | tf_op jit(solution)/shard_map/all_to_all | solution.py:240
  236.7 2.2 multiply_convert_fusion
  240.7 2.0 fusion.87
  242.8 21.6 %collective-permute-done.7 = bf16[144,1024]{1,0:T(8,128)(2,1)S(1)} collective-permute-done((bf16[144,1024]{1,0:T(8,128)(2,1)S(1)}, bf16[144,1024]{1,0:T(8,128)(2,1)S(1)}, u32[]{:S(2)}, u32[]{:S(2)}) %collective-permute-start.7) | collective-permute-done | bytes 294944 | tf_op jit(solution)/shard_map/ppermute | solution.py:76
  265.3 13.4 %all_to_all.67 = bf16[4,216,256]{2,1,0:T(8,128)(2,1)} all-to-all(bf16[4,216,256]{2,1,0:T(8,128)(2,1)S(1)} %maximum_bitcast_fusion.1), channel_id=1, replica_groups=mesh['da'=2,'db'=4,'mp'=4] {'db'}, dimensions={0} | all-to-all | bytes 884736 | tf_op jit(solution)/shard_map/all_to_all | solution.py:204
  278.7 2.0 copy.264
  280.7 2.6 fusion.9
  283.4 1.6 collective-permute-done.8
  286.6 1.5 collective-permute-start.9
  289.7 3.0 collective-permute-done.9
  293.8 1.3 fusion.79
  295.3 1.9 multiply_dynamic-update-slice_fusion.2
  299.4 1.5 fusion.67
  302.2 3.3 all-to-all-start.6
  306.3 13.5 %reduce-scatter.7.cloned.1.call-done = bf16[144,2304]{1,0:T(8,128)(2,1)} async-done(((bf16[1152,2304]{1,0:T(8,128)(2,1)}), bf16[144,2304]{1,0:T(8,128)(2,1)}) %reduce-scatter.7.cloned.1.call-update) | async-done | bytes 663568
  319.9 2.3 copy.279
  322.1 2.4 copy.280
  327.2 3.7 all-to-all-start.9
  332.3 36.6 %all-to-all-done.9 = bf16[8,144,288]{2,1,0:T(8,128)(2,1)S(1)} async-done(((bf16[8,144,288]{2,1,0:T(8,128)(2,1)}), bf16[8,144,288]{2,1,0:T(8,128)(2,1)S(1)}, u32[]{:S(2)}, u32[]{:S(2)}) %all-to-all-start.9) | async-done | bytes 663584 | tf_op jit(solution)/shard_map/all_to_all | solution.py:263
  369.6 3.0 all-to-all-start.7
  373.4 7.8 %all-to-all-done.7 = f32[32,1,1224]{2,1,0:T(1,128)S(1)} async-done(((f32[32,1,1224]{2,1,0:T(1,128)}), f32[32,1,1224]{2,1,0:T(1,128)S(1)}, u32[]{:S(2)}, u32[]{:S(2)}) %all-to-all-start.7) | async-done | bytes 156704 | tf_op jit(solution)/shard_map/all_to_all | solution.py:62
  383.2 2.8 all-to-all-start.8
  389.8 1.6 fusion.94
  391.4 2.4 all-to-all-done.8
  396.1 2.4 copy.273
  399.7 4.1 reduce-scatter.9.cloned.1.call-done
  (308 shorter events, 59.8 us)
Async XLA Ops:
  7.2 5.3 %copy-start = (bf16[144,1728]{1,0:T(8,128)(2,1)S(1)}, bf16[144,1728]{1,0:T(8,128)(2,1)}, u32[]{:S(2)}) copy-start(bf16[144,1728]{1,0:T(8,128)(2,1)} %param.29) | copy-start | bytes 1492996
  7.2 2.5 copy-start.60
  7.2 2.5 copy-start.61
  7.2 64.7 %all-gather.3.cloned.1.call-start = ((), (), s32[]{:S(2)}) async-start(), calls=%async_computation.12 | async-start | bytes 2985984 | tf_op jit(solution)/shard_map/all_gather | solution.py:124
  11.3 9.6 %copy-start.44 = (bf16[1152,144]{0,1:T(8,128)(2,1)S(1)}, bf16[1152,144]{0,1:T(8,128)(2,1)}, u32[]{:S(2)}) copy-start(bf16[1152,144]{0,1:T(8,128)(2,1)} %param.27) | copy-start | bytes 995332
  11.3 9.6 %copy-start.45 = (bf16[144,1152]{1,0:T(8,128)(2,1)S(1)}, bf16[144,1152]{1,0:T(8,128)(2,1)}, u32[]{:S(2)}) copy-start(bf16[144,1152]{1,0:T(8,128)(2,1)} %param.25) | copy-start | bytes 995332
  12.5 10.0 %copy-start.4 = (bf16[256,1152]{1,0:T(8,128)(2,1)S(1)}, bf16[256,1152]{1,0:T(8,128)(2,1)}, u32[]{:S(2)}) copy-start(bf16[256,1152]{1,0:T(8,128)(2,1)} %param.17) | copy-start | bytes 1769476
  13.5 14.1 %all-to-all-start = ((f32[8,1,864]{2,1,0:T(1,128)}), f32[8,1,864]{2,1,0:T(1,128)S(1)}, u32[]{:S(2)}, u32[]{:S(2)}) async-start(f32[8,1,864]{2,1,0:T(1,128)} %all_to_all.54), calls=%async_computation | async-start | bytes 57344 | tf_op jit(solution)/shard_map/all_to_all | solution.py:141
  20.8 154.0 %all-gather.5.cloned.1.call-start = ((), (), s32[]{:S(2)}) async-start(), calls=%async_computation.13 | async-start | bytes 5971968 | tf_op jit(solution)/shard_map/all_gather | solution.py:128
  20.9 2.1 copy-start.58
  20.9 2.3 copy-start.52
  28.4 12.0 %all-to-all-start.1 = ((f32[32,1,864]{2,1,0:T(1,128)}), f32[32,1,864]{2,1,0:T(1,128)S(1)}, u32[]{:S(2)}, u32[]{:S(2)}) async-start(f32[32,1,864]{2,1,0:T(1,128)} %broadcast_in_dim.24), calls=%async_computation.1 | async-start | bytes 229376 | tf_op jit(solution)/shard_map/all_to_all | solution.py:62
  31.0 11.9 %copy-start.56 = (f32[256]{0:T(256)}, f32[256]{0:T(256)S(1)}, u32[]{:S(2)}) copy-start(f32[256]{0:T(256)S(1)} %add_rsqrt_fusion) | copy-start | bytes 3076
  44.2 30.1 %copy-start.23 = (bf16[256,1152]{1,0:T(8,128)(2,1)}, bf16[256,1152]{1,0:T(8,128)(2,1)S(1)}, u32[]{:S(2)}) copy-start(bf16[256,1152]{1,0:T(8,128)(2,1)S(1)} %get-tuple-element.155) | copy-start | bytes 1769476
  84.5 32.8 %collective-permute-start = (bf16[4,152,256]{2,1,0:T(8,128)(2,1)S(1)}, bf16[4,152,256]{2,1,0:T(8,128)(2,1)S(1)}, u32[]{:S(2)}, u32[]{:S(2)}) collective-permute-start(bf16[4,152,256]{2,1,0:T(8,128)(2,1)S(1)} %get-tuple-element.157), channel_id=1, source_target_pairs={{0,16},{16,0},{1,17},{17,1},{2,18},{18,2},{3,19},{19,3},{4,20},{20... | collective-permute-start | bytes 933896 | tf_op jit(solution)/shard_map/ppermute | solution.py:67
  118.0 10.9 %copy-start.15 = (bf16[72,2048]{1,0:T(8,128)(2,1)}, bf16[72,2048]{1,0:T(8,128)(2,1)S(1)}, u32[]{:S(2)}) copy-start(bf16[72,2048]{1,0:T(8,128)(2,1)S(1)} %slice.115) | copy-start | bytes 884740
  118.3 5.6 %copy-start.32 = (bf16[72,2048]{1,0:T(8,128)(2,1)}, bf16[72,2048]{1,0:T(8,128)(2,1)S(1)}, u32[]{:S(2)}) copy-start(bf16[72,2048]{1,0:T(8,128)(2,1)S(1)} %slice.120) | copy-start | bytes 884740
  124.0 3.5 copy-start.1
  131.0 14.6 %copy-start.27 = (bf16[72,1024]{1,0:T(8,128)(2,1)}, bf16[72,1024]{1,0:T(8,128)(2,1)S(1)}, u32[]{:S(2)}) copy-start(bf16[72,1024]{1,0:T(8,128)(2,1)S(1)} %convolution_convert_fusion.4) | copy-start | bytes 442372
  131.7 13.8 %all-to-all-start.3 = ((bf16[4,72,256]{2,1,0:T(8,128)(2,1)}), bf16[4,72,256]{2,1,0:T(8,128)(2,1)S(1)}, u32[]{:S(2)}, u32[]{:S(2)}) async-start(bf16[4,72,256]{2,1,0:T(8,128)(2,1)} %bitcast.197), calls=%async_computation.3 | async-start | bytes 294912 | tf_op jit(solution)/shard_map/all_to_all | solution.py:204
  135.0 184.9 %reduce-scatter.7.cloned.1.call-start = ((), (), s32[]{:S(2)}) async-start(), calls=%async_computation.14 | async-start | bytes 5971968
  135.2 19.9 %copy-start.48 = (pred[256,4]{1,0:T(32,128)(4,1)}, pred[256,4]{1,0:T(32,128)(4,1)S(1)}, u32[]{:S(2)}) copy-start(pred[256,4]{1,0:T(32,128)(4,1)S(1)} %iota_compare_fusion.1) | copy-start | bytes 3076
  148.6 3.9 collective-permute-start.1
  150.9 61.1 %copy-start.53 = (f32[64]{0:T(128)}, f32[64]{0:T(128)S(1)}, u32[]{:S(2)}) copy-start(f32[64]{0:T(128)S(1)} %dynamic-slice.6) | copy-start | bytes 772
  152.4 2.6 copy-start.38
  152.5 7.5 %copy-start.50 = (f32[1152]{0:T(1024)S(1)}, f32[1152]{0:T(1024)}, u32[]{:S(2)}) copy-start(f32[1152]{0:T(1024)} %param.24) | copy-start | bytes 13828
  153.5 7.7 %copy-start.11 = (f32[2,64,1152]{2,1,0:T(8,128)}, f32[2,64,1152]{2,1,0:T(8,128)S(1)}, u32[]{:S(2)}) copy-start(f32[2,64,1152]{2,1,0:T(8,128)S(1)} %bitcast_add_fusion.3) | copy-start | bytes 1769476
  153.6 6.4 %collective-permute-start.2 = (bf16[64,1152]{1,0:T(8,128)(2,1)S(1)}, bf16[64,1152]{1,0:T(8,128)(2,1)S(1)}, u32[]{:S(2)}, u32[]{:S(2)}) collective-permute-start(bf16[64,1152]{1,0:T(8,128)(2,1)S(1)} %fusion.53), channel_id=1, source_target_pairs={{0,2},{1,3},{2,0},{3,1},{4,6},{5,7},{6,4},{7,5},{8,10},{9,11},{10,... | collective-permute-start | bytes 442376 | tf_op jit(solution)/shard_map/ppermute | solution.py:58
  161.2 13.7 %copy-start.63 = (f32[1152]{0:T(1024)S(1)}, f32[1152]{0:T(1024)}, u32[]{:S(2)}) copy-start(f32[1152]{0:T(1024)} %param.26) | copy-start | bytes 13828
  177.8 2.5 copy-start.62
  184.9 14.7 %collective-permute-start.5 = (bf16[2,64,1152]{2,1,0:T(8,128)(2,1)}, bf16[2,64,1152]{2,1,0:T(8,128)(2,1)}, u32[]{:S(2)}, u32[]{:S(2)}) collective-permute-start(bf16[2,64,1152]{2,1,0:T(8,128)(2,1)} %fusion.38), channel_id=1, source_target_pairs={{0,1},{1,0},{2,3},{3,2},{4,5},{5,4},{6,7},{7,6},{8,9},{9,8},{10,11... | collective-permute-start | bytes 884744 | tf_op jit(solution)/shard_map/ppermute | solution.py:55
  187.8 14.8 %collective-permute-start.3 = (bf16[2,64,1152]{2,1,0:T(8,128)(2,1)}, bf16[2,64,1152]{2,1,0:T(8,128)(2,1)}, u32[]{:S(2)}, u32[]{:S(2)}) collective-permute-start(bf16[2,64,1152]{2,1,0:T(8,128)(2,1)} %fusion.40), channel_id=1, source_target_pairs={{0,1},{1,0},{2,3},{3,2},{4,5},{5,4},{6,7},{7,6},{8,9},{9,8},{10,11... | collective-permute-start | bytes 884744 | tf_op jit(solution)/shard_map/ppermute | solution.py:55
  199.6 3.0 copy-start.35
  199.6 10.4 %copy-start.51 = (f32[1152]{0:T(1024)S(1)}, f32[1152]{0:T(1024)}, u32[]{:S(2)}) copy-start(f32[1152]{0:T(1024)} %param.28) | copy-start | bytes 13828
  199.6 37.0 %slice-start = ((s8[8388608]{0:T(1024)(128)(4,1)}), s8[4194304]{0:T(1024)(128)(4,1)S(1)}, s32[]{:S(2)}) async-start(s8[8388608]{0:T(1024)(128)(4,1)} %bitcast.205), calls=%async_computation.16 | async-start | bytes 8388608
  201.0 6.9 %copy-start.7 = (f32[2,64,1152]{2,1,0:T(8,128)}, f32[2,64,1152]{2,1,0:T(8,128)S(1)}, u32[]{:S(2)}) copy-start(f32[2,64,1152]{2,1,0:T(8,128)S(1)} %bitcast_add_fusion.1) | copy-start | bytes 1769476
  201.0 6.7 %collective-permute-start.6 = (bf16[64,1152]{1,0:T(8,128)(2,1)S(1)}, bf16[64,1152]{1,0:T(8,128)(2,1)S(1)}, u32[]{:S(2)}, u32[]{:S(2)}) collective-permute-start(bf16[64,1152]{1,0:T(8,128)(2,1)S(1)} %fusion.55), channel_id=1, source_target_pairs={{0,2},{1,3},{2,0},{3,1},{4,6},{5,7},{6,4},{7,5},{8,10},{9,11},{10,... | collective-permute-start | bytes 442376 | tf_op jit(solution)/shard_map/ppermute | solution.py:58
  203.6 8.4 %copy-start.13 = (f32[2,64,1152]{2,1,0:T(8,128)}, f32[2,64,1152]{2,1,0:T(8,128)S(1)}, u32[]{:S(2)}) copy-start(f32[2,64,1152]{2,1,0:T(8,128)S(1)} %bitcast_add_fusion.2) | copy-start | bytes 1769476
  203.6 6.4 %collective-permute-start.4 = (bf16[64,1152]{1,0:T(8,128)(2,1)S(1)}, bf16[64,1152]{1,0:T(8,128)(2,1)S(1)}, u32[]{:S(2)}, u32[]{:S(2)}) collective-permute-start(bf16[64,1152]{1,0:T(8,128)(2,1)S(1)} %fusion.54), channel_id=1, source_target_pairs={{0,2},{1,3},{2,0},{3,1},{4,6},{5,7},{6,4},{7,5},{8,10},{9,11},{10,... | collective-permute-start | bytes 442376 | tf_op jit(solution)/shard_map/ppermute | solution.py:58
  207.7 2.3 copy-start.25
  210.0 25.6 %copy-start.28 = (bf16[72,1024]{1,0:T(8,128)(2,1)S(1)}, bf16[72,1024]{1,0:T(8,128)(2,1)}, u32[]{:S(2)}) copy-start(bf16[72,1024]{1,0:T(8,128)(2,1)} %copy-done.27) | copy-start | bytes 442372
  212.0 10.0 %copy-start.17 = (f32[64,1152]{1,0:T(8,128)}, f32[64,1152]{1,0:T(8,128)S(1)}, u32[]{:S(2)}) copy-start(f32[64,1152]{1,0:T(8,128)S(1)} %get-tuple-element.141) | copy-start | bytes 884740
  212.0 23.7 %copy-start.3 = (bf16[1024,2048]{1,0:T(8,128)(2,1)S(1)}, bf16[1024,2048]{1,0:T(8,128)(2,1)}, u32[]{:S(2)}) copy-start(bf16[1024,2048]{1,0:T(8,128)(2,1)} %copy-done.2) | copy-start | bytes 12582916
  212.1 24.5 %slice-start.1 = ((s8[8388608]{0:T(1024)(128)(4,1)}), s8[4194304]{0:T(1024)(128)(4,1)S(1)}, s32[]{:S(2)}) async-start(s8[8388608]{0:T(1024)(128)(4,1)} %bitcast.205), calls=%async_computation.17 | async-start | bytes 8388608
  219.7 15.9 %copy-start.21 = (bf16[256,1152]{1,0:T(8,128)(2,1)}, bf16[256,1152]{1,0:T(8,128)(2,1)S(1)}, u32[]{:S(2)}) copy-start(bf16[256,1152]{1,0:T(8,128)(2,1)S(1)} %all_gather.15) | copy-start | bytes 1769476
  236.7 2.2 copy-start.41
  239.8 24.5 %collective-permute-start.7 = (bf16[144,1024]{1,0:T(8,128)(2,1)S(1)}, bf16[144,1024]{1,0:T(8,128)(2,1)S(1)}, u32[]{:S(2)}, u32[]{:S(2)}) collective-permute-start(bf16[144,1024]{1,0:T(8,128)(2,1)S(1)} %fusion.36), channel_id=1, source_target_pairs={{0,16},{16,0},{1,17},{17,1},{2,18},{18,2},{3,19},{19,3},{4,20},{20... | collective-permute-start | bytes 884744 | tf_op jit(solution)/shard_map/ppermute | solution.py:76
  283.3 4.8 %copy-start.57 = (f32[256]{0:T(256)S(1)}, f32[256]{0:T(256)}, u32[]{:S(2)}) copy-start(f32[256]{0:T(256)} %copy-done.56) | copy-start | bytes 3076
  283.4 1.6 collective-permute-start.8
  286.6 6.2 %collective-permute-start.9 = (bf16[64,1152]{1,0:T(8,128)(2,1)}, bf16[64,1152]{1,0:T(8,128)(2,1)}, u32[]{:S(2)}, u32[]{:S(2)}) collective-permute-start(bf16[64,1152]{1,0:T(8,128)(2,1)} %fusion.56), channel_id=1, source_target_pairs={{0,2},{1,3},{2,0},{3,1},{4,6},{5,7},{6,4},{7,5},{8,10},{9,11},{10,... | collective-permute-start | bytes 442376 | tf_op jit(solution)/shard_map/ppermute | solution.py:58
  288.2 7.0 %copy-start.12 = (f32[2,64,1152]{2,1,0:T(8,128)S(1)}, f32[2,64,1152]{2,1,0:T(8,128)}, u32[]{:S(2)}) copy-start(f32[2,64,1152]{2,1,0:T(8,128)} %copy-done.11) | copy-start | bytes 1769476
  288.2 7.0 %copy-start.18 = (f32[64,1152]{1,0:T(8,128)S(1)}, f32[64,1152]{1,0:T(8,128)}, u32[]{:S(2)}) copy-start(f32[64,1152]{1,0:T(8,128)} %copy-done.17) | copy-start | bytes 884740
  288.2 7.0 %copy-start.43 = (bf16[64,1152]{1,0:T(8,128)(2,1)S(1)}, bf16[64,1152]{1,0:T(8,128)(2,1)}, u32[]{:S(2)}) copy-start(bf16[64,1152]{1,0:T(8,128)(2,1)} %copy-done.42) | copy-start | bytes 442372
  288.2 7.0 %copy-start.54 = (f32[64]{0:T(128)S(1)}, f32[64]{0:T(128)}, u32[]{:S(2)}) copy-start(f32[64]{0:T(128)} %copy-done.53) | copy-start | bytes 772
  299.3 6.2 %copy-start.9 = (bf16[4,216,256]{2,1,0:T(8,128)(2,1)S(1)}, bf16[4,216,256]{2,1,0:T(8,128)(2,1)}, u32[]{:S(2)}) copy-start(bf16[4,216,256]{2,1,0:T(8,128)(2,1)} %all_to_all.67) | copy-start | bytes 1327108
  299.4 6.2 %copy-start.24 = (bf16[256,1152]{1,0:T(8,128)(2,1)S(1)}, bf16[256,1152]{1,0:T(8,128)(2,1)}, u32[]{:S(2)}) copy-start(bf16[256,1152]{1,0:T(8,128)(2,1)} %copy-done.23) | copy-start | bytes 1769476
  302.2 25.0 %all-to-all-start.6 = ((f32[32,1,1080]{2,1,0:T(1,128)}), f32[32,1,1080]{2,1,0:T(1,128)}, u32[]{:S(2)}, u32[]{:S(2)}) async-start(f32[32,1,1080]{2,1,0:T(1,128)} %copy.267), calls=%async_computation.6 | async-start | bytes 294912 | tf_op jit(solution)/shard_map/all_to_all | solution.py:294
  305.5 98.3 %reduce-scatter.9.cloned.1.call-start = ((), (), s32[]{:S(2)}) async-start(), calls=%async_computation.15 | async-start | bytes 2322432
  326.0 5.0 %copy-start.29 = (f32[144,1024]{1,0:T(8,128)S(1)}, f32[144,1024]{1,0:T(8,128)}, u32[]{:S(2)}) copy-start(f32[144,1024]{1,0:T(8,128)} %get-tuple-element.144) | copy-start | bytes 1769476
  327.2 5.0 %copy-start.59 = (f32[72]{0:T(128)S(1)}, f32[72]{0:T(128)}, u32[]{:S(2)}) copy-start(f32[72]{0:T(128)} %get-tuple-element.158) | copy-start | bytes 868
  327.2 41.6 %all-to-all-start.9 = ((bf16[8,144,288]{2,1,0:T(8,128)(2,1)}), bf16[8,144,288]{2,1,0:T(8,128)(2,1)S(1)}, u32[]{:S(2)}, u32[]{:S(2)}) async-start(bf16[8,144,288]{2,1,0:T(8,128)(2,1)} %bitcast.56), calls=%async_computation.9 | async-start | bytes 1769472 | tf_op jit(solution)/shard_map/all_to_all | solution.py:263
  369.6 11.6 %all-to-all-start.7 = ((f32[32,1,1224]{2,1,0:T(1,128)}), f32[32,1,1224]{2,1,0:T(1,128)S(1)}, u32[]{:S(2)}, u32[]{:S(2)}) async-start(f32[32,1,1224]{2,1,0:T(1,128)} %broadcast_in_dim.30), calls=%async_computation.7 | async-start | bytes 327680 | tf_op jit(solution)/shard_map/all_to_all | solution.py:62
  381.9 13.0 %copy-start.5 = (bf16[144,2304]{0,1:T(8,128)(2,1)S(1)}, bf16[144,2304]{0,1:T(8,128)(2,1)}, u32[]{:S(2)}) copy-start(bf16[144,2304]{0,1:T(8,128)(2,1)} %copy.279) | copy-start | bytes 1990660
  383.2 10.5 %all-to-all-start.8 = ((f32[32,1,576]{2,1,0:T(1,128)}), f32[32,1,576]{2,1,0:T(1,128)S(1)}, u32[]{:S(2)}, u32[]{:S(2)}) async-start(f32[32,1,576]{2,1,0:T(1,128)} %broadcast_in_dim.32), calls=%async_computation.8 | async-start | bytes 163840 | tf_op jit(solution)/shard_map/all_to_all | solution.py:62
  (23 other events, 31.0 us)
Sparse Core Ops, SparseCore 0:
  12.4 59.4 all-gather.2
  74.7 100.1 all-gather.4
  199.7 120.1 reduce-scatter.6
  324.7 79.1 reduce-scatter.8

commit v4 on v3

--- a/solution.py
+++ b/solution.py
@@ -60,6 +60,12 @@
 
 def spread(values, axes, count):
     return lax.all_to_all(jnp.broadcast_to(values[None], (count,) + values.shape), axes, 0, 0)
+
+
+def doubled(rows, axis, bit):
+    got = lax.ppermute(rows, axis, [(i, i ^ bit) for i in range(4)])
+    low = (lax.axis_index(axis) & bit) == 0
+    return jnp.concatenate([jnp.where(low, rows, got), jnp.where(low, got, rows)])
 
 
 def neighbours(block_kv, blocks):
@@ -120,7 +126,9 @@
     attn_local = jnp.transpose(
         attn_weight.reshape(3, weight_rows, heads_here, HD), (1, 2, 0, 3)
     )
-    attn_local = attn_local[:, :, jnp.array([1, 2, 0])].reshape(weight_rows, 3 * columns)
+    attn_local = jnp.concatenate([attn_local[:, :, 1:], attn_local[:, :, :1]], axis=2).reshape(
+        weight_rows, 3 * columns
+    )
     attn_and_out = lax.all_gather(
         jnp.concatenate([attn_local, out_weight.T], axis=1), DP, axis=0, tiled=True
     )
@@ -161,6 +169,8 @@
     token_s = own_rows(token_vals)
     normed_one, inv_one = normalize(token_vals)
     attn_input = (normed_one * (1.0 + scale_attn) + shift_attn).astype(BF)
+    block_input = doubled(doubled(own_rows(attn_input), "db", 1), "db", 2)
+    block_input = doubled(doubled(block_input, "mp", 2), "mp", 1)
 
     head_bias = attn_bias.reshape(2, heads_here, HD)
     bias_t = jnp.stack([jnp.zeros_like(head_bias[0]), head_bias[1], head_bias[0]], axis=1)
@@ -254,18 +264,21 @@
     attn_b_part = jnp.concatenate(
         [jnp.sum(grad_query_t, axis=1), jnp.sum(grad_kv_own[HD:], axis=1)]
     )
-    grad_kvq_t = to_owners(jnp.concatenate([grad_kv_own, grad_query_t]).astype(BF))
-    grad_attn_w = dot(attn_input, grad_kvq_t, 0, 1)
+    head_grads = jnp.concatenate([grad_kv_own, grad_query_t]).astype(BF)
+    grad_kvq_t = to_owners(head_grads)
+    ordered = jnp.transpose(
+        head_grads.reshape(3 * HD, BLOCK, 2, 2, share), (0, 3, 2, 1, 4)
+    ).reshape(3 * HD, block_rows)
+    grad_attn_w = dot(block_input, ordered, 0, 1)
     grad_out_w = dot(grad_attn_b, attended_t, 0, 1)
-    attn_terms, mlp_w = lax.optimization_barrier((grad_attn_w.astype(BF), mlp_w))
+    terms = jnp.concatenate([grad_attn_w.astype(BF), grad_out_w.astype(BF)], axis=1)
+    terms, mlp_w = lax.optimization_barrier((terms, mlp_w))
     up_w_out, down_w_out = mlp_w[:, :hidden_cols].astype(F32), mlp_w[:, hidden_cols:].T.astype(F32)
-    pieces = grad_out_w.astype(BF).reshape(n_dp, weight_rows, columns)
-    out_w_out = jnp.sum(lax.all_to_all(pieces, DP, 0, 0).astype(F32), axis=0).T
-    attn_w = lax.psum_scatter(attn_terms, DP, scatter_dimension=0, tiled=True).astype(F32)
-    attn_w_out = attn_w.reshape(weight_rows, heads_here, 3, HD)
-    attn_w_out = jnp.transpose(attn_w_out[:, :, jnp.array([2, 0, 1])], (2, 0, 1, 3)).reshape(
-        3, weight_rows, columns
-    )
+    terms = lax.all_to_all(terms.reshape(n_dp, weight_rows, 3 * HD + columns), DP, 0, 0)
+    out_w_out = jnp.sum(terms[:, :, 3 * HD :].astype(F32), axis=0).T
+    attn_w = terms[:, :, : 3 * HD].astype(F32).reshape(blocks, heads_here, weight_rows, 3, HD)
+    attn_w = jnp.transpose(jnp.sum(attn_w, axis=0), (2, 1, 0, 3)).reshape(3, weight_rows, columns)
+    attn_w_out = jnp.stack([attn_w[2], attn_w[0], attn_w[1]])
     grad_attn_in_s = scatter_rows(dot(grad_kvq_t, attn_full, 0, 1))
     normed_one_s = own_rows(normed_one)
     inv_one_s = own_rows(inv_one)

time: 420 us -> 403 us (0.960)
  blocking collectives: 52.7 us -> 15.3 us
  waiting for transfers between devices: 187 us -> 169 us
  other arithmetic: 30.7 us -> 45.4 us
  starting transfers between devices: 34.5 us -> 48.7 us
  matrix products: 36.8 us -> 43.7 us
    all_to_all x3 -> x0, blocking collectives: 37 us -> none  [the longest x1 13.6 us: shards(): lax.all_to_all(grad_attended_t.reshape(heads_here, HD, tok_rows), 'db', 0...]
    ppermute x0 -> x4, waiting for transfers between devices: none -> 19 us  [doubled(): got = lax.ppermute(rows, axis, [(i, i ^ bit) for i in range(4)])]
    unnamed x6 -> x4, waiting for transfers between devices: 17.7 us -> 0.07 us
    all_to_all x1 -> x3, starting transfers between devices: 3.73 us -> 11.8 us  [the longest x1 4.16 us: shards(): lax.all_to_all(grad_attended_t.reshape(heads_here, HD, tok_rows), 'db', 0...]
    dot_general x19, matrix products: 30 us -> 37 us  [dot(): lax.dot_general(left, right, (((left_dim,), (right_dim,)), ((), ())), pre...]
    select_n x0 -> x4, other arithmetic: none -> 6.58 us  [doubled(): jnp.where(low, rows, got)]
    ppermute x1, waiting for transfers between devices: 21.6 us -> 15 us  [return_grads(): return lax.ppermute(pieces[0], 'da', [(0, 1), (1, 0)]).astype(F32)]
    all_to_all x1, waiting for transfers between devices: 0.01 us -> 6.54 us  [shards(): lax.all_to_all(jnp.concatenate([pieces, both_piece, up_piece], axis=1), A...]
  transfers between devices with their start and end apart: 21 -> 27, of which waited for: 17 -> 19; matrix products, arithmetic and copies ran while one was open for 23% -> 31% of each run, Pallas kernels for 0% -> 0%
where the time goes in v4:
time: 403 us; the launch traced here: 397 us
  waiting for transfers between devices  169 us (42%)
  local copies, waits for them, and re-layouts  58.7 us (15%)
  starting transfers between devices  48.7 us (12%)
  other arithmetic  45.4 us (11%)
  matrix products  43.7 us (11%)
  between operations  16.2 us (4%)
  blocking collectives  15.3 us (4%)
    dot_general x19, matrix products, dot(): lax.dot_general(left, right, (((left_dim,), (right_dim,)), ((), ())), pre...  37 us
    all_gather x1, waiting for transfers between devices, shards(): lax.all_gather(jnp.concatenate([attn_local, out_weight.T], axis=1), DP, a...  28.5 us
    ppermute x1, waiting for transfers between devices, neighbours(): return [lax.ppermute(block_kv, 'da', [(0, 1), (1, 0)])]  25.6 us
    unnamed x135, local copies, waits for them, and re-layouts  24.5 us
    ppermute x4, waiting for transfers between devices, doubled(): got = lax.ppermute(rows, axis, [(i, i ^ bit) for i in range(4)])  19 us
    all_to_all x1, waiting for transfers between devices, shards(): lax.all_to_all(terms.reshape(n_dp, weight_rows, 3 * HD + columns), DP, 0, 0)  17.4 us
    all_to_all x3, waiting for transfers between devices, spread(): lax.all_to_all(jnp.broadcast_to(values[None], (count,) + values.shape), a...  15.8 us
    ppermute x1, waiting for transfers between devices, return_grads(): return lax.ppermute(pieces[0], 'da', [(0, 1), (1, 0)]).astype(F32)  15 us
  transfers between devices with their start and end apart: 27, of which 19 were waited for; matrix products, arithmetic and copies ran while one was open for 31% of the time, Pallas kernels for 0%

profile of v4, /device:TPU:0, one launch (start us, length us, event | category | flops | bytes accessed | tf_op | source)
XLA Modules:
  0.0 396.7 jit_solution(15632005000448742818)
XLA Ops:
  11.5 7.3 %all-to-all-start = ((f32[8,1,864]{2,1,0:T(1,128)}), f32[8,1,864]{2,1,0:T(1,128)S(1)}, u32[]{:S(2)}, u32[]{:S(2)}) async-start(f32[8,1,864]{2,1,0:T(1,128)} %all_to_all.54), calls=%async_computation | async-start | bytes 57344 | tf_op jit(solution)/shard_map/all_to_all | solution.py:149
  21.3 4.3 %all-to-all-done = f32[8,1,864]{2,1,0:T(1,128)S(1)} async-done(((f32[8,1,864]{2,1,0:T(1,128)}), f32[8,1,864]{2,1,0:T(1,128)S(1)}, u32[]{:S(2)}, u32[]{:S(2)}) %all-to-all-start) | async-done | bytes 27680 | tf_op jit(solution)/shard_map/all_to_all | solution.py:149
  26.4 2.6 all-to-all-start.1
  29.0 9.6 %all-to-all-done.1 = f32[32,1,864]{2,1,0:T(1,128)S(1)} async-done(((f32[32,1,864]{2,1,0:T(1,128)}), f32[32,1,864]{2,1,0:T(1,128)S(1)}, u32[]{:S(2)}, u32[]{:S(2)}) %all-to-all-start.1) | async-done | bytes 110624 | tf_op jit(solution)/shard_map/all_to_all | solution.py:62
  40.4 1.4 subtract_multiply_fusion
  41.7 28.5 %all-gather.3.cloned.1.call-done = bf16[1152,1152]{1,0:T(8,128)(2,1)} async-done(((bf16[144,1152]{1,0:T(8,128)(2,1)}), bf16[1152,1152]{1,0:T(8,128)(2,1)}) %all-gather.3.cloned.1.call-update) | async-done | bytes 2654224 | tf_op jit(solution)/shard_map/all_gather | solution.py:132
  70.3 2.4 fusion.20
  73.5 4.1 %all-to-all-start.2 = ((bf16[4,224,256]{2,1,0:T(8,128)(2,1)}), bf16[4,224,256]{2,1,0:T(8,128)(2,1)S(1)}, u32[]{:S(2)}, u32[]{:S(2)}) async-start(bf16[4,224,256]{2,1,0:T(8,128)(2,1)} %pad_maximum_fusion.8), calls=%async_computation.2 | async-start | bytes 917504 | tf_op jit(solution)/shard_map/all_to_all | solution.py:185
  81.4 7.7 %all-to-all-done.2 = bf16[4,224,256]{2,1,0:T(8,128)(2,1)S(1)} async-done(((bf16[4,224,256]{2,1,0:T(8,128)(2,1)}), bf16[4,224,256]{2,1,0:T(8,128)(2,1)S(1)}, u32[]{:S(2)}, u32[]{:S(2)}) %all-to-all-start.2) | async-done | bytes 458784 | tf_op jit(solution)/shard_map/all_to_all | solution.py:185
  90.0 1.7 collective-permute-start.10
  92.4 25.6 %collective-permute-done = bf16[4,152,256]{2,1,0:T(8,128)(2,1)S(1)} collective-permute-done((bf16[4,152,256]{2,1,0:T(8,128)(2,1)S(1)}, bf16[4,152,256]{2,1,0:T(8,128)(2,1)S(1)}, u32[]{:S(2)}, u32[]{:S(2)}) %collective-permute-start) | collective-permute-done | bytes 311328 | tf_op jit(solution)/shard_map/ppermute | solution.py:73
  119.4 1.9 copy.265
  124.5 3.6 fusion.95
  129.4 2.0 copy-done.1
  131.4 1.5 fusion.1
  133.0 1.4 convolution_convert_fusion.4
  135.7 3.3 all-to-all-start.3
  139.1 1.4 fusion.60
  140.5 7.7 %all-to-all-done.3 = bf16[4,72,256]{2,1,0:T(8,128)(2,1)S(1)} async-done(((bf16[4,72,256]{2,1,0:T(8,128)(2,1)}), bf16[4,72,256]{2,1,0:T(8,128)(2,1)S(1)}, u32[]{:S(2)}, u32[]{:S(2)}) %all-to-all-start.3) | async-done | bytes 147488 | tf_op jit(solution)/shard_map/all_to_all | solution.py:214
  148.4 1.8 fusion.33
  152.0 1.5 collective-permute-start.2
  153.5 19.0 %collective-permute-done.11 = bf16[128,1152]{1,0:T(8,128)(2,1)S(1)} collective-permute-done((bf16[128,1152]{1,0:T(8,128)(2,1)S(1)}, bf16[128,1152]{1,0:T(8,128)(2,1)S(1)}, u32[]{:S(2)}, u32[]{:S(2)}) %collective-permute-start.11) | collective-permute-done | bytes 294944 | tf_op jit(solution)/shard_map/ppermute | solution.py:66
  175.0 8.1 %all_gather.13 = bf16[256,1152]{1,0:T(8,128)(2,1)} all-gather(bf16[64,1152]{1,0:T(8,128)(2,1)S(1)} %fusion.45), channel_id=1, replica_groups=mesh['da'=2,'db'=4,'mp'=4] {'mp'}, dimensions={0}, use_global_device_ids=true | all-gather | bytes 737280 | tf_op jit(solution)/shard_map/all_gather | solution.py:221
  183.1 2.9 convolution_add_fusion
  188.6 1.4 fusion.96
  196.6 2.7 pad_maximum_fusion
  199.3 8.6 %copy.293 = bf16[1152,2304]{1,0:T(8,128)(2,1)} copy(bf16[1152,2304]{0,1:T(8,128)(2,1)} %pad_maximum_fusion) | data formatting | bytes 10616832
  212.5 3.5 collective-permute-done.6
  216.2 2.3 collective-permute-done.4
  218.6 1.9 fusion.68
  220.6 7.1 %all_gather.15 = bf16[256,1152]{1,0:T(8,128)(2,1)S(1)} all-gather(bf16[64,1152]{1,0:T(8,128)(2,1)S(1)} %fusion.69), channel_id=1, replica_groups=mesh['da'=2,'db'=4,'mp'=4] {'mp'}, dimensions={0}, use_global_device_ids=true | all-gather | bytes 737280 | tf_op jit(solution)/shard_map/all_gather | solution.py:237
  228.6 2.7 convolution_convert_fusion.5
  231.3 4.2 %all-to-all-start.4 = ((bf16[4,72,256]{2,1,0:T(8,128)(2,1)}), bf16[4,72,256]{2,1,0:T(8,128)(2,1)}, u32[]{:S(2)}, u32[]{:S(2)}) async-start(bf16[4,72,256]{2,1,0:T(8,128)(2,1)} %bitcast.251), calls=%async_computation.4 | async-start | bytes 294912 | tf_op jit(solution)/shard_map/all_to_all | solution.py:250
  235.4 1.9 pad_maximum_fusion.7
  238.3 7.9 %all-to-all-done.4 = bf16[4,72,256]{2,1,0:T(8,128)(2,1)} async-done(((bf16[4,72,256]{2,1,0:T(8,128)(2,1)}), bf16[4,72,256]{2,1,0:T(8,128)(2,1)}, u32[]{:S(2)}, u32[]{:S(2)}) %all-to-all-start.4) | async-done | bytes 147488 | tf_op jit(solution)/shard_map/all_to_all | solution.py:250
  248.0 3.1 fusion.97
  251.1 4.8 %multiply_convert_fusion = bf16[1024,2048]{1,0:T(8,128)(2,1)S(1)} fusion(f32[1024,2048]{1,0:T(8,128)} %copy-done.1, bf16[72,1024]{1,0:T(8,128)(2,1)S(1)} %bitcast.215, bf16[72,2048]{1,0:T(8,128)(2,1)S(1)} %copy-done.18, f32[1024]{0:T(1024)S(1)} %multiply_reduce_fusion.2, f32[1024]{0:T(1024)S(1)} %log_add_fusion), kind=kOutput, calls=%fused_computation | convolution fusion | flops 310378496 | bytes 13033472 | tf_op jit(solution)/shard_map/dot_general | solution.py:43
  257.8 1.5 fusion.92
  259.9 15.0 %collective-permute-done.7 = bf16[144,1024]{1,0:T(8,128)(2,1)S(1)} collective-permute-done((bf16[144,1024]{1,0:T(8,128)(2,1)S(1)}, bf16[144,1024]{1,0:T(8,128)(2,1)S(1)}, u32[]{:S(2)}, u32[]{:S(2)}) %collective-permute-start.7) | collective-permute-done | bytes 294944 | tf_op jit(solution)/shard_map/ppermute | solution.py:82
  277.4 4.1 %all-to-all-start.5 = ((bf16[4,216,256]{2,1,0:T(8,128)(2,1)}), bf16[4,216,256]{2,1,0:T(8,128)(2,1)}, u32[]{:S(2)}, u32[]{:S(2)}) async-start(bf16[4,216,256]{2,1,0:T(8,128)(2,1)} %maximum_bitcast_fusion.2), calls=%async_computation.5 | async-start | bytes 884736 | tf_op jit(solution)/shard_map/all_to_all | solution.py:214
  281.5 1.5 broadcast_select_fusion.3
  284.4 4.6 %all-to-all-done.5 = bf16[4,216,256]{2,1,0:T(8,128)(2,1)} async-done(((bf16[4,216,256]{2,1,0:T(8,128)(2,1)}), bf16[4,216,256]{2,1,0:T(8,128)(2,1)}, u32[]{:S(2)}, u32[]{:S(2)}) %all-to-all-start.5) | async-done | bytes 442400 | tf_op jit(solution)/shard_map/all_to_all | solution.py:214
  289.0 2.0 copy.275
  291.0 2.7 fusion.12
  300.1 1.7 collective-permute-start.9
  301.9 3.2 broadcast_select_fusion.1
  308.9 1.9 multiply_dynamic-update-slice_fusion.2
  312.9 1.4 fusion.70
  315.7 3.3 all-to-all-start.6
  320.8 6.5 %all-to-all-done.6 = f32[32,1,1080]{2,1,0:T(1,128)} async-done(((f32[32,1,1080]{2,1,0:T(1,128)}), f32[32,1,1080]{2,1,0:T(1,128)}, u32[]{:S(2)}, u32[]{:S(2)}) %all-to-all-start.6) | async-done | bytes 138272 | tf_op jit(solution)/shard_map/all_to_all | solution.py:307
  329.3 2.8 all-to-all-start.7
  332.2 1.4 maximum_bitcast_fusion
  333.5 2.2 copy.281
  335.8 3.0 convolution_convert_fusion.3
  338.7 2.0 all-to-all-done.7
  342.8 3.9 all-to-all-start.8
  346.9 1.5 copy.294
  348.4 1.7 copy.282
  350.1 4.2 %all-to-all-done.8 = f32[32,1,576]{2,1,0:T(1,128)S(1)} async-done(((f32[32,1,576]{2,1,0:T(1,128)}), f32[32,1,576]{2,1,0:T(1,128)S(1)}, u32[]{:S(2)}, u32[]{:S(2)}) %all-to-all-start.8) | async-done | bytes 73760 | tf_op jit(solution)/shard_map/all_to_all | solution.py:62
  354.3 3.6 all-to-all-start.9
  361.6 1.6 fusion.99
  364.3 1.6 convert_bitcast_fusion
  365.9 2.5 copy.288
  369.6 17.4 %all-to-all-done.9 = bf16[8,144,504]{2,1,0:T(8,128)(2,1)S(1)} async-done(((bf16[8,144,504]{2,1,0:T(8,128)(2,1)}), bf16[8,144,504]{2,1,0:T(8,128)(2,1)S(1)}, u32[]{:S(2)}, u32[]{:S(2)}) %all-to-all-start.9) | async-done | bytes 1161248 | tf_op jit(solution)/shard_map/all_to_all | solution.py:277
  (324 shorter events, 78.2 us)
Async XLA Ops:
  7.2 3.3 copy-start
  7.2 63.1 %all-gather.3.cloned.1.call-start = ((), (), s32[]{:S(2)}) async-start(), calls=%async_computation.11 | async-start | bytes 2985984 | tf_op jit(solution)/shard_map/all_gather | solution.py:132
  9.3 9.5 %copy-start.51 = (bf16[1152,144]{0,1:T(8,128)(2,1)S(1)}, bf16[1152,144]{0,1:T(8,128)(2,1)}, u32[]{:S(2)}) copy-start(bf16[1152,144]{0,1:T(8,128)(2,1)} %param.25) | copy-start | bytes 995332
  9.3 9.5 %copy-start.52 = (bf16[144,1152]{1,0:T(8,128)(2,1)S(1)}, bf16[144,1152]{1,0:T(8,128)(2,1)}, u32[]{:S(2)}) copy-start(bf16[144,1152]{1,0:T(8,128)(2,1)} %param.23) | copy-start | bytes 995332
  10.6 9.8 %copy-start.3 = (bf16[256,1152]{1,0:T(8,128)(2,1)S(1)}, bf16[256,1152]{1,0:T(8,128)(2,1)}, u32[]{:S(2)}) copy-start(bf16[256,1152]{1,0:T(8,128)(2,1)} %param.15) | copy-start | bytes 1769476
  11.5 14.1 %all-to-all-start = ((f32[8,1,864]{2,1,0:T(1,128)}), f32[8,1,864]{2,1,0:T(1,128)S(1)}, u32[]{:S(2)}, u32[]{:S(2)}) async-start(f32[8,1,864]{2,1,0:T(1,128)} %all_to_all.54), calls=%async_computation | async-start | bytes 57344 | tf_op jit(solution)/shard_map/all_to_all | solution.py:149
  18.8 164.3 %all-gather.5.cloned.1.call-start = ((), (), s32[]{:S(2)}) async-start(), calls=%async_computation.12 | async-start | bytes 5971968 | tf_op jit(solution)/shard_map/all_gather | solution.py:136
  26.4 12.2 %all-to-all-start.1 = ((f32[32,1,864]{2,1,0:T(1,128)}), f32[32,1,864]{2,1,0:T(1,128)S(1)}, u32[]{:S(2)}, u32[]{:S(2)}) async-start(f32[32,1,864]{2,1,0:T(1,128)} %broadcast_in_dim.19), calls=%async_computation.1 | async-start | bytes 229376 | tf_op jit(solution)/shard_map/all_to_all | solution.py:62
  39.2 41.5 %copy-start.43 = (f32[4,6912]{1,0:T(4,128)}, f32[4,6912]{1,0:T(4,128)S(1)}, u32[]{:S(2)}) copy-start(f32[4,6912]{1,0:T(4,128)S(1)} %reshape.288) | copy-start | bytes 331780
  41.7 47.5 %copy-start.34 = (bf16[256,1152]{1,0:T(8,128)(2,1)}, bf16[256,1152]{1,0:T(8,128)(2,1)S(1)}, u32[]{:S(2)}) copy-start(bf16[256,1152]{1,0:T(8,128)(2,1)S(1)} %get-tuple-element.162) | copy-start | bytes 1769476
  73.5 5.2 %copy-start.23 = (bf16[256,1152]{1,0:T(8,128)(2,1)S(1)}, bf16[256,1152]{1,0:T(8,128)(2,1)}, u32[]{:S(2)}) copy-start(bf16[256,1152]{1,0:T(8,128)(2,1)} %param.29) | copy-start | bytes 1769476
  73.5 15.6 %all-to-all-start.2 = ((bf16[4,224,256]{2,1,0:T(8,128)(2,1)}), bf16[4,224,256]{2,1,0:T(8,128)(2,1)S(1)}, u32[]{:S(2)}, u32[]{:S(2)}) async-start(bf16[4,224,256]{2,1,0:T(8,128)(2,1)} %pad_maximum_fusion.8), calls=%async_computation.2 | async-start | bytes 917504 | tf_op jit(solution)/shard_map/all_to_all | solution.py:185
  89.2 28.8 %collective-permute-start = (bf16[4,152,256]{2,1,0:T(8,128)(2,1)S(1)}, bf16[4,152,256]{2,1,0:T(8,128)(2,1)S(1)}, u32[]{:S(2)}, u32[]{:S(2)}) collective-permute-start(bf16[4,152,256]{2,1,0:T(8,128)(2,1)S(1)} %get-tuple-element.166), channel_id=1, source_target_pairs={{0,16},{16,0},{1,17},{17,1},{2,18},{18,2},{3,19},{19,3},{4,20},{20... | collective-permute-start | bytes 933896 | tf_op jit(solution)/shard_map/ppermute | solution.py:73
  90.0 60.3 %collective-permute-start.10 = (bf16[64,1152]{1,0:T(8,128)(2,1)}, bf16[64,1152]{1,0:T(8,128)(2,1)}, u32[]{:S(2)}, u32[]{:S(2)}) collective-permute-start(bf16[64,1152]{1,0:T(8,128)(2,1)} %constant_dynamic-slice_fusion.1), channel_id=1, source_target_pairs={{0,4},{4,0},{8,12},{12,8},{1,5},{5,1},{9,13},{13,9},{2,6},{6,2},{1... | collective-permute-start | bytes 442376 | tf_op jit(solution)/shard_map/ppermute | solution.py:66
  119.4 13.5 %copy-start.17 = (bf16[72,2048]{1,0:T(8,128)(2,1)}, bf16[72,2048]{1,0:T(8,128)(2,1)S(1)}, u32[]{:S(2)}) copy-start(bf16[72,2048]{1,0:T(8,128)(2,1)S(1)} %slice.147) | copy-start | bytes 884740
  122.5 5.6 %copy-start.35 = (bf16[72,2048]{1,0:T(8,128)(2,1)}, bf16[72,2048]{1,0:T(8,128)(2,1)S(1)}, u32[]{:S(2)}) copy-start(bf16[72,2048]{1,0:T(8,128)(2,1)S(1)} %slice.152) | copy-start | bytes 884740
  128.1 3.3 copy-start.1
  133.0 6.2 %copy-start.44 = (f32[4,6912]{1,0:T(4,128)S(1)}, f32[4,6912]{1,0:T(4,128)}, u32[]{:S(2)}) copy-start(f32[4,6912]{1,0:T(4,128)} %copy-done.43) | copy-start | bytes 331780
  135.0 4.1 %copy-start.30 = (bf16[72,1024]{1,0:T(8,128)(2,1)}, bf16[72,1024]{1,0:T(8,128)(2,1)S(1)}, u32[]{:S(2)}) copy-start(bf16[72,1024]{1,0:T(8,128)(2,1)S(1)} %convolution_convert_fusion.4) | copy-start | bytes 442372
  135.7 12.5 %all-to-all-start.3 = ((bf16[4,72,256]{2,1,0:T(8,128)(2,1)}), bf16[4,72,256]{2,1,0:T(8,128)(2,1)S(1)}, u32[]{:S(2)}, u32[]{:S(2)}) async-start(bf16[4,72,256]{2,1,0:T(8,128)(2,1)} %bitcast.201), calls=%async_computation.3 | async-start | bytes 294912 | tf_op jit(solution)/shard_map/all_to_all | solution.py:214
  139.1 207.8 %reduce-scatter.4.cloned.1.call-start = ((), (), s32[]{:S(2)}) async-start(), calls=%async_computation.13 | async-start | bytes 5971968
  150.2 1.6 collective-permute-start.1
  151.4 22.0 %copy-start.55 = (f32[1152]{0:T(1024)S(1)}, f32[1152]{0:T(1024)}, u32[]{:S(2)}) copy-start(f32[1152]{0:T(1024)} %param.22) | copy-start | bytes 13828
  151.4 21.1 %collective-permute-start.11 = (bf16[128,1152]{1,0:T(8,128)(2,1)S(1)}, bf16[128,1152]{1,0:T(8,128)(2,1)S(1)}, u32[]{:S(2)}, u32[]{:S(2)}) collective-permute-start(bf16[128,1152]{1,0:T(8,128)(2,1)S(1)} %pad_maximum_fusion.10), channel_id=1, source_target_pairs={{0,8},{4,12},{8,0},{12,4},{1,9},{5,13},{9,1},{13,5},{2,10},{6,14},... | collective-permute-start | bytes 884744 | tf_op jit(solution)/shard_map/ppermute | solution.py:66
  151.9 22.7 %copy-start.13 = (f32[2,64,1152]{2,1,0:T(8,128)}, f32[2,64,1152]{2,1,0:T(8,128)S(1)}, u32[]{:S(2)}) copy-start(f32[2,64,1152]{2,1,0:T(8,128)S(1)} %bitcast_add_fusion.3) | copy-start | bytes 1769476
  152.0 21.4 %collective-permute-start.2 = (bf16[64,1152]{1,0:T(8,128)(2,1)S(1)}, bf16[64,1152]{1,0:T(8,128)(2,1)S(1)}, u32[]{:S(2)}, u32[]{:S(2)}) collective-permute-start(bf16[64,1152]{1,0:T(8,128)(2,1)S(1)} %fusion.56), channel_id=1, source_target_pairs={{0,2},{1,3},{2,0},{3,1},{4,6},{5,7},{6,4},{7,5},{8,10},{9,11},{10,... | collective-permute-start | bytes 442376 | tf_op jit(solution)/shard_map/ppermute | solution.py:58
  174.6 8.5 %copy-start.62 = (f32[1152]{0:T(1024)S(1)}, f32[1152]{0:T(1024)}, u32[]{:S(2)}) copy-start(f32[1152]{0:T(1024)} %param.24) | copy-start | bytes 13828
  186.1 2.5 copy-start.61
  193.2 14.7 %collective-permute-start.5 = (bf16[2,64,1152]{2,1,0:T(8,128)(2,1)}, bf16[2,64,1152]{2,1,0:T(8,128)(2,1)}, u32[]{:S(2)}, u32[]{:S(2)}) collective-permute-start(bf16[2,64,1152]{2,1,0:T(8,128)(2,1)} %fusion.41), channel_id=1, source_target_pairs={{0,1},{1,0},{2,3},{3,2},{4,5},{5,4},{6,7},{7,6},{8,9},{9,8},{10,11... | collective-permute-start | bytes 884744 | tf_op jit(solution)/shard_map/ppermute | solution.py:55
  196.4 14.0 %collective-permute-start.3 = (bf16[2,64,1152]{2,1,0:T(8,128)(2,1)}, bf16[2,64,1152]{2,1,0:T(8,128)(2,1)}, u32[]{:S(2)}, u32[]{:S(2)}) collective-permute-start(bf16[2,64,1152]{2,1,0:T(8,128)(2,1)} %fusion.43), channel_id=1, source_target_pairs={{0,1},{1,0},{2,3},{3,2},{4,5},{5,4},{6,7},{7,6},{8,9},{9,8},{10,11... | collective-permute-start | bytes 884744 | tf_op jit(solution)/shard_map/ppermute | solution.py:55
  207.9 2.6 copy-start.40
  209.2 7.0 %copy-start.10 = (f32[2,64,1152]{2,1,0:T(8,128)}, f32[2,64,1152]{2,1,0:T(8,128)S(1)}, u32[]{:S(2)}) copy-start(f32[2,64,1152]{2,1,0:T(8,128)S(1)} %bitcast_add_fusion.1) | copy-start | bytes 1769476
  209.2 6.8 %collective-permute-start.6 = (bf16[64,1152]{1,0:T(8,128)(2,1)S(1)}, bf16[64,1152]{1,0:T(8,128)(2,1)S(1)}, u32[]{:S(2)}, u32[]{:S(2)}) collective-permute-start(bf16[64,1152]{1,0:T(8,128)(2,1)S(1)} %fusion.58), channel_id=1, source_target_pairs={{0,2},{1,3},{2,0},{3,1},{4,6},{5,7},{6,4},{7,5},{8,10},{9,11},{10,... | collective-permute-start | bytes 442376 | tf_op jit(solution)/shard_map/ppermute | solution.py:58
  211.4 9.1 %copy-start.15 = (f32[2,64,1152]{2,1,0:T(8,128)}, f32[2,64,1152]{2,1,0:T(8,128)S(1)}, u32[]{:S(2)}) copy-start(f32[2,64,1152]{2,1,0:T(8,128)S(1)} %bitcast_add_fusion.2) | copy-start | bytes 1769476
  211.5 7.1 %copy-start.56 = (f32[1152]{0:T(1024)S(1)}, f32[1152]{0:T(1024)}, u32[]{:S(2)}) copy-start(f32[1152]{0:T(1024)} %param.26) | copy-start | bytes 13828
  211.5 7.1 %collective-permute-start.4 = (bf16[64,1152]{1,0:T(8,128)(2,1)S(1)}, bf16[64,1152]{1,0:T(8,128)(2,1)S(1)}, u32[]{:S(2)}, u32[]{:S(2)}) collective-permute-start(bf16[64,1152]{1,0:T(8,128)(2,1)S(1)} %fusion.57), channel_id=1, source_target_pairs={{0,2},{1,3},{2,0},{3,1},{4,6},{5,7},{6,4},{7,5},{8,10},{9,11},{10,... | collective-permute-start | bytes 442376 | tf_op jit(solution)/shard_map/ppermute | solution.py:58
  216.0 2.5 copy-start.26
  220.5 10.8 %copy-start.21 = (f32[64,1152]{1,0:T(8,128)}, f32[64,1152]{1,0:T(8,128)S(1)}, u32[]{:S(2)}) copy-start(f32[64,1152]{1,0:T(8,128)S(1)} %get-tuple-element.141) | copy-start | bytes 884740
  231.3 14.8 %all-to-all-start.4 = ((bf16[4,72,256]{2,1,0:T(8,128)(2,1)}), bf16[4,72,256]{2,1,0:T(8,128)(2,1)}, u32[]{:S(2)}, u32[]{:S(2)}) async-start(bf16[4,72,256]{2,1,0:T(8,128)(2,1)} %bitcast.251), calls=%async_computation.4 | async-start | bytes 294912 | tf_op jit(solution)/shard_map/all_to_all | solution.py:250
  237.4 44.1 %collective-permute-start.12 = (bf16[256,1152]{1,0:T(8,128)(2,1)}, bf16[256,1152]{1,0:T(8,128)(2,1)}, u32[]{:S(2)}, u32[]{:S(2)}) collective-permute-start(bf16[256,1152]{1,0:T(8,128)(2,1)} %pad_maximum_fusion.7), channel_id=1, source_target_pairs={{0,2},{1,3},{2,0},{3,1},{4,6},{5,7},{6,4},{7,5},{8,10},{9,11},{10,... | collective-permute-start | bytes 1769480 | tf_op jit(solution)/shard_map/ppermute | solution.py:66
  248.0 3.1 copy-start.18
  251.1 4.8 %copy-start.47 = (bf16[4,9,8,256]{3,2,0,1:T(8,128)(2,1)S(1)}, bf16[4,9,8,256]{3,2,0,1:T(8,128)(2,1)}, u32[]{:S(2)}) copy-start(bf16[4,9,8,256]{3,2,0,1:T(8,128)(2,1)} %copy.308) | copy-start | bytes 442372
  256.8 18.1 %collective-permute-start.7 = (bf16[144,1024]{1,0:T(8,128)(2,1)S(1)}, bf16[144,1024]{1,0:T(8,128)(2,1)S(1)}, u32[]{:S(2)}, u32[]{:S(2)}) collective-permute-start(bf16[144,1024]{1,0:T(8,128)(2,1)S(1)} %fusion.39), channel_id=1, source_target_pairs={{0,16},{16,0},{1,17},{17,1},{2,18},{18,2},{3,19},{19,3},{4,20},{20... | collective-permute-start | bytes 884744 | tf_op jit(solution)/shard_map/ppermute | solution.py:82
  277.4 11.7 %all-to-all-start.5 = ((bf16[4,216,256]{2,1,0:T(8,128)(2,1)}), bf16[4,216,256]{2,1,0:T(8,128)(2,1)}, u32[]{:S(2)}, u32[]{:S(2)}) async-start(bf16[4,216,256]{2,1,0:T(8,128)(2,1)} %maximum_bitcast_fusion.2), calls=%async_computation.5 | async-start | bytes 884736 | tf_op jit(solution)/shard_map/all_to_all | solution.py:214
  284.4 17.4 %collective-permute-start.13 = (bf16[512,1152]{1,0:T(8,128)(2,1)}, bf16[512,1152]{1,0:T(8,128)(2,1)}, u32[]{:S(2)}, u32[]{:S(2)}) collective-permute-start(bf16[512,1152]{1,0:T(8,128)(2,1)} %pad_maximum_fusion.1), channel_id=1, source_target_pairs={{0,1},{1,0},{2,3},{3,2},{4,5},{5,4},{6,7},{7,6},{8,9},{9,8},{10,11... | collective-permute-start | bytes 3538952 | tf_op jit(solution)/shard_map/ppermute | solution.py:66
  295.5 1.9 collective-permute-start.8
  296.1 5.7 %copy-start.5 = (bf16[256,1152]{1,0:T(8,128)(2,1)S(1)}, bf16[256,1152]{1,0:T(8,128)(2,1)}, u32[]{:S(2)}) copy-start(bf16[256,1152]{1,0:T(8,128)(2,1)} %copy-done.4) | copy-start | bytes 1769476
  296.1 5.7 %copy-start.7 = (bf16[256,1152]{1,0:T(8,128)(2,1)S(1)}, bf16[256,1152]{1,0:T(8,128)(2,1)}, u32[]{:S(2)}) copy-start(bf16[256,1152]{1,0:T(8,128)(2,1)} %copy-done.6) | copy-start | bytes 1769476
  300.1 6.2 %collective-permute-start.9 = (bf16[64,1152]{1,0:T(8,128)(2,1)}, bf16[64,1152]{1,0:T(8,128)(2,1)}, u32[]{:S(2)}, u32[]{:S(2)}) collective-permute-start(bf16[64,1152]{1,0:T(8,128)(2,1)} %fusion.59), channel_id=1, source_target_pairs={{0,2},{1,3},{2,0},{3,1},{4,6},{5,7},{6,4},{7,5},{8,10},{9,11},{10,... | collective-permute-start | bytes 442376 | tf_op jit(solution)/shard_map/ppermute | solution.py:58
  305.3 3.6 copy-start.14
  305.3 3.6 copy-start.22
  305.3 3.6 copy-start.49
  305.3 3.6 copy-start.60
  314.3 4.7 %copy-start.25 = (bf16[256,1152]{1,0:T(8,128)(2,1)S(1)}, bf16[256,1152]{1,0:T(8,128)(2,1)}, u32[]{:S(2)}) copy-start(bf16[256,1152]{1,0:T(8,128)(2,1)} %copy-done.24) | copy-start | bytes 1769476
  314.3 4.7 %copy-start.33 = (bf16[4,72,256]{2,1,0:T(8,128)(2,1)S(1)}, bf16[4,72,256]{2,1,0:T(8,128)(2,1)}, u32[]{:S(2)}) copy-start(bf16[4,72,256]{2,1,0:T(8,128)(2,1)} %copy-done.32) | copy-start | bytes 442372
  314.8 4.6 %copy-start.29 = (bf16[72,1024]{1,0:T(8,128)(2,1)S(1)}, bf16[72,1024]{1,0:T(8,128)(2,1)}, u32[]{:S(2)}) copy-start(bf16[72,1024]{1,0:T(8,128)(2,1)} %copy-done.28) | copy-start | bytes 442372
  314.9 5.5 %copy-start.20 = (bf16[144,1024]{1,0:T(8,128)(2,1)S(1)}, bf16[144,1024]{1,0:T(8,128)(2,1)}, u32[]{:S(2)}) copy-start(bf16[144,1024]{1,0:T(8,128)(2,1)} %copy-done.19) | copy-start | bytes 884740
  315.7 11.7 %all-to-all-start.6 = ((f32[32,1,1080]{2,1,0:T(1,128)}), f32[32,1,1080]{2,1,0:T(1,128)}, u32[]{:S(2)}, u32[]{:S(2)}) async-start(f32[32,1,1080]{2,1,0:T(1,128)} %copy.278), calls=%async_computation.6 | async-start | bytes 294912 | tf_op jit(solution)/shard_map/all_to_all | solution.py:307
  320.8 11.3 %copy-start.38 = (bf16[72,4,2,2,64]{4,3,2,1,0:T(2,128)(2,1)S(1)}, bf16[72,4,2,2,64]{4,3,2,1,0:T(2,128)(2,1)}, u32[]{:S(2)}) copy-start(bf16[72,4,2,2,64]{4,3,2,1,0:T(2,128)(2,1)} %concatenate.86) | copy-start | bytes 442372
  329.3 11.5 %all-to-all-start.7 = ((f32[32,1,1224]{2,1,0:T(1,128)}), f32[32,1,1224]{2,1,0:T(1,128)S(1)}, u32[]{:S(2)}, u32[]{:S(2)}) async-start(f32[32,1,1224]{2,1,0:T(1,128)} %broadcast_in_dim.25), calls=%async_computation.7 | async-start | bytes 327680 | tf_op jit(solution)/shard_map/all_to_all | solution.py:62
  338.7 8.0 %copy-start.50 = (bf16[1152,216]{0,1:T(8,128)(2,1)S(1)}, bf16[1152,216]{0,1:T(8,128)(2,1)}, u32[]{:S(2)}) copy-start(bf16[1152,216]{0,1:T(8,128)(2,1)} %convolution_convert_fusion.3) | copy-start | bytes 1492996
  342.8 11.5 %all-to-all-start.8 = ((f32[32,1,576]{2,1,0:T(1,128)}), f32[32,1,576]{2,1,0:T(1,128)S(1)}, u32[]{:S(2)}, u32[]{:S(2)}) async-start(f32[32,1,576]{2,1,0:T(1,128)} %broadcast_in_dim.27), calls=%async_computation.8 | async-start | bytes 163840 | tf_op jit(solution)/shard_map/all_to_all | solution.py:62
  354.3 32.6 %all-to-all-start.9 = ((bf16[8,144,504]{2,1,0:T(8,128)(2,1)}), bf16[8,144,504]{2,1,0:T(8,128)(2,1)S(1)}, u32[]{:S(2)}, u32[]{:S(2)}) async-start(bf16[8,144,504]{2,1,0:T(8,128)(2,1)} %bitcast.209), calls=%async_computation.9 | async-start | bytes 2359296 | tf_op jit(solution)/shard_map/all_to_all | solution.py:277
  365.9 2.5 copy-start.8
  (26 other events, 35.6 us)
Sparse Core Ops, SparseCore 0:
  10.8 59.4 all-gather.2
  73.0 103.2 all-gather.4
  208.0 108.2 reduce-scatter.3
